TPU v7x, 128 devices: a whole 4x4x4 slice. The times are simulated.
128 devices in a mesh: face: 4 (over z_hi, core), tile: 32 (over x, y, z_lo).
Axes of the slice: x: 4, y: 4, z: 4 (z_hi: 2, z_lo: 2; z = z_hi * 2 + z_lo), core: 2. Of those that a mesh axis runs over, the one named last changes fastest.
Arguments:
- predicted_field: bfloat16 [16, 8192, 128], P(None, ('face', 'tile')), may hold values from -6 to 6
- parent_band_holder: int32 [8192, 2], P(('face', 'tile')), may hold values from 0 to 127, all different within a row; in each aligned block of 64 rows (0 to 63, 64 to 127, ...) at most 2 rows name the same one
- parent_band_slot: int32 [8192, 2], P(('face', 'tile')), may hold values from 0 to 63
- neighbour_positions: int32 [4, 8192, 128], P(None, ('face', 'tile')), may hold values from 0 to 255
- unscaled_neighbour_factor: float32 [4, 8192, 128], P(None, ('face', 'tile')), may hold values from 0.05 to 1
- truth_field: float32 [1024, 1024], P('tile', 'face'), may hold values from -6 to 6
Outputs:
- predicted_field_slope: float32 [16, 8192, 128], P(None, ('face', 'tile'))
Inputs may be any that keep to these rules, and one draw needn't show every extreme that they name: `parent_band_holder`: the two entries of a row differ. Within the 64 rows of one device no device is named more than 2 times, and some device is named exactly 2 times.
All inputs are finite; a program needn't handle non-finite values.
Results may differ from a plain program's by a relative error of at most 0.0003.
Values may be sent and summed in bfloat16 or wider, within the bound.
No kernel may reach another device: no remote copies, remote signals or barrier semaphores. Data moves between devices by JAX's collectives and lax.ppermute only.
A program may use at most 128 MiB of HBM per device.

v0:
```python
import jax
import jax.numpy as jnp
from jax import lax
from jax.sharding import PartitionSpec as P

RANGE = 8


FLOOR = 0.01


def with_halo(cells, sides, width, closed):
    for axis, dim in sides:
        count = lax.axis_size(axis)
        ends = count if closed else count - 1
        head = lax.slice_in_dim(cells, 0, width, axis=dim)
        tail = lax.slice_in_dim(cells, cells.shape[dim] - width, cells.shape[dim], axis=dim)
        cells = jnp.concatenate(
            [
                lax.ppermute(tail, axis, [(i, (i + 1) % count) for i in range(ends)]),
                cells,
                lax.ppermute(head, axis, [((i + 1) % count, i) for i in range(ends)]),
            ],
            axis=dim,
        )
    return cells


def pair_push(first, second, weight, participant_count):
    diff = first[:participant_count] - second[:participant_count]
    square_sum = diff * diff + FLOOR
    inverse_power = square_sum ** (-0.75)
    spread = jnp.mean(square_sum * inverse_power, axis=0)
    observed = first[participant_count] - second[participant_count]
    mismatch = (observed * observed + FLOOR) ** 0.25 - spread
    return weight / participant_count * mismatch * diff * inverse_power


def gather_weighted(values, neighbour_positions, norm_weight):
    participant_count = values.shape[0]
    band_ids = jnp.arange(values.shape[1], dtype=jnp.int32)[:, None]
    summed = jnp.zeros((participant_count,) + neighbour_positions.shape[1:], jnp.float32)
    for point in range(neighbour_positions.shape[0]):
        picked = values[:, band_ids, neighbour_positions[point]]
        summed = summed + picked.astype(jnp.float32) * norm_weight[point][None]
    return summed


def local(
    predicted_field,
    parent_band_holder,
    parent_band_slot,
    neighbour_positions,
    unscaled_neighbour_factor,
    truth_field,
):
    participant_count, resident_band_count, band_pixel_count = predicted_field.shape
    tile_count = lax.axis_size("tile")
    device_count = lax.axis_size(("face", "tile"))
    slot_count = max(2, 4 * resident_band_count // device_count)
    pair_owner = parent_band_holder.reshape(-1)
    owner_hot = (pair_owner[:, None] == jnp.arange(device_count, dtype=jnp.int32)[None, :]).astype(
        jnp.int32
    )
    slot_rank = jnp.sum((jnp.cumsum(owner_hot, axis=0) - owner_hot) * owner_hot, axis=1)
    place = pair_owner * slot_count + slot_rank
    wanted = (
        jnp.zeros((device_count * slot_count,), jnp.int32)
        .at[place]
        .set(parent_band_slot.reshape(-1))
    )
    wanted_band_numbers = lax.all_to_all(
        wanted.reshape(device_count, slot_count),
        ("face", "tile"),
        split_axis=0,
        concat_axis=0,
        tiled=True,
    ).reshape(-1)
    outgoing_bands = jnp.take(predicted_field, wanted_band_numbers, axis=1)
    incoming = lax.all_to_all(
        outgoing_bands.reshape(participant_count, device_count, slot_count, band_pixel_count),
        ("face", "tile"),
        split_axis=1,
        concat_axis=1,
        tiled=True,
    )
    incoming = incoming.reshape(participant_count, device_count * slot_count, band_pixel_count)
    incoming_bands = jnp.take(incoming, place, axis=1).reshape(
        participant_count, resident_band_count, 2 * band_pixel_count
    )
    norm_weight = unscaled_neighbour_factor / jnp.sum(
        unscaled_neighbour_factor, axis=0, keepdims=True
    )
    regridded = gather_weighted(incoming_bands, neighbour_positions, norm_weight)
    row_count = resident_band_count // 2
    col_count = 2 * band_pixel_count
    field = regridded.reshape(participant_count, row_count, col_count)
    stacked = jnp.concatenate([field, truth_field[None]], axis=0)
    tall_ext = with_halo(stacked, (("tile", 1),), RANGE, False)
    wide_ext = with_halo(stacked, (("face", 2),), RANGE, True)
    row_start = lax.axis_index("tile") * row_count - RANGE
    total_rows = row_count * tile_count
    row_ids = row_start + jnp.arange(row_count + 2 * RANGE, dtype=jnp.int32)
    gradient = jnp.zeros((participant_count, row_count, col_count), jnp.float32)
    for offset in range(1, RANGE + 1):
        span = row_count + 2 * RANGE - offset
        pushed = pair_push(
            tall_ext[:, :span], tall_ext[:, offset:], 1.0 / offset, participant_count
        )
        inside = (row_ids[:span] >= 0) & (row_ids[offset:] < total_rows)
        pushed = jnp.where(inside[None, :, None], pushed, 0.0)
        gradient = (
            gradient
            - pushed[:, RANGE : RANGE + row_count]
            + pushed[:, RANGE - offset : RANGE - offset + row_count]
        )
    for offset in range(1, RANGE + 1):
        span = col_count + 2 * RANGE - offset
        pushed = pair_push(
            wide_ext[:, :, :span], wide_ext[:, :, offset:], 1.0 / offset, participant_count
        )
        gradient = (
            gradient
            - pushed[:, :, RANGE : RANGE + col_count]
            + pushed[:, :, RANGE - offset : RANGE - offset + col_count]
        )
    grad_blocks = gradient.reshape(participant_count, resident_band_count, band_pixel_count)
    unused, pullback = jax.vjp(
        lambda values: gather_weighted(values, neighbour_positions, norm_weight),
        jnp.zeros((participant_count, resident_band_count, 2 * band_pixel_count), jnp.float32),
    )
    incoming_slope_parts = pullback(grad_blocks)[0].reshape(
        participant_count, 2 * resident_band_count, band_pixel_count
    )
    slot_grads = (
        jnp.zeros((participant_count, device_count * slot_count, band_pixel_count), jnp.float32)
        .at[:, place]
        .set(incoming_slope_parts)
    )
    returned = lax.all_to_all(
        slot_grads.reshape(participant_count, device_count, slot_count, band_pixel_count),
        ("face", "tile"),
        split_axis=1,
        concat_axis=1,
        tiled=True,
    )
    returned = returned.reshape(participant_count, device_count * slot_count, band_pixel_count)
    predicted_field_slope = (
        jnp.zeros((participant_count, resident_band_count, band_pixel_count), jnp.float32)
        .at[:, wanted_band_numbers]
        .add(returned)
    )
    return predicted_field_slope


def solution(mesh):
    in_specs = (
        P(None, ("face", "tile"), None),
        P(("face", "tile"), None),
        P(("face", "tile"), None),
        P(None, ("face", "tile"), None),
        P(None, ("face", "tile"), None),
        P("tile", "face"),
    )
    out_specs = P(None, ("face", "tile"), None)
    return jax.shard_map(local, mesh=mesh, in_specs=in_specs, out_specs=out_specs, check_vma=False)
```

profile of v0, /device:TPU:1, one launch (start us, length us, event | category | flops | bytes accessed | tf_op | source)
XLA Modules:
  0.0 804.7 jit_solution(15031600663335900444)
XLA Ops:
  5.0 11.5 %all-to-all-start = ((s32[128,1,2]{2,1,0:T(1,128)}), s32[128,1,2]{2,1,0:T(1,128)S(1)}, u32[]{:S(2)}, u32[]{:S(2)}) async-start(s32[128,1,2]{2,1,0:T(1,128)} %bitcast.2), calls=%async_computation | async-start | bytes 131072 | tf_op jit(solution)/shard_map/all_to_all | solution.py:72
  27.6 5.0 gather_fusion
  34.6 8.6 %all-to-all-start.1 = ((bf16[16,128,2,128]{3,2,0,1:T(2,128)(2,1)}), bf16[16,128,2,128]{3,2,0,1:T(2,128)(2,1)S(1)}, u32[]{:S(2)}, u32[]{:S(2)}) async-start(bf16[16,128,2,128]{3,2,0,1:T(2,128)(2,1)} %broadcast_select_fusion), calls=%async_computation.1 | async-start | bytes 2097152 | tf_op jit(solution)/shard_map/all_to_all | solution.py:80
  45.1 17.4 %all-to-all-done.1 = bf16[16,128,2,128]{3,2,0,1:T(2,128)(2,1)S(1)} async-done(((bf16[16,128,2,128]{3,2,0,1:T(2,128)(2,1)}), bf16[16,128,2,128]{3,2,0,1:T(2,128)(2,1)S(1)}, u32[]{:S(2)}, u32[]{:S(2)}) %all-to-all-start.1) | async-done | bytes 1048608 | tf_op jit(solution)/shard_map/all_to_all | solution.py:80
  63.4 3.1 copy.81
  66.4 7.6 bitcast_select_fusion
  74.1 96.2 %gather_fusion.2 = bf16[8192,16]{1,0:T(8,128)(2,1)S(1)} fusion(bf16[16,64,256]{0,2,1:T(8,128)(2,1)} %bitcast_select_fusion, s32[8192]{0:T(1024)S(1)} %get-tuple-element.29), kind=kCustom, calls=%fused_computation.2 | custom fusion | bytes 589824 | tf_op jit(solution)/shard_map/gather | solution.py:44
  175.7 96.0 %gather_fusion.3 = bf16[8192,16]{1,0:T(8,128)(2,1)S(1)} fusion(bf16[16,64,256]{0,2,1:T(8,128)(2,1)} %bitcast_select_fusion, s32[8192]{0:T(1024)S(1)} %get-tuple-element.31), kind=kCustom, calls=%fused_computation.3 | custom fusion | bytes 589824 | tf_op jit(solution)/shard_map/gather | solution.py:44
  277.0 95.9 %gather_fusion.4 = bf16[8192,16]{1,0:T(8,128)(2,1)S(1)} fusion(bf16[16,64,256]{0,2,1:T(8,128)(2,1)} %bitcast_select_fusion, s32[8192]{0:T(1024)S(1)} %get-tuple-element.30), kind=kCustom, calls=%fused_computation.4 | custom fusion | bytes 589824 | tf_op jit(solution)/shard_map/gather | solution.py:44
  375.4 3.5 copy.84
  379.0 96.2 %gather_fusion.5 = bf16[8192,16]{1,0:T(8,128)(2,1)S(1)} fusion(bf16[16,64,256]{0,2,1:T(8,128)(2,1)} %bitcast_select_fusion, s32[8192]{0:T(1024)S(1)} %get-tuple-element.32), kind=kCustom, calls=%fused_computation.5 | custom fusion | bytes 589824 | tf_op jit(solution)/shard_map/gather | solution.py:44
  477.6 2.9 copy.85
  486.2 9.4 %collective-permute-done.3 = f32[17,32,8]{2,1,0:T(8,128)S(1)} collective-permute-done((f32[17,32,8]{2,1,0:T(8,128)S(1)}, f32[17,32,8]{2,1,0:T(8,128)S(1)}, u32[]{:S(2)}, u32[]{:S(2)}) %collective-permute-start.3) | collective-permute-done | bytes 17440 | tf_op jit(solution)/shard_map/ppermute | solution.py:22
  518.1 2.9 copy.76
  528.9 48.0 %scatter_custom_fusion.4 = f32[16,16384]{0,1:T(8,128)} fusion(s32[8192]{0:T(1024)} %get-tuple-element.39, f32[8192,16]{1,0:T(8,128)} %bitcast.177, f32[]{:T(128)} %constant.34.clone.1), kind=kCustom, calls=%fused_computation.16 | custom fusion | flops 131072 | bytes 1049088
  576.9 48.0 %scatter_custom_fusion.3 = f32[16,16384]{0,1:T(8,128)} fusion(s32[8192]{0:T(1024)} %get-tuple-element.40, f32[8192,16]{1,0:T(8,128)} %bitcast.176, f32[]{:T(128)} %constant.34.clone.1), kind=kCustom, calls=%fused_computation.18 | custom fusion | flops 131072 | bytes 1049088
  624.9 9.8 %add_any.9 = f32[16,16384]{0,1:T(8,128)} add(f32[16,16384]{0,1:T(8,128)} %scatter_custom_fusion.3, f32[16,16384]{0,1:T(8,128)} %scatter_custom_fusion.4) | non-fusion elementwise | flops 262144 | bytes 3145728 | tf_op jit(solution)/shard_map/transpose(jvp())/add_any | solution.py:44
  634.6 48.0 %scatter_custom_fusion.6 = f32[16,16384]{0,1:T(8,128)} fusion(s32[8192]{0:T(1024)} %get-tuple-element.37, f32[8192,16]{1,0:T(8,128)} %bitcast.175, f32[]{:T(128)} %constant.34.clone.1), kind=kCustom, calls=%fused_computation.14 | custom fusion | flops 131072 | bytes 1049088
  682.6 46.7 %scatter_fusion.2 = f32[16,16384]{0,1:T(8,128)} fusion(f32[16,16384]{0,1:T(8,128)} %add_any.9, s32[8192]{0:T(1024)S(1)} %copy-done.7, f32[8192,16]{1,0:T(8,128)} %bitcast.172), kind=kCustom, calls=%fused_computation.11 | custom fusion | flops 131072 | bytes 1605632
  729.3 9.7 %add_any.10 = f32[16,16384]{0,1:T(8,128)} add(f32[16,16384]{0,1:T(8,128)} %scatter_fusion.2, f32[16,16384]{0,1:T(8,128)} %scatter_custom_fusion.6) | non-fusion elementwise | flops 262144 | bytes 3145728 | tf_op jit(solution)/shard_map/transpose(jvp())/add_any | solution.py:44
  739.1 5.1 copy.79
  744.4 4.3 scatter_fusion
  748.7 33.9 %all_to_all.19 = f32[16,128,2,128]{3,0,2,1:T(8,128)} all-to-all(f32[16,128,2,128]{3,0,2,1:T(8,128)S(1)} %bitcast.170), channel_id=1, replica_groups=mesh['face'=4,'tile'=32] {'face','tile'}, dimensions={1} | all-to-all | bytes 4194304 | tf_op jit(solution)/shard_map/all_to_all | solution.py:140
  782.7 20.6 %scatter_fusion.1 = f32[16,64,128]{2,0,1:T(8,128)S(1)} fusion(f32[16,64,128]{2,0,1:T(8,128)S(1)} %broadcast_in_dim.136, s32[256]{0:T(256)S(1)} %bitcast.198, f32[256,16,128]{2,1,0:T(8,128)} %bitcast.171), kind=kCustom, calls=%fused_computation.8 | custom fusion | flops 524288 | bytes 6292480 | tf_op jit(solution)/shard_map/scatter-add | solution.py:151
  (153 shorter events, 73.0 us)
Async XLA Ops:
  0.0 27.6 %copy-start = (bf16[16,64,128]{2,1,0:T(8,128)(2,1)S(1)}, bf16[16,64,128]{2,1,0:T(8,128)(2,1)}, u32[]{:S(2)}) copy-start(bf16[16,64,128]{2,1,0:T(8,128)(2,1)} %param.6) | copy-start | bytes 786436
  5.0 21.0 %all-to-all-start = ((s32[128,1,2]{2,1,0:T(1,128)}), s32[128,1,2]{2,1,0:T(1,128)S(1)}, u32[]{:S(2)}, u32[]{:S(2)}) async-start(s32[128,1,2]{2,1,0:T(1,128)} %bitcast.2), calls=%async_computation | async-start | bytes 131072 | tf_op jit(solution)/shard_map/all_to_all | solution.py:72
  32.6 10.9 %copy-start.8 = (s32[2]{0:T(128)S(1)}, s32[2]{0:T(128)}, u32[]{:S(2)}) copy-start(s32[2]{0:T(128)} %constant.65) | copy-start | bytes 28
  34.6 27.9 %all-to-all-start.1 = ((bf16[16,128,2,128]{3,2,0,1:T(2,128)(2,1)}), bf16[16,128,2,128]{3,2,0,1:T(2,128)(2,1)S(1)}, u32[]{:S(2)}, u32[]{:S(2)}) async-start(bf16[16,128,2,128]{3,2,0,1:T(2,128)(2,1)} %broadcast_select_fusion), calls=%async_computation.1 | async-start | bytes 2097152 | tf_op jit(solution)/shard_map/all_to_all | solution.py:80
  477.6 2.9 copy-start.3
  477.6 3.2 copy-start.2
  481.0 5.2 collective-permute-start.2
  482.1 13.4 %collective-permute-start.3 = (f32[17,32,8]{2,1,0:T(8,128)S(1)}, f32[17,32,8]{2,1,0:T(8,128)S(1)}, u32[]{:S(2)}, u32[]{:S(2)}) collective-permute-start(f32[17,32,8]{2,1,0:T(8,128)S(1)} %get-tuple-element.16), channel_id=1, source_target_pairs={{32,0},{64,32},{96,64},{0,96},{33,1},{65,33},{97,65},{1,97},{34,2}... | collective-permute-start | bytes 52232 | tf_op jit(solution)/shard_map/ppermute | solution.py:22
  482.2 23.0 %collective-permute-start = (f32[17,8,256]{2,1,0:T(8,128)S(1)}, f32[17,8,256]{2,1,0:T(8,128)S(1)}, u32[]{:S(2)}, u32[]{:S(2)}) collective-permute-start(f32[17,8,256]{2,1,0:T(8,128)S(1)} %get-tuple-element.13), channel_id=1, source_target_pairs={{0,1},{1,2},{2,3},{3,4},{4,5},{5,6},{6,7},{7,8},{8,9},{9,10},{10,1... | collective-permute-start | bytes 417800 | tf_op jit(solution)/shard_map/ppermute | solution.py:20
  484.7 20.5 %collective-permute-start.1 = (f32[17,8,256]{2,1,0:T(8,128)S(1)}, f32[17,8,256]{2,1,0:T(8,128)S(1)}, u32[]{:S(2)}, u32[]{:S(2)}) collective-permute-start(f32[17,8,256]{2,1,0:T(8,128)S(1)} %get-tuple-element.14), channel_id=1, source_target_pairs={{1,0},{2,1},{3,2},{4,3},{5,4},{6,5},{7,6},{8,7},{9,8},{10,9},{11,1... | collective-permute-start | bytes 417800 | tf_op jit(solution)/shard_map/ppermute | solution.py:22
  506.8 2.6 copy-start.12
  507.3 2.6 copy-start.11
  508.6 1.9 copy-start.10
  509.2 1.9 copy-start.9
  513.9 4.0 copy-start.4
  513.9 4.0 copy-start.5
  513.9 4.0 copy-start.6
  634.6 48.0 %copy-start.7 = (s32[8192]{0:T(1024)S(1)}, s32[8192]{0:T(1024)}, u32[]{:S(2)}) copy-start(s32[8192]{0:T(1024)} %get-tuple-element.38) | copy-start | bytes 98308
  748.7 55.5 %copy-start.1 = (bf16[16,64,128]{2,1,0:T(8,128)(2,1)S(1)}, bf16[16,64,128]{2,1,0:T(8,128)(2,1)}, u32[]{:S(2)}) copy-start(bf16[16,64,128]{2,1,0:T(8,128)(2,1)} %param.6) | copy-start | bytes 786436
where the time goes:
time: 814 us; the launch traced here: 805 us
  local copies, waits for them, and re-layouts  434 us (53%)
  other arithmetic  282 us (35%)
  blocking collectives  33.9 us (4%)
  waiting for transfers between devices  28.6 us (4%)
  starting transfers between devices  25.2 us (3%)
    gather x4, local copies, waits for them, and re-layouts, gather_weighted(): picked = values[:, band_ids, neighbour_positions[point]]  384 us
    unnamed x8, other arithmetic  193 us
    all_to_all x1, blocking collectives, local(): lax.all_to_all(slot_grads.reshape(participant_count, device_count, slot_c...  33.9 us
    scatter-add x1, other arithmetic, local(): predicted_field_slope = jnp.zeros((participant_count, resident_band_count...  20.6 us
    add_any x2, other arithmetic, gather_weighted(): picked = values[:, band_ids, neighbour_positions[point]]  19.5 us
    all_to_all x1, waiting for transfers between devices, local(): lax.all_to_all(outgoing_bands.reshape(participant_count, device_count, sl...  17.4 us
  transfers between devices with their start and end apart: 6, of which 3 were waited for; matrix products, arithmetic and copies ran while one was open for 2% of the time, Pallas kernels for 0%

commit v1 on v0

v1 whole, which is shorter than its diff:
```python
import jax
import jax.numpy as jnp
from jax import lax
from jax.experimental import pallas as pl
from jax.experimental.pallas import tpu as pltpu
from jax.sharding import PartitionSpec as P

RANGE = 8
FLOOR = 0.01
M = 16
BANDS = 64
LANES = 128
ROWS = 32
EXT = ROWS + 2 * RANGE
DEVICES = 128
POINTS = 4
F32 = jnp.float32
I32 = jnp.int32
BF16 = jnp.bfloat16
AXES = ("face", "tile")


def struct(shape, dtype=F32):
    return jax.ShapeDtypeStruct(shape, dtype)


def lane_ids(rows=8):
    return lax.broadcasted_iota(I32, (rows, LANES), 1)


def row_ids(rows=8):
    return lax.broadcasted_iota(I32, (rows, LANES), 0)


def request_kernel(holder_ref, slot_ref, wanted_ref, place_ref):
    owner = lane_ids(BANDS).astype(F32)
    band = row_ids(BANDS)
    big = float(1 << 20)
    hots, codes = [], []
    for k in range(2):
        holder = holder_ref[:, k : k + 1].astype(F32)
        slot = slot_ref[:, k : k + 1]
        hots.append(jnp.broadcast_to(holder, (BANDS, LANES)) == owner)
        codes.append(((band + k * BANDS) * BANDS + slot).astype(F32))
    low = [jnp.min(jnp.where(h, c, big), axis=0, keepdims=True) for h, c in zip(hots, codes)]
    high = [jnp.max(jnp.where(h, c, -1.0), axis=0, keepdims=True) for h, c in zip(hots, codes)]
    first = jnp.minimum(low[0], low[1])
    last = jnp.maximum(high[0], high[1])
    named, twice = last >= 0.0, last > first
    slots = [
        jnp.where(named, (first.astype(I32) & (BANDS - 1)).astype(F32), 0.0),
        jnp.where(twice, (last.astype(I32) & (BANDS - 1)).astype(F32), 0.0),
    ]
    rows = row_ids(LANES)
    table = jnp.where(rows == 0, slots[0], jnp.where(rows == 1, slots[1], 0.0))
    wanted_ref[...] = jnp.transpose(table).astype(I32)
    lanes = lane_ids(BANDS)
    columns = jnp.zeros((BANDS, LANES), F32)
    for k in range(2):
        spot = 2.0 * owner + jnp.where(codes[k] == first, 0.0, 1.0)
        spot = jnp.sum(jnp.where(hots[k], spot, 0.0), axis=1, keepdims=True)
        columns = jnp.where(lanes == k, spot, columns)
    columns = jnp.concatenate([columns, jnp.zeros((LANES - BANDS, LANES), F32)], axis=0)
    place_ref[...] = jnp.transpose(columns)[:8].astype(I32)


def request(holder, slot):
    return pl.pallas_call(
        request_kernel,
        out_shape=(struct((DEVICES, LANES), I32), struct((8, LANES), I32)),
        name="request",
    )(holder, slot)


def pack_kernel(asked_ref, bands_ref, out_ref, slots_ref, smem, sem):
    table = jnp.transpose(asked_ref[...].astype(F32))[:8].astype(I32)
    slots_ref[...] = table
    copy = pltpu.make_async_copy(slots_ref, smem, sem)
    copy.start()
    copy.wait()

    def step(i, carry):
        for r in range(2):
            out_ref[2 * i + r] = bands_ref[smem[r, i]]
        return carry

    lax.fori_loop(0, DEVICES, step, 0, unroll=8)


def pack(asked, bands):
    return pl.pallas_call(
        pack_kernel,
        out_shape=(struct((2 * DEVICES, M, LANES), BF16), struct((8, LANES), I32)),
        scratch_shapes=[pltpu.SMEM((8, LANES), I32), pltpu.SemaphoreType.DMA],
        name="pack",
    )(asked, bands)


def regrid_kernel(
    place_ref, recv_ref, pos_ref, factor_ref, truth_ref,
    field_ref, posn_ref, weight_ref, north_ref, south_ref, west_ref, east_ref,
    low_ref, high_ref,
):
    def spread(row, carry):
        for half in range(2):
            for k, tab in enumerate((low_ref, high_ref)):
                strip = recv_ref[place_ref[k, 2 * row + half]].astype(F32)
                tab[pl.ds(half * ROWS + row, M, stride=BANDS), :] = strip
        return carry

    lax.fori_loop(0, ROWS, spread, 0, unroll=4)

    for half in range(2):
        factors = [factor_ref[pl.ds(j * BANDS + half, ROWS, stride=2), :] for j in range(POINTS)]
        total = factors[0] + factors[1] + factors[2] + factors[3]
        for j in range(POINTS):
            spot = j * BANDS + half * ROWS
            posn_ref[pl.ds(spot, ROWS), :] = pos_ref[pl.ds(j * BANDS + half, ROWS, stride=2), :]
            weight_ref[pl.ds(spot, ROWS), :] = factors[j] / total

    def regrid(block, carry):
        row = pl.multiple_of(block * 8, 8)
        posn = [posn_ref[pl.ds(j * BANDS + row, 8), :] for j in range(POINTS)]
        weight = [weight_ref[pl.ds(j * BANDS + row, 8), :] for j in range(POINTS)]
        lane = [p & (LANES - 1) for p in posn]
        upper = [p >= LANES for p in posn]
        for m in range(M):
            low = low_ref[pl.ds(m * BANDS + row, 8), :]
            high = high_ref[pl.ds(m * BANDS + row, 8), :]
            out = jnp.zeros((8, LANES), F32)
            for j in range(POINTS):
                a = jnp.take_along_axis(low, lane[j], axis=1, mode="promise_in_bounds")
                b = jnp.take_along_axis(high, lane[j], axis=1, mode="promise_in_bounds")
                out = out + weight[j] * jnp.where(upper[j], b, a)
            field_ref[pl.ds(m * BANDS + row, 8), :] = out
        return carry

    lax.fori_loop(0, BANDS // 8, regrid, 0)

    for half in range(2):
        field_ref[pl.ds(M * BANDS + half * ROWS, ROWS), :] = truth_ref[:, half * LANES : (half + 1) * LANES]
    for m in range(M + 1):
        for half in range(2):
            spot = m * BANDS + half * ROWS
            north_ref[pl.ds((2 * m + half) * 8, 8), :] = field_ref[pl.ds(spot, 8), :]
            south_ref[pl.ds((2 * m + half) * 8, 8), :] = field_ref[pl.ds(spot + ROWS - 8, 8), :]
    lanes = lane_ids()
    for rb in range(ROWS // 8):
        west = jnp.zeros((8, LANES), F32)
        east = jnp.zeros((8, LANES), F32)
        for m in range(M):
            mine = (lanes >> 3) == m
            left = field_ref[pl.ds(m * BANDS + rb * 8, 8), :]
            right = field_ref[pl.ds(m * BANDS + ROWS + rb * 8, 8), :]
            west = jnp.where(mine, pltpu.roll(left, (8 * m) % LANES, 1), west)
            east = jnp.where(mine, pltpu.roll(right, (8 * m + 8) % LANES, 1), east)
        west_ref[pl.ds(rb * 8, 8), :] = west
        east_ref[pl.ds(rb * 8, 8), :] = east
    west_ref[pl.ds(ROWS, ROWS), :] = truth_ref[:, :LANES]
    east_ref[pl.ds(ROWS, ROWS), :] = truth_ref[:, LANES:]


VMEM = pl.BlockSpec(memory_space=pltpu.VMEM)
SMEM = pl.BlockSpec(memory_space=pltpu.SMEM)


def regrid(place, recv, pos, factor, truth):
    tall = struct(((M + 1) * 2 * RANGE, LANES))
    wide = struct((2 * ROWS, LANES))
    return pl.pallas_call(
        regrid_kernel,
        in_specs=[SMEM, VMEM, VMEM, VMEM, VMEM],
        out_shape=(
            struct(((M + 1) * BANDS, LANES)),
            struct((POINTS * BANDS, LANES), I32),
            struct((POINTS * BANDS, LANES)),
            tall, tall, wide, wide,
        ),
        scratch_shapes=[pltpu.VMEM((M * BANDS, LANES), F32)] * 2,
        name="regrid",
    )(place, recv, pos, factor, truth)


def fall(square_sum):
    root = lax.rsqrt(square_sum)
    return root * (root * lax.rsqrt(root))


def spread_of(diff):
    square_sum = diff * diff + FLOOR
    return square_sum * fall(square_sum)


def push_kernel(
    place_ref, tile_ref, field_ref, posn_ref, weight_ref, top_ref, bottom_ref, left_ref, right_ref,
    out_ref, ext, grad, ring,
):
    for mh in range(2 * (M + 1)):
        ext[pl.ds(mh * EXT, 8), :] = top_ref[pl.ds(mh * 8, 8), :]
        ext[pl.ds(mh * EXT + 8, ROWS), :] = field_ref[pl.ds(mh * ROWS, ROWS), :]
        ext[pl.ds(mh * EXT + 8 + ROWS, 8), :] = bottom_ref[pl.ds(mh * 8, 8), :]
    grad[...] = jnp.zeros_like(grad)
    first_row = tile_ref[0] * ROWS - RANGE

    def latitude(step, carry):
        half = step // 5
        block = step % 5
        base = pl.multiple_of(half * EXT + block * 8, 8)
        rows = row_ids() + (first_row + block * 8)
        firsts = [ext[pl.ds(base + m * 2 * EXT, 8), :] for m in range(M + 1)]
        for k in range(1, RANGE + 1):
            total = jnp.zeros((8, LANES), F32)
            slopes = []
            for m in range(M):
                diff = firsts[m] - ext[pl.ds(base + m * 2 * EXT + k, 8), :]
                square_sum = diff * diff + FLOOR
                power = fall(square_sum)
                total = total + square_sum * power
                slopes.append(diff * power)
            seen = spread_of(firsts[M] - ext[pl.ds(base + M * 2 * EXT + k, 8), :])
            inside = (rows >= 0) & (rows + k < ROWS * 32)
            push = jnp.where(inside, (1.0 / (k * M)) * (seen - total * (1.0 / M)), 0.0)
            for m in range(M):
                pushed = push * slopes[m]
                here = base + m * 2 * EXT
                grad[pl.ds(here, 8), :] -= pushed
                grad[pl.ds(here + k, 8), :] += pushed
        return carry

    lax.fori_loop(0, 10, latitude, 0)

    lanes = lane_ids()

    def longitude(rb, carry):
        row = pl.multiple_of(rb * 8, 8)
        left = left_ref[pl.ds(row, 8), :]
        right = right_ref[pl.ds(row, 8), :]
        for m in range(M + 1):
            spot = m * 2 * EXT + 8 + row
            ring[m * 3] = ext[pl.ds(spot, 8), :]
            ring[m * 3 + 1] = ext[pl.ds(spot + EXT, 8), :]
            if m < M:
                after = pltpu.roll(right, (LANES - 8 * m) % LANES, 1)
                before = pltpu.roll(left, (LANES - 8 - 8 * m) % LANES, 1)
            else:
                after = right_ref[pl.ds(ROWS + row, 8), :]
                before = left_ref[pl.ds(ROWS + row, 8), :]
            ring[m * 3 + 2] = jnp.where(lanes < RANGE, after, jnp.where(lanes >= LANES - RANGE, before, 0.0))

        for k in range(1, RANGE + 1):
            def pair_diff(m):
                here = [ring[m * 3 + v] for v in range(3)]
                moved = [pltpu.roll(x, LANES - k, 1) for x in here]
                return [
                    here[v] - jnp.where(lanes < LANES - k, moved[v], moved[(v + 1) % 3])
                    for v in range(3)
                ]

            totals = [jnp.zeros((8, LANES), F32)] * 3
            slopes = []
            for m in range(M):
                diffs = pair_diff(m)
                row_slopes = []
                for v in range(3):
                    square_sum = diffs[v] * diffs[v] + FLOOR
                    power = fall(square_sum)
                    totals[v] = totals[v] + square_sum * power
                    row_slopes.append(diffs[v] * power)
                slopes.append(row_slopes)
            seen = [spread_of(d) for d in pair_diff(M)]
            push = [(1.0 / (k * M)) * (seen[v] - totals[v] * (1.0 / M)) for v in range(3)]
            for m in range(M):
                pushed = [push[v] * slopes[m][v] for v in range(3)]
                moved = [pltpu.roll(x, k, 1) for x in pushed]
                for v in range(2):
                    spot = m * 2 * EXT + 8 + row + v * EXT
                    grad[pl.ds(spot, 8), :] += jnp.where(lanes >= k, moved[v], moved[(v + 2) % 3]) - pushed[v]
        return carry

    lax.fori_loop(0, ROWS // 8, longitude, 0)

    def clear(i, carry):
        out_ref[i] = jnp.zeros((M, LANES), F32)
        return carry

    lax.fori_loop(0, 2 * DEVICES, clear, 0, unroll=8)

    cells = row_ids(2 * LANES)

    def adjoint(row, carry):
        for half in range(2):
            tile = grad[pl.ds(half * EXT + 8 + row, M, stride=2 * EXT), :]
            parts, hots = [], []
            for j in range(POINTS):
                spot = j * BANDS + half * ROWS + row
                parts.append(tile * weight_ref[pl.ds(spot, 1), :])
                hots.append(jnp.where(cells == posn_ref[pl.ds(spot, 1), :], 1.0, 0.0).astype(BF16))
            part = jnp.concatenate(parts, axis=1)
            high = part.astype(BF16)
            low = (part - high.astype(F32)).astype(BF16)
            both = lax.dot_general(
                jnp.concatenate([high, low], axis=0),
                jnp.concatenate(hots, axis=1),
                (((1,), (1,)), ((), ())),
                preferred_element_type=F32,
            )
            both = both[:M] + both[M:]
            for k in range(2):
                out_ref[place_ref[k, 2 * row + half]] = both[:, k * LANES : (k + 1) * LANES]
        return carry

    lax.fori_loop(0, ROWS, adjoint, 0)


def push(place, tile, field, posn, weight, top, bottom, left, right):
    return pl.pallas_call(
        push_kernel,
        in_specs=[SMEM, SMEM] + [VMEM] * 7,
        out_shape=struct((2 * DEVICES, M, LANES)),
        scratch_shapes=[
            pltpu.VMEM((2 * (M + 1) * EXT, LANES), F32),
            pltpu.VMEM((2 * M * EXT, LANES), F32),
            pltpu.VMEM((3 * (M + 1), 8, LANES), F32),
        ],
        name="push",
    )(place, tile, field, posn, weight, top, bottom, left, right)


def collect_kernel(slots_ref, back_ref, out_ref):
    out_ref[...] = jnp.zeros_like(out_ref)

    def step(i, carry):
        for r in range(2):
            where = pl.ds(slots_ref[r, i], M, stride=BANDS)
            out_ref[where, :] += back_ref[2 * i + r]
        return carry

    lax.fori_loop(0, DEVICES, step, 0, unroll=4)


def collect(slots, back):
    return pl.pallas_call(
        collect_kernel,
        in_specs=[SMEM, VMEM],
        out_shape=struct((M * BANDS, LANES)),
        name="collect",
    )(slots, back)


def exchange(x):
    return lax.all_to_all(x, AXES, split_axis=0, concat_axis=0, tiled=True)


def local(predicted_field, parent_band_holder, parent_band_slot, neighbour_positions, unscaled_neighbour_factor, truth_field):
    tiles, faces = lax.axis_size("tile"), lax.axis_size("face")
    bands = jnp.transpose(predicted_field, (1, 0, 2))
    wanted, place = request(parent_band_holder, parent_band_slot)
    asked = exchange(wanted)
    outgoing, slots = pack(asked, bands)
    recv = exchange(outgoing.reshape(DEVICES, 2, M, LANES)).reshape(2 * DEVICES, M, LANES)
    field, posn, weight, north, south, west, east = regrid(
        place,
        recv,
        neighbour_positions.reshape(POINTS * BANDS, LANES),
        unscaled_neighbour_factor.reshape(POINTS * BANDS, LANES),
        truth_field,
    )
    up = [(i + 1, i) for i in range(tiles - 1)]
    down = [(i, i + 1) for i in range(tiles - 1)]
    bottom = lax.ppermute(north, "tile", up)
    top = lax.ppermute(south, "tile", down)
    right = lax.ppermute(west, "face", [((i + 1) % faces, i) for i in range(faces)])
    left = lax.ppermute(east, "face", [(i, (i + 1) % faces) for i in range(faces)])
    tile = lax.axis_index("tile").astype(I32).reshape(1)
    back = push(place, tile, field, posn, weight, top, bottom, left, right)
    back = exchange(back.reshape(DEVICES, 2, M, LANES)).reshape(2 * DEVICES, M, LANES)
    return collect(slots, back).reshape(M, BANDS, LANES)


def solution(mesh):
    in_specs = (
        P(None, AXES, None),
        P(AXES, None),
        P(AXES, None),
        P(None, AXES, None),
        P(None, AXES, None),
        P("tile", "face"),
    )
    return jax.shard_map(local, mesh=mesh, in_specs=in_specs, out_specs=P(None, AXES, None), check_vma=False)
```

time: 814 us -> 140 us (0.17); the launches traced: 805 us -> 140 us
  local copies, waits for them, and re-layouts: 434 us -> 5.89 us
  other arithmetic: 282 us -> 0 us
  Pallas kernels: 0 us -> 40.2 us
  blocking collectives: 33.9 us -> 62.7 us
  waiting for transfers between devices: 28.6 us -> 13.4 us
    gather x7 -> x0, local copies, waits for them, and re-layouts: 393 us -> none  [the longest x4 384 us: gather_weighted(): picked = values[:, band_ids, neighbour_positions[point]]]
    unnamed x8 -> x0, other arithmetic: 193 us -> none
    pallas_call x0 -> x5, Pallas kernels: none -> 40.2 us  [the longest x1 22.2 us: push(): pl.pallas_call(push_kernel, in_specs=[SMEM, SMEM] + [VMEM] * 7, out_shape...]
    all_to_all x1 -> x2, blocking collectives: 33.9 us -> 62.7 us  [exchange(): return lax.all_to_all(x, AXES, split_axis=0, concat_axis=0, tiled=True)]
    scatter-add x1 -> x0, other arithmetic: 20.6 us -> none  [local(): predicted_field_slope = jnp.zeros((participant_count, resident_band_count...]
    add_any x2 -> x0, other arithmetic: 19.5 us -> none  [gather_weighted(): picked = values[:, band_ids, neighbour_positions[point]]]
    select_n x12 -> x0, other arithmetic: 13.5 us -> none  [the longest x1 7.64 us: local(): jnp.take(incoming, place, axis=1)]
    convert_element_type x4 -> x0, local copies, waits for them, and re-layouts: 12.2 us -> none  [gather_weighted(): summed = summed + picked.astype(jnp.float32) * norm_weight[point][None]]
  transfers between devices with their start and end apart: 6 -> 5, of which waited for: 3 -> 3; matrix products, arithmetic and copies ran while one was open for 2% -> 1% of each run, Pallas kernels for 0% -> 0%
where the time goes in v1:
time: 140 us
  blocking collectives  62.7 us (45%)
  Pallas kernels  40.2 us (29%)
  starting transfers between devices  17.5 us (12%)
  waiting for transfers between devices  13.4 us (10%)
  local copies, waits for them, and re-layouts  5.89 us (4%)
    all_to_all x2, blocking collectives, exchange(): return lax.all_to_all(x, AXES, split_axis=0, concat_axis=0, tiled=True)  62.7 us
    pallas_call x1, Pallas kernels, push(): pl.pallas_call(push_kernel, in_specs=[SMEM, SMEM] + [VMEM] * 7, out_shape...  22.2 us
    all_to_all x1, starting transfers between devices, exchange(): return lax.all_to_all(x, AXES, split_axis=0, concat_axis=0, tiled=True)  11.5 us
    all_to_all x1, waiting for transfers between devices, exchange(): return lax.all_to_all(x, AXES, split_axis=0, concat_axis=0, tiled=True)  7.77 us
    pallas_call x1, Pallas kernels, collect(): pl.pallas_call(collect_kernel, in_specs=[SMEM, VMEM], out_shape=struct((M...  6.65 us
    pallas_call x1, Pallas kernels, regrid(): pl.pallas_call(regrid_kernel, in_specs=[SMEM, VMEM, VMEM, VMEM, VMEM], ou...  6.51 us
    unnamed x13, local copies, waits for them, and re-layouts  5.89 us
    ppermute x1, waiting for transfers between devices, local(): lax.ppermute(east, 'face', [(i, (i + 1) % faces) for i in range(faces)])  3.95 us
  transfers between devices with their start and end apart: 5, of which 3 were waited for; matrix products, arithmetic and copies ran while one was open for 1% of the time, Pallas kernels for 0%

profile of v1, /device:TPU:1, one launch (start us, length us, event | category | flops | bytes accessed | tf_op | source)
XLA Modules:
  0.0 139.8 jit_solution(16522800195972769290)
XLA Ops:
  0.0 1.4 copy.10.holder_ref
  1.4 1.4 copy.11.slot_ref
  2.8 1.7 %request.1 = (s32[128,128]{1,0:T(8,128)}, s32[8,128]{1,0:T(8,128)}) custom-call(s32[64,2]{1,0:T(8,128)} %copy.10.holder_ref, s32[64,2]{1,0:T(8,128)} %copy.11.slot_ref), custom_call_target="tpu_custom_call" | custom-call | tf_op jit(solution)/shard_map/request/pallas_call | solution.py:68
  4.4 11.5 %all-to-all-start = ((s32[128,1,128]{2,1,0:T(1,128)}), s32[128,1,128]{2,1,0:T(1,128)S(1)}, u32[]{:S(2)}, u32[]{:S(2)}) async-start(s32[128,1,128]{2,1,0:T(1,128)} %bitcast.23), calls=%async_computation | async-start | bytes 131072 | tf_op jit(solution)/shard_map/all_to_all | solution.py:351
  15.9 1.8 %copy.15 = bf16[16,64,128]{2,0,1:T(8,128)(2,1)} copy(bf16[16,64,128]{2,1,0:T(8,128)(2,1)} %param.6) | data formatting | bytes 524288 | tf_op args[0]
  17.8 7.8 %all-to-all-done = s32[128,1,128]{2,1,0:T(1,128)S(1)} async-done(((s32[128,1,128]{2,1,0:T(1,128)}), s32[128,1,128]{2,1,0:T(1,128)S(1)}, u32[]{:S(2)}, u32[]{:S(2)}) %all-to-all-start) | async-done | bytes 65568 | tf_op jit(solution)/shard_map/all_to_all | solution.py:351
  25.5 0.6 copy-done
  26.1 3.2 %pack.1 = (bf16[256,16,128]{2,1,0:T(8,128)(2,1)}, s32[8,128]{1,0:T(8,128)}) custom-call(s32[128,128]{1,0:T(8,128)} %bitcast.20, bf16[64,16,128]{2,1,0:T(8,128)(2,1)} %bitcast.18), custom_call_target="tpu_custom_call" | custom-call | tf_op jit(solution)/shard_map/pack/pallas_call | solution.py:91
  29.3 24.7 %all_to_all.21 = bf16[128,2,16,128]{3,2,1,0:T(8,128)(2,1)} all-to-all(bf16[128,2,16,128]{3,2,1,0:T(8,128)(2,1)} %bitcast.19), channel_id=1, replica_groups=mesh['face'=4,'tile'=32] {'face','tile'}, dimensions={0} | all-to-all | bytes 2097152 | tf_op jit(solution)/shard_map/all_to_all | solution.py:351
  54.0 6.5 %regrid.1 = (f32[1088,128]{1,0:T(8,128)}, s32[256,128]{1,0:T(8,128)}, f32[256,128]{1,0:T(8,128)}, f32[272,128]{1,0:T(8,128)}, f32[272,128]{1,0:T(8,128)}, /*index=5*/f32[64,128]{1,0:T(8,128)}, f32[64,128]{1,0:T(8,128)}) custom-call(s32[8,128]{1,0:T(8,128)} %get-tuple-element.18.place_ref, bf16[256,16,128]{2,1,0:T(8,128)(2,1)} %bitcast.17, ...), custom_call_target="tpu_custom_call" | custom-call | tf_op jit(solution)/shard_map/regrid/pallas_call | solution.py:170
  60.5 2.0 %collective-permute-start = (f32[272,128]{1,0:T(8,128)}, f32[272,128]{1,0:T(8,128)S(1)}, u32[]{:S(2)}, u32[]{:S(2)}) collective-permute-start(f32[272,128]{1,0:T(8,128)} %get-tuple-element.23), channel_id=1, source_target_pairs={{0,1},{1,2},{2,3},{3,4},{4,5},{5,6},{6,7},{7,8},{8,9},{9,10},{10,1... | collective-permute-start | bytes 417800 | tf_op jit(solution)/shard_map/ppermute | solution.py:371
  62.6 1.3 collective-permute-start.1
  63.9 2.7 %collective-permute-start.2 = (f32[64,128]{1,0:T(8,128)}, f32[64,128]{1,0:T(8,128)S(1)}, u32[]{:S(2)}, u32[]{:S(2)}) collective-permute-start(f32[64,128]{1,0:T(8,128)} %get-tuple-element.25), channel_id=1, source_target_pairs={{0,32},{32,64},{64,96},{96,0},{1,33},{33,65},{65,97},{97,1},{2,34}... | collective-permute-start | bytes 98312 | tf_op jit(solution)/shard_map/ppermute | solution.py:373
  66.5 0.0 collective-permute-start.3
  66.5 4.0 %collective-permute-done.2.left_ref = f32[64,128]{1,0:T(8,128)S(1)} collective-permute-done((f32[64,128]{1,0:T(8,128)}, f32[64,128]{1,0:T(8,128)S(1)}, u32[]{:S(2)}, u32[]{:S(2)}) %collective-permute-start.2) | collective-permute-done | bytes 32800 | tf_op jit(solution)/shard_map/ppermute | solution.py:373
  70.5 1.7 %collective-permute-done.3.right_ref = f32[64,128]{1,0:T(8,128)S(1)} collective-permute-done((f32[64,128]{1,0:T(8,128)}, f32[64,128]{1,0:T(8,128)S(1)}, u32[]{:S(2)}, u32[]{:S(2)}) %collective-permute-start.3) | collective-permute-done | bytes 32800 | tf_op jit(solution)/shard_map/ppermute | solution.py:372
  72.2 0.0 collective-permute-done.top_ref
  72.2 0.0 copy-start.2
  72.2 0.6 copy-done.4
  72.8 0.1 copy-done.1
  72.8 0.1 copy-done.2
  72.9 22.2 %push.1 = f32[256,16,128]{2,1,0:T(8,128)} custom-call(s32[8,128]{1,0:T(8,128)} %get-tuple-element.18.place_ref, s32[1]{0:T(128)} %bitcast.4.tile_ref, f32[1088,128]{1,0:T(8,128)} %get-tuple-element.20.field_ref, s32[256,128]{1,0:T(8,128)} %get-tuple-element.21.posn_ref, f32[256,128]{1,0:T(8,128)} %get-tuple-element.22.weight_ref, f32[272,128]{1,0:T(8,128)} %copy-done.1, ...), custom_call_target="tpu_custom_call" | custom-call | tf_op jit(solution)/shard_map/push/pallas_call | solution.py:316
  95.1 38.0 %all_to_all.22 = f32[128,2,16,128]{3,2,1,0:T(8,128)} all-to-all(f32[128,2,16,128]{3,2,1,0:T(8,128)} %bitcast.16), channel_id=1, replica_groups=mesh['face'=4,'tile'=32] {'face','tile'}, dimensions={0} | all-to-all | bytes 4194304 | tf_op jit(solution)/shard_map/all_to_all | solution.py:351
  133.1 6.7 %collect.1 = f32[1024,128]{1,0:T(8,128)} custom-call(s32[8,128]{1,0:T(8,128)} %get-tuple-element.17.slots_ref, f32[256,16,128]{2,1,0:T(8,128)} %bitcast.15), custom_call_target="tpu_custom_call" | custom-call | tf_op jit(solution)/shard_map/collect/pallas_call | solution.py:342
  (6 shorter events, 0.0 us)
Async XLA Ops:
  4.4 21.1 %all-to-all-start = ((s32[128,1,128]{2,1,0:T(1,128)}), s32[128,1,128]{2,1,0:T(1,128)S(1)}, u32[]{:S(2)}, u32[]{:S(2)}) async-start(s32[128,1,128]{2,1,0:T(1,128)} %bitcast.23), calls=%async_computation | async-start | bytes 131072 | tf_op jit(solution)/shard_map/all_to_all | solution.py:351
  25.5 0.6 copy-start
  60.5 11.7 %collective-permute-start = (f32[272,128]{1,0:T(8,128)}, f32[272,128]{1,0:T(8,128)S(1)}, u32[]{:S(2)}, u32[]{:S(2)}) collective-permute-start(f32[272,128]{1,0:T(8,128)} %get-tuple-element.23), channel_id=1, source_target_pairs={{0,1},{1,2},{2,3},{3,4},{4,5},{5,6},{6,7},{7,8},{8,9},{9,10},{10,1... | collective-permute-start | bytes 417800 | tf_op jit(solution)/shard_map/ppermute | solution.py:371
  62.6 9.6 %collective-permute-start.1 = (f32[272,128]{1,0:T(8,128)}, f32[272,128]{1,0:T(8,128)S(1)}, u32[]{:S(2)}, u32[]{:S(2)}) collective-permute-start(f32[272,128]{1,0:T(8,128)} %get-tuple-element.24), channel_id=1, source_target_pairs={{1,0},{2,1},{3,2},{4,3},{5,4},{6,5},{7,6},{8,7},{9,8},{10,9},{11,1... | collective-permute-start | bytes 417800 | tf_op jit(solution)/shard_map/ppermute | solution.py:370
  63.9 6.6 %collective-permute-start.2 = (f32[64,128]{1,0:T(8,128)}, f32[64,128]{1,0:T(8,128)S(1)}, u32[]{:S(2)}, u32[]{:S(2)}) collective-permute-start(f32[64,128]{1,0:T(8,128)} %get-tuple-element.25), channel_id=1, source_target_pairs={{0,32},{32,64},{64,96},{96,0},{1,33},{33,65},{65,97},{97,1},{2,34}... | collective-permute-start | bytes 98312 | tf_op jit(solution)/shard_map/ppermute | solution.py:373
  66.5 5.6 %collective-permute-start.3 = (f32[64,128]{1,0:T(8,128)}, f32[64,128]{1,0:T(8,128)S(1)}, u32[]{:S(2)}, u32[]{:S(2)}) collective-permute-start(f32[64,128]{1,0:T(8,128)} %get-tuple-element.26), channel_id=1, source_target_pairs={{32,0},{64,32},{96,64},{0,96},{33,1},{65,33},{97,65},{1,97},{34,2}... | collective-permute-start | bytes 98312 | tf_op jit(solution)/shard_map/ppermute | solution.py:372
  70.5 1.7 %copy-start.3 = (f32[64,128]{1,0:T(8,128)}, f32[64,128]{1,0:T(8,128)S(1)}, u32[]{:S(2)}) copy-start(f32[64,128]{1,0:T(8,128)S(1)} %collective-permute-done.2.left_ref) | copy-start | bytes 98308
  72.2 0.6 copy-start.4
  72.2 0.7 copy-start.1
  72.2 0.7 copy-start.2

commit v2 on v1

v2 whole, which is shorter than its diff:
```python
import jax
import jax.numpy as jnp
from jax import lax
from jax.experimental import pallas as pl
from jax.experimental.pallas import tpu as pltpu
from jax.sharding import PartitionSpec as P

RANGE = 8
FLOOR = 0.01
M = 16
BANDS = 64
LANES = 128
ROWS = 32
EXT = ROWS + 2 * RANGE
DEVICES = 128
POINTS = 4
QUADS = M // 4
TURN = 2 * LANES + 2 * RANGE
MESSAGE = M + 1
TOP = 32700.0
F32 = jnp.float32
I32 = jnp.int32
BF16 = jnp.bfloat16
AXES = ("face", "tile")


def struct(shape, dtype=F32):
    return jax.ShapeDtypeStruct(shape, dtype)


def lane_ids(rows=8):
    return lax.broadcasted_iota(I32, (rows, LANES), 1)


def row_ids(rows=8):
    return lax.broadcasted_iota(I32, (rows, LANES), 0)


def request_kernel(holder_ref, slot_ref, wanted_ref, place_ref):
    owner = lax.broadcasted_iota(I32, (DEVICES, BANDS), 0).astype(F32)
    band = lax.broadcasted_iota(I32, (1, BANDS), 1)
    big = float(1 << 20)
    hots, codes = [], []
    for k in range(2):
        holder = holder_ref[k : k + 1, :].astype(F32)
        code = (band + k * BANDS) * BANDS + slot_ref[k : k + 1, :]
        hots.append(holder == owner)
        codes.append(jnp.broadcast_to(code.astype(F32), (DEVICES, BANDS)))
    low = [jnp.min(jnp.where(h, c, big), axis=1, keepdims=True) for h, c in zip(hots, codes)]
    high = [jnp.max(jnp.where(h, c, -1.0), axis=1, keepdims=True) for h, c in zip(hots, codes)]
    first = jnp.minimum(low[0], low[1])
    last = jnp.maximum(high[0], high[1])
    slots = [
        jnp.where(last >= 0.0, first.astype(I32) & (BANDS - 1), 0),
        jnp.where(last > first, last.astype(I32) & (BANDS - 1), 0),
    ]
    lanes = lane_ids(DEVICES)
    wanted_ref[...] = jnp.where(lanes == 0, slots[0], jnp.where(lanes == 1, slots[1], 0))
    place_ref[...] = jnp.zeros((8, LANES), I32)
    for k in range(2):
        spot = 2.0 * owner + jnp.where(codes[k] == first, 0.0, 1.0)
        spot = jnp.sum(jnp.where(hots[k], spot, 0.0), axis=0, keepdims=True)
        place_ref[k : k + 1, :BANDS] = spot.astype(I32)


def request(holder, slot):
    return pl.pallas_call(
        request_kernel,
        out_shape=(struct((DEVICES, LANES), I32), struct((8, LANES), I32)),
        name="request",
    )(holder, slot)


def pack_kernel(asked_ref, bands_ref, out_ref, slots_ref, smem, sem):
    table = jnp.transpose(asked_ref[...].astype(F32))[:8].astype(I32)
    slots_ref[...] = table
    copy = pltpu.make_async_copy(slots_ref, smem, sem)
    copy.start()
    copy.wait()

    def step(i, carry):
        for r in range(2):
            out_ref[2 * i + r] = bands_ref[smem[r, i]]
        return carry

    lax.fori_loop(0, DEVICES, step, 0, unroll=8)


def pack(asked, bands):
    return pl.pallas_call(
        pack_kernel,
        out_shape=(struct((2 * DEVICES, M, LANES), BF16), struct((8, LANES), I32)),
        scratch_shapes=[pltpu.SMEM((8, LANES), I32), pltpu.SemaphoreType.DMA],
        name="pack",
    )(asked, bands)


def regrid_kernel(
    place_ref, recv_ref, pos_ref, factor_ref, truth_ref,
    field_ref, turned_ref, posn_ref, weight_ref, north_ref, south_ref, west_ref, east_ref,
    low_ref, high_ref,
):
    def spread(row, carry):
        for half in range(2):
            for k, tab in enumerate((low_ref, high_ref)):
                strip = recv_ref[place_ref[k, 2 * row + half]].astype(F32)
                tab[pl.ds(half * ROWS + row, M, stride=BANDS), :] = strip
        return carry

    lax.fori_loop(0, ROWS, spread, 0, unroll=4)

    for half in range(2):
        factors = [factor_ref[pl.ds(j * BANDS + half, ROWS, stride=2), :] for j in range(POINTS)]
        total = factors[0] + factors[1] + factors[2] + factors[3]
        for j in range(POINTS):
            spot = j * BANDS + half * ROWS
            posn_ref[pl.ds(spot, ROWS), :] = pos_ref[pl.ds(j * BANDS + half, ROWS, stride=2), :]
            weight_ref[pl.ds(spot, ROWS), :] = factors[j] / total

    def regrid(block, carry):
        row = pl.multiple_of(block * 8, 8)
        posn = [posn_ref[pl.ds(j * BANDS + row, 8), :] for j in range(POINTS)]
        weight = [weight_ref[pl.ds(j * BANDS + row, 8), :] for j in range(POINTS)]
        lane = [p & (LANES - 1) for p in posn]
        upper = [p >= LANES for p in posn]
        for m in range(M):
            low = low_ref[pl.ds(m * BANDS + row, 8), :]
            high = high_ref[pl.ds(m * BANDS + row, 8), :]
            out = jnp.zeros((8, LANES), F32)
            for j in range(POINTS):
                a = jnp.take_along_axis(low, lane[j], axis=1, mode="promise_in_bounds")
                b = jnp.take_along_axis(high, lane[j], axis=1, mode="promise_in_bounds")
                out = out + weight[j] * jnp.where(upper[j], b, a)
            field_ref[pl.ds(m * BANDS + row, 8), :] = out
        return carry

    lax.fori_loop(0, BANDS // 8, regrid, 0)

    for half in range(2):
        field_ref[pl.ds(M * BANDS + half * ROWS, ROWS), :] = truth_ref[:, half * LANES : (half + 1) * LANES]
    for m in range(M + 1):
        for half in range(2):
            spot = m * BANDS + half * ROWS
            north_ref[pl.ds((2 * m + half) * 8, 8), :] = field_ref[pl.ds(spot, 8), :]
            south_ref[pl.ds((2 * m + half) * 8, 8), :] = field_ref[pl.ds(spot + ROWS - 8, 8), :]
    for q in range(QUADS + 1):
        for half in range(2):
            if q < QUADS:
                parts = [field_ref[pl.ds((4 * q + i) * BANDS + half * ROWS, ROWS), :] for i in range(4)]
            else:
                parts = [truth_ref[:, half * LANES : (half + 1) * LANES]] * 4
            turned = jnp.transpose(jnp.concatenate(parts, axis=0))
            turned_ref[pl.ds(q * 2 * LANES + half * LANES, LANES), :] = turned
            if half == 0:
                west_ref[pl.ds(q * 8, 8), :] = turned[:8]
            else:
                east_ref[pl.ds(q * 8, 8), :] = turned[LANES - 8 :]


VMEM = pl.BlockSpec(memory_space=pltpu.VMEM)
SMEM = pl.BlockSpec(memory_space=pltpu.SMEM)


def regrid(place, recv, pos, factor, truth):
    tall = struct(((M + 1) * 2 * RANGE, LANES))
    wide = struct(((QUADS + 1) * RANGE, LANES))
    return pl.pallas_call(
        regrid_kernel,
        in_specs=[SMEM, VMEM, VMEM, VMEM, VMEM],
        out_shape=(
            struct(((M + 1) * BANDS, LANES)),
            struct(((QUADS + 1) * 2 * LANES, LANES)),
            struct((POINTS * BANDS, LANES), I32),
            struct((POINTS * BANDS, LANES)),
            tall, tall, wide, wide,
        ),
        scratch_shapes=[pltpu.VMEM((M * BANDS, LANES), F32)] * 2,
        name="regrid",
    )(place, recv, pos, factor, truth)


def steep(diff):
    root = lax.rsqrt(diff * diff + FLOOR)
    value = lax.rsqrt(root)
    return value, (diff * root) * (value * root)


def push_kernel(
    place_ref, tile_ref, field_ref, turned_ref, posn_ref, weight_ref, top_ref, bottom_ref, left_ref, right_ref,
    out_ref, ext, grad, side, turn,
):
    for mh in range(2 * (M + 1)):
        ext[pl.ds(mh * EXT, 8), :] = top_ref[pl.ds(mh * 8, 8), :]
        ext[pl.ds(mh * EXT + 8, ROWS), :] = field_ref[pl.ds(mh * ROWS, ROWS), :]
        ext[pl.ds(mh * EXT + 8 + ROWS, 8), :] = bottom_ref[pl.ds(mh * 8, 8), :]
    for q in range(QUADS + 1):
        side[pl.ds(q * TURN, 8), :] = left_ref[pl.ds(q * 8, 8), :]
        side[pl.ds(q * TURN + 8, 2 * LANES), :] = turned_ref[pl.ds(q * 2 * LANES, 2 * LANES), :]
        side[pl.ds(q * TURN + 8 + 2 * LANES, 8), :] = right_ref[pl.ds(q * 8, 8), :]
    grad[...] = jnp.zeros_like(grad)
    turn[...] = jnp.zeros_like(turn)
    out_ref[...] = jnp.zeros_like(out_ref)
    first_row = tile_ref[0] * ROWS - RANGE

    def latitude(step, carry):
        half = step // 5
        block = step % 5
        base = pl.multiple_of(half * EXT + block * 8, 8)
        rows = row_ids() + (first_row + block * 8)
        for k in range(1, RANGE + 1):
            def diff(m):
                here = base + m * 2 * EXT
                return ext[pl.ds(here, 8), :] - ext[pl.ds(here + k, 8), :]

            total = jnp.zeros((8, LANES), F32)
            slopes = []
            for m in range(M):
                value, slope = steep(diff(m))
                total = total + value
                slopes.append(slope)
            seen, unused = steep(diff(M))
            inside = (rows >= 0) & (rows + k < ROWS * 32)
            push = jnp.where(inside, (1.0 / (k * M)) * (seen - total * (1.0 / M)), 0.0)
            for m in range(M):
                pushed = push * slopes[m]
                here = base + m * 2 * EXT
                grad[pl.ds(here, 8), :] -= pushed
                grad[pl.ds(here + k, 8), :] += pushed
        return carry

    lax.fori_loop(0, 10, latitude, 0)

    def longitude(block, carry):
        base = pl.multiple_of(block * 8, 8)
        for k in range(1, RANGE + 1):
            def diff(q):
                here = base + q * TURN
                return side[pl.ds(here, 8), :] - side[pl.ds(here + k, 8), :]

            total = jnp.zeros((8, LANES), F32)
            slopes = []
            for q in range(QUADS):
                value, slope = steep(diff(q))
                total = total + value
                slopes.append(slope)
            total = total + pltpu.roll(total, 2 * ROWS, 1)
            total = total + pltpu.roll(total, ROWS, 1)
            seen, unused = steep(diff(QUADS))
            push = (1.0 / (k * M)) * (seen - total * (1.0 / M))
            for q in range(QUADS):
                pushed = push * slopes[q]
                here = base + q * TURN
                turn[pl.ds(here, 8), :] -= pushed
                turn[pl.ds(here + k, 8), :] += pushed
        return carry

    lax.fori_loop(0, TURN // 8 - 1, longitude, 0)

    for q in range(QUADS):
        for half in range(2):
            back = jnp.transpose(turn[pl.ds(q * TURN + 8 + half * LANES, LANES), :])
            for i in range(4):
                spot = ((4 * q + i) * 2 + half) * EXT + 8
                grad[pl.ds(spot, ROWS), :] += back[i * ROWS : (i + 1) * ROWS]

    cells = [(lax.broadcasted_iota(I32, (16, LANES), 0) + 16 * i).astype(F32).astype(BF16) for i in range(16)]
    one, zero = jnp.ones((16, LANES), BF16), jnp.zeros((16, LANES), BF16)

    def adjoint(row, carry):
        for half in range(2):
            tile = grad[pl.ds(half * EXT + 8 + row, M, stride=2 * EXT), :]
            parts, hots = [], []
            for j in range(POINTS):
                spot = j * BANDS + half * ROWS + row
                parts.append(tile * weight_ref[pl.ds(spot, 1), :])
                posn = jnp.broadcast_to(posn_ref[pl.ds(spot, 1), :].astype(F32), (16, LANES)).astype(BF16)
                hots.append(jnp.concatenate([jnp.where(c == posn, one, zero) for c in cells], axis=0))
            part = jnp.concatenate(parts, axis=1)
            high = part.astype(BF16)
            low = (part - high.astype(F32)).astype(BF16)
            both = lax.dot_general(
                jnp.concatenate([high, low], axis=0),
                jnp.concatenate(hots, axis=1),
                (((1,), (1,)), ((), ())),
                preferred_element_type=F32,
            )
            both = both[:M] + both[M:]
            for k in range(2):
                strip = both[:, k * LANES : (k + 1) * LANES]
                largest = jnp.maximum(jnp.max(jnp.abs(strip), axis=0, keepdims=True), 1e-36)
                scale = jnp.ceil(jnp.log2(largest) * 256.0)
                code = jnp.round(strip * (jnp.exp2(scale * (-1.0 / 256.0)) * TOP)).astype(I32)
                place = place_ref[k, 2 * row + half]
                spot = (place >> 1) * MESSAGE
                shift = (place & 1) * 16
                out_ref[pl.ds(spot, M), :] |= (code & 0xFFFF) << shift
                out_ref[pl.ds(spot + M, 1), :] |= (scale.astype(I32) & 0xFFFF) << shift
        return carry

    lax.fori_loop(0, ROWS, adjoint, 0)


def push(place, tile, field, turned, posn, weight, top, bottom, left, right):
    return pl.pallas_call(
        push_kernel,
        in_specs=[SMEM, SMEM] + [VMEM] * 8,
        out_shape=struct((DEVICES * MESSAGE, LANES), I32),
        scratch_shapes=[
            pltpu.VMEM((2 * (M + 1) * EXT, LANES), F32),
            pltpu.VMEM((2 * M * EXT, LANES), F32),
            pltpu.VMEM(((QUADS + 1) * TURN, LANES), F32),
            pltpu.VMEM((QUADS * TURN, LANES), F32),
        ],
        name="push",
    )(place, tile, field, turned, posn, weight, top, bottom, left, right)


def collect_kernel(slots_ref, back_ref, out_ref, sums):
    sums[...] = jnp.zeros_like(sums)

    def step(i, carry):
        codes = back_ref[pl.ds(i * MESSAGE, M), :]
        scales = back_ref[pl.ds(i * MESSAGE + M, 1), :]
        for r in range(2):
            code, scale = [((x << 16) if r == 0 else x) >> 16 for x in (codes, scales)]
            scale = jnp.exp2(scale.astype(F32) * (1.0 / 256.0)) * (1.0 / TOP)
            sums[slots_ref[r, i]] += code.astype(F32) * scale
        return carry

    lax.fori_loop(0, DEVICES, step, 0, unroll=4)

    def turn(s, carry):
        out_ref[pl.ds(s, M, stride=BANDS), :] = sums[s]
        return carry

    lax.fori_loop(0, BANDS, turn, 0, unroll=8)


def collect(slots, back):
    return pl.pallas_call(
        collect_kernel,
        in_specs=[SMEM, VMEM],
        out_shape=struct((M * BANDS, LANES)),
        scratch_shapes=[pltpu.VMEM((BANDS, M, LANES), F32)],
        name="collect",
    )(slots, back)


def exchange(x):
    return lax.all_to_all(x, AXES, split_axis=0, concat_axis=0, tiled=True)


def local(predicted_field, parent_band_holder, parent_band_slot, neighbour_positions, unscaled_neighbour_factor, truth_field):
    tiles, faces = lax.axis_size("tile"), lax.axis_size("face")
    bands = jnp.transpose(predicted_field, (1, 0, 2))
    wanted, place = request(parent_band_holder.T, parent_band_slot.T)
    asked = exchange(wanted)
    outgoing, slots = pack(asked, bands)
    recv = exchange(outgoing.reshape(DEVICES, 2, M, LANES)).reshape(2 * DEVICES, M, LANES)
    field, turned, posn, weight, north, south, west, east = regrid(
        place,
        recv,
        neighbour_positions.reshape(POINTS * BANDS, LANES),
        unscaled_neighbour_factor.reshape(POINTS * BANDS, LANES),
        truth_field,
    )
    up = [(i + 1, i) for i in range(tiles - 1)]
    down = [(i, i + 1) for i in range(tiles - 1)]
    bottom = lax.ppermute(north, "tile", up)
    top = lax.ppermute(south, "tile", down)
    right = lax.ppermute(west, "face", [((i + 1) % faces, i) for i in range(faces)])
    left = lax.ppermute(east, "face", [(i, (i + 1) % faces) for i in range(faces)])
    tile = lax.axis_index("tile").astype(I32).reshape(1)
    back = push(place, tile, field, turned, posn, weight, top, bottom, left, right)
    back = exchange(back.reshape(DEVICES, MESSAGE, 1, LANES)).reshape(DEVICES * MESSAGE, LANES)
    return collect(slots, back).reshape(M, BANDS, LANES)


def solution(mesh):
    in_specs = (
        P(None, AXES, None),
        P(AXES, None),
        P(AXES, None),
        P(None, AXES, None),
        P(None, AXES, None),
        P("tile", "face"),
    )
    return jax.shard_map(local, mesh=mesh, in_specs=in_specs, out_specs=P(None, AXES, None), check_vma=False)
```

time: 140 us -> 127 us (0.907)
  blocking collectives: 62.7 us -> 52.6 us
  local copies, waits for them, and re-layouts: 5.89 us -> 3.14 us
    all_to_all x2, blocking collectives: 62.7 us -> 52.6 us  [exchange(): return lax.all_to_all(x, AXES, split_axis=0, concat_axis=0, tiled=True)]
    unnamed x13 -> x11, local copies, waits for them, and re-layouts: 5.89 us -> 3.14 us
    pallas_call x1, Pallas kernels: 6.65 us -> 3.98 us  [collect(): pl.pallas_call(collect_kernel, in_specs=[SMEM, VMEM], out_shape=struct((M...]
    ppermute x1, waiting for transfers between devices: 3.95 us -> 1.37 us  [local(): lax.ppermute(east, 'face', [(i, (i + 1) % faces) for i in range(faces)])]
    pallas_call x1, Pallas kernels: 22.2 us -> 24.7 us  [push(): pl.pallas_call(push_kernel, in_specs=[SMEM, SMEM] + [VMEM] * 8, out_shape...]
    ppermute x1, waiting for transfers between devices: 1.67 us -> 3.98 us  [local(): lax.ppermute(west, 'face', [((i + 1) % faces, i) for i in range(faces)])]
where the time goes in v2:
time: 127 us; the launch traced here: 126 us
  blocking collectives  52.6 us (41%)
  Pallas kernels  39.9 us (31%)
  starting transfers between devices  17.5 us (14%)
  waiting for transfers between devices  13.1 us (10%)
  local copies, waits for them, and re-layouts  3.14 us (2%)
    all_to_all x2, blocking collectives, exchange(): return lax.all_to_all(x, AXES, split_axis=0, concat_axis=0, tiled=True)  52.6 us
    pallas_call x1, Pallas kernels, push(): pl.pallas_call(push_kernel, in_specs=[SMEM, SMEM] + [VMEM] * 8, out_shape...  24.7 us
    all_to_all x1, starting transfers between devices, exchange(): return lax.all_to_all(x, AXES, split_axis=0, concat_axis=0, tiled=True)  11.5 us
    all_to_all x1, waiting for transfers between devices, exchange(): return lax.all_to_all(x, AXES, split_axis=0, concat_axis=0, tiled=True)  7.77 us
    pallas_call x1, Pallas kernels, regrid(): pl.pallas_call(regrid_kernel, in_specs=[SMEM, VMEM, VMEM, VMEM, VMEM], ou...  6.62 us
    ppermute x1, waiting for transfers between devices, local(): lax.ppermute(west, 'face', [((i + 1) % faces, i) for i in range(faces)])  3.98 us
    pallas_call x1, Pallas kernels, collect(): pl.pallas_call(collect_kernel, in_specs=[SMEM, VMEM], out_shape=struct((M...  3.98 us
    pallas_call x1, Pallas kernels, pack(): pl.pallas_call(pack_kernel, out_shape=(struct((2 * DEVICES, M, LANES), BF...  3.15 us
  transfers between devices with their start and end apart: 5, of which 3 were waited for; matrix products, arithmetic and copies ran while one was open for 1% of the time, Pallas kernels for 0%

profile of v2, /device:TPU:1, one launch (start us, length us, event | category | flops | bytes accessed | tf_op | source)
XLA Modules:
  0.0 126.4 jit_solution(2721154150676619012)
XLA Ops:
  0.0 1.5 %request.1 = (s32[128,128]{1,0:T(8,128)}, s32[8,128]{1,0:T(8,128)}) custom-call(s32[2,64]{1,0:T(2,128)} %bitcast.26, s32[2,64]{1,0:T(2,128)} %bitcast.27), custom_call_target="tpu_custom_call" | custom-call | tf_op jit(solution)/shard_map/request/pallas_call | solution.py:67
  1.5 11.5 %all-to-all-start = ((s32[128,1,128]{2,1,0:T(1,128)}), s32[128,1,128]{2,1,0:T(1,128)S(1)}, u32[]{:S(2)}, u32[]{:S(2)}) async-start(s32[128,1,128]{2,1,0:T(1,128)} %bitcast.25), calls=%async_computation | async-start | bytes 131072 | tf_op jit(solution)/shard_map/all_to_all | solution.py:350
  13.0 1.8 %copy.13 = bf16[16,64,128]{2,0,1:T(8,128)(2,1)} copy(bf16[16,64,128]{2,1,0:T(8,128)(2,1)} %param.6) | data formatting | bytes 524288 | tf_op args[0]
  14.8 7.8 %all-to-all-done = s32[128,1,128]{2,1,0:T(1,128)S(1)} async-done(((s32[128,1,128]{2,1,0:T(1,128)}), s32[128,1,128]{2,1,0:T(1,128)S(1)}, u32[]{:S(2)}, u32[]{:S(2)}) %all-to-all-start) | async-done | bytes 65568 | tf_op jit(solution)/shard_map/all_to_all | solution.py:350
  22.6 0.6 copy-done
  23.2 3.2 %pack.1 = (bf16[256,16,128]{2,1,0:T(8,128)(2,1)}, s32[8,128]{1,0:T(8,128)}) custom-call(s32[128,128]{1,0:T(8,128)} %bitcast.22, bf16[64,16,128]{2,1,0:T(8,128)(2,1)} %bitcast.20), custom_call_target="tpu_custom_call" | custom-call | tf_op jit(solution)/shard_map/pack/pallas_call | solution.py:90
  26.4 24.7 %all_to_all.21 = bf16[128,2,16,128]{3,2,1,0:T(8,128)(2,1)} all-to-all(bf16[128,2,16,128]{3,2,1,0:T(8,128)(2,1)} %bitcast.21), channel_id=1, replica_groups=mesh['face'=4,'tile'=32] {'face','tile'}, dimensions={0} | all-to-all | bytes 2097152 | tf_op jit(solution)/shard_map/all_to_all | solution.py:350
  51.1 6.6 %regrid.1 = (f32[1088,128]{1,0:T(8,128)}, f32[1280,128]{1,0:T(8,128)}, s32[256,128]{1,0:T(8,128)}, f32[256,128]{1,0:T(8,128)}, f32[272,128]{1,0:T(8,128)}, /*ind...) custom-call(s32[8,128]{1,0:T(8,128)} %get-tuple-element.19.place_ref, bf16[256,16,128]{2,1,0:T(8,128)(2,1)} %bitcast.19, ...), custom_call_target="tpu_custom_call" | custom-call | tf_op jit(solution)/shard_map/regrid/pallas_call | solution.py:167
  57.7 2.0 %collective-permute-start = (f32[272,128]{1,0:T(8,128)}, f32[272,128]{1,0:T(8,128)S(1)}, u32[]{:S(2)}, u32[]{:S(2)}) collective-permute-start(f32[272,128]{1,0:T(8,128)} %get-tuple-element.25), channel_id=1, source_target_pairs={{0,1},{1,2},{2,3},{3,4},{4,5},{5,6},{6,7},{7,8},{8,9},{9,10},{10,1... | collective-permute-start | bytes 417800 | tf_op jit(solution)/shard_map/ppermute | solution.py:370
  59.7 1.3 %collective-permute-start.1 = (f32[272,128]{1,0:T(8,128)}, f32[272,128]{1,0:T(8,128)S(1)}, u32[]{:S(2)}, u32[]{:S(2)}) collective-permute-start(f32[272,128]{1,0:T(8,128)} %get-tuple-element.26), channel_id=1, source_target_pairs={{1,0},{2,1},{3,2},{4,3},{5,4},{6,5},{7,6},{8,7},{9,8},{10,9},{11,1... | collective-permute-start | bytes 417800 | tf_op jit(solution)/shard_map/ppermute | solution.py:369
  61.0 2.7 %collective-permute-start.2 = (f32[40,128]{1,0:T(8,128)}, f32[40,128]{1,0:T(8,128)S(1)}, u32[]{:S(2)}, u32[]{:S(2)}) collective-permute-start(f32[40,128]{1,0:T(8,128)} %get-tuple-element.27), channel_id=1, source_target_pairs={{0,32},{32,64},{64,96},{96,0},{1,33},{33,65},{65,97},{97,1},{2,34}... | collective-permute-start | bytes 61448 | tf_op jit(solution)/shard_map/ppermute | solution.py:372
  63.7 0.0 collective-permute-start.3
  63.7 1.4 %collective-permute-done.2.left_ref = f32[40,128]{1,0:T(8,128)S(1)} collective-permute-done((f32[40,128]{1,0:T(8,128)}, f32[40,128]{1,0:T(8,128)S(1)}, u32[]{:S(2)}, u32[]{:S(2)}) %collective-permute-start.2) | collective-permute-done | bytes 20512 | tf_op jit(solution)/shard_map/ppermute | solution.py:372
  65.1 4.0 %collective-permute-done.3.right_ref = f32[40,128]{1,0:T(8,128)S(1)} collective-permute-done((f32[40,128]{1,0:T(8,128)}, f32[40,128]{1,0:T(8,128)S(1)}, u32[]{:S(2)}, u32[]{:S(2)}) %collective-permute-start.3) | collective-permute-done | bytes 20512 | tf_op jit(solution)/shard_map/ppermute | solution.py:371
  69.1 0.0 collective-permute-done.top_ref
  69.1 0.0 collective-permute-done.1.bottom_ref
  69.1 0.0 copy-start.2
  69.1 0.0 copy-done.3
  69.1 0.6 copy-done.4
  69.7 0.1 copy-done.1
  69.7 0.1 copy-done.2
  69.8 24.7 %push.1 = s32[2176,128]{1,0:T(8,128)} custom-call(s32[8,128]{1,0:T(8,128)} %get-tuple-element.19.place_ref, s32[1]{0:T(128)} %bitcast.6.tile_ref, f32[1088,128]{1,0:T(8,128)} %get-tuple-element.21.field_ref, f32[1280,128]{1,0:T(8,128)} %get-tuple-element.22.turned_ref, s32[256,128]{1,0:T(8,128)} %get-tuple-element.23.posn_ref, ...), custom_call_target="tpu_custom_call" | custom-call | tf_op jit(solution)/shard_map/push/pallas_call | solution.py:304
  94.4 27.9 %all_to_all.22 = s32[128,17,1,128]{3,2,1,0:T(1,128)} all-to-all(s32[128,17,1,128]{3,2,1,0:T(1,128)} %bitcast.17), channel_id=1, replica_groups=mesh['face'=4,'tile'=32] {'face','tile'}, dimensions={0} | all-to-all | bytes 2228224 | tf_op jit(solution)/shard_map/all_to_all | solution.py:350
  122.4 4.0 %collect.1 = f32[1024,128]{1,0:T(8,128)} custom-call(s32[8,128]{1,0:T(8,128)} %get-tuple-element.18.slots_ref, s32[2176,128]{1,0:T(8,128)} %bitcast.18), custom_call_target="tpu_custom_call" | custom-call | tf_op jit(solution)/shard_map/collect/pallas_call | solution.py:340
  (4 shorter events, 0.0 us)
Async XLA Ops:
  1.5 21.1 %all-to-all-start = ((s32[128,1,128]{2,1,0:T(1,128)}), s32[128,1,128]{2,1,0:T(1,128)S(1)}, u32[]{:S(2)}, u32[]{:S(2)}) async-start(s32[128,1,128]{2,1,0:T(1,128)} %bitcast.25), calls=%async_computation | async-start | bytes 131072 | tf_op jit(solution)/shard_map/all_to_all | solution.py:350
  22.6 0.6 copy-start
  57.7 11.4 %collective-permute-start = (f32[272,128]{1,0:T(8,128)}, f32[272,128]{1,0:T(8,128)S(1)}, u32[]{:S(2)}, u32[]{:S(2)}) collective-permute-start(f32[272,128]{1,0:T(8,128)} %get-tuple-element.25), channel_id=1, source_target_pairs={{0,1},{1,2},{2,3},{3,4},{4,5},{5,6},{6,7},{7,8},{8,9},{9,10},{10,1... | collective-permute-start | bytes 417800 | tf_op jit(solution)/shard_map/ppermute | solution.py:370
  59.7 9.3 %collective-permute-start.1 = (f32[272,128]{1,0:T(8,128)}, f32[272,128]{1,0:T(8,128)S(1)}, u32[]{:S(2)}, u32[]{:S(2)}) collective-permute-start(f32[272,128]{1,0:T(8,128)} %get-tuple-element.26), channel_id=1, source_target_pairs={{1,0},{2,1},{3,2},{4,3},{5,4},{6,5},{7,6},{8,7},{9,8},{10,9},{11,1... | collective-permute-start | bytes 417800 | tf_op jit(solution)/shard_map/ppermute | solution.py:369
  61.0 4.1 %collective-permute-start.2 = (f32[40,128]{1,0:T(8,128)}, f32[40,128]{1,0:T(8,128)S(1)}, u32[]{:S(2)}, u32[]{:S(2)}) collective-permute-start(f32[40,128]{1,0:T(8,128)} %get-tuple-element.27), channel_id=1, source_target_pairs={{0,32},{32,64},{64,96},{96,0},{1,33},{33,65},{65,97},{97,1},{2,34}... | collective-permute-start | bytes 61448 | tf_op jit(solution)/shard_map/ppermute | solution.py:372
  63.7 5.4 %collective-permute-start.3 = (f32[40,128]{1,0:T(8,128)}, f32[40,128]{1,0:T(8,128)S(1)}, u32[]{:S(2)}, u32[]{:S(2)}) collective-permute-start(f32[40,128]{1,0:T(8,128)} %get-tuple-element.28), channel_id=1, source_target_pairs={{32,0},{64,32},{96,64},{0,96},{33,1},{65,33},{97,65},{1,97},{34,2}... | collective-permute-start | bytes 61448 | tf_op jit(solution)/shard_map/ppermute | solution.py:371
  65.1 4.0 %copy-start.3 = (f32[40,128]{1,0:T(8,128)}, f32[40,128]{1,0:T(8,128)S(1)}, u32[]{:S(2)}) copy-start(f32[40,128]{1,0:T(8,128)S(1)} %collective-permute-done.2.left_ref) | copy-start | bytes 61444
  69.1 0.6 copy-start.4
  69.1 0.6 copy-start.1
  69.1 0.7 copy-start.2

commit v3 on v2

--- a/solution.py
+++ b/solution.py
@@ -68,6 +68,7 @@
         request_kernel,
         out_shape=(struct((DEVICES, LANES), I32), struct((8, LANES), I32)),
         name="request",
+        compiler_params=pltpu.CompilerParams(vmem_limit_bytes=1 << 20),
     )(holder, slot)
 
 
@@ -92,6 +93,7 @@
         out_shape=(struct((2 * DEVICES, M, LANES), BF16), struct((8, LANES), I32)),
         scratch_shapes=[pltpu.SMEM((8, LANES), I32), pltpu.SemaphoreType.DMA],
         name="pack",
+        compiler_params=pltpu.CompilerParams(vmem_limit_bytes=4 << 20),
     )(asked, bands)
 
 
@@ -121,17 +123,17 @@
         row = pl.multiple_of(block * 8, 8)
         posn = [posn_ref[pl.ds(j * BANDS + row, 8), :] for j in range(POINTS)]
         weight = [weight_ref[pl.ds(j * BANDS + row, 8), :] for j in range(POINTS)]
-        lane = [p & (LANES - 1) for p in posn]
-        upper = [p >= LANES for p in posn]
+        sums = [jnp.zeros((8, LANES), F32)] * M
+        for j in range(POINTS):
+            lane, upper = posn[j] & (LANES - 1), posn[j] >= LANES
+            for m in range(M):
+                a, b = [
+                    jnp.take_along_axis(tab[pl.ds(m * BANDS + row, 8), :], lane, axis=1, mode="promise_in_bounds")
+                    for tab in (low_ref, high_ref)
+                ]
+                sums[m] = sums[m] + weight[j] * jnp.where(upper, b, a)
         for m in range(M):
-            low = low_ref[pl.ds(m * BANDS + row, 8), :]
-            high = high_ref[pl.ds(m * BANDS + row, 8), :]
-            out = jnp.zeros((8, LANES), F32)
-            for j in range(POINTS):
-                a = jnp.take_along_axis(low, lane[j], axis=1, mode="promise_in_bounds")
-                b = jnp.take_along_axis(high, lane[j], axis=1, mode="promise_in_bounds")
-                out = out + weight[j] * jnp.where(upper[j], b, a)
-            field_ref[pl.ds(m * BANDS + row, 8), :] = out
+            field_ref[pl.ds(m * BANDS + row, 8), :] = sums[m]
         return carry
 
     lax.fori_loop(0, BANDS // 8, regrid, 0)
@@ -176,6 +178,7 @@
         ),
         scratch_shapes=[pltpu.VMEM((M * BANDS, LANES), F32)] * 2,
         name="regrid",
+        compiler_params=pltpu.CompilerParams(vmem_limit_bytes=8 << 20),
     )(place, recv, pos, factor, truth)
 
 
@@ -187,7 +190,7 @@
 
 def push_kernel(
     place_ref, tile_ref, field_ref, turned_ref, posn_ref, weight_ref, top_ref, bottom_ref, left_ref, right_ref,
-    out_ref, ext, grad, side, turn,
+    out_ref, ext, grad, side, turn, kept_rows, kept_columns,
 ):
     for mh in range(2 * (M + 1)):
         ext[pl.ds(mh * EXT, 8), :] = top_ref[pl.ds(mh * 8, 8), :]
@@ -197,16 +200,21 @@
         side[pl.ds(q * TURN, 8), :] = left_ref[pl.ds(q * 8, 8), :]
         side[pl.ds(q * TURN + 8, 2 * LANES), :] = turned_ref[pl.ds(q * 2 * LANES, 2 * LANES), :]
         side[pl.ds(q * TURN + 8 + 2 * LANES, 8), :] = right_ref[pl.ds(q * 8, 8), :]
-    grad[...] = jnp.zeros_like(grad)
-    turn[...] = jnp.zeros_like(turn)
     out_ref[...] = jnp.zeros_like(out_ref)
     first_row = tile_ref[0] * ROWS - RANGE
+
+    def ending(kept, spot, pushed, k):
+        moved = pltpu.roll(pushed, k % 8, 0)
+        earlier = kept[spot]
+        kept[spot] = moved
+        return jnp.where(row_ids() >= k, moved, earlier)
 
     def latitude(step, carry):
         half = step // 5
         block = step % 5
         base = pl.multiple_of(half * EXT + block * 8, 8)
         rows = row_ids() + (first_row + block * 8)
+        sums = [jnp.zeros((8, LANES), F32)] * M
         for k in range(1, RANGE + 1):
             def diff(m):
                 here = base + m * 2 * EXT
@@ -223,38 +231,38 @@
             push = jnp.where(inside, (1.0 / (k * M)) * (seen - total * (1.0 / M)), 0.0)
             for m in range(M):
                 pushed = push * slopes[m]
-                here = base + m * 2 * EXT
-                grad[pl.ds(here, 8), :] -= pushed
-                grad[pl.ds(here + k, 8), :] += pushed
-        return carry
-
-    lax.fori_loop(0, 10, latitude, 0)
+                sums[m] = sums[m] - pushed + ending(kept_rows, (k - 1) * M + m, pushed, k)
+        for m in range(M):
+            grad[pl.ds(base + m * 2 * EXT, 8), :] = sums[m]
+        return carry
+
+    lax.fori_loop(0, 10, latitude, 0, unroll=2)
 
     def longitude(block, carry):
         base = pl.multiple_of(block * 8, 8)
+        totals, slopes, sights = [], [], []
         for k in range(1, RANGE + 1):
             def diff(q):
                 here = base + q * TURN
                 return side[pl.ds(here, 8), :] - side[pl.ds(here + k, 8), :]
 
-            total = jnp.zeros((8, LANES), F32)
-            slopes = []
+            pairs = [steep(diff(q)) for q in range(QUADS)]
+            slopes.append([p[1] for p in pairs])
+            totals.append((pairs[0][0] + pairs[1][0]) + (pairs[2][0] + pairs[3][0]))
+            sights.append(steep(diff(QUADS))[0])
+        totals = [t + pltpu.roll(t, 2 * ROWS, 1) for t in totals]
+        totals = [t + pltpu.roll(t, ROWS, 1) for t in totals]
+        sums = [jnp.zeros((8, LANES), F32)] * QUADS
+        for k in range(1, RANGE + 1):
+            push = (1.0 / (k * M)) * (sights[k - 1] - totals[k - 1] * (1.0 / M))
             for q in range(QUADS):
-                value, slope = steep(diff(q))
-                total = total + value
-                slopes.append(slope)
-            total = total + pltpu.roll(total, 2 * ROWS, 1)
-            total = total + pltpu.roll(total, ROWS, 1)
-            seen, unused = steep(diff(QUADS))
-            push = (1.0 / (k * M)) * (seen - total * (1.0 / M))
-            for q in range(QUADS):
-                pushed = push * slopes[q]
-                here = base + q * TURN
-                turn[pl.ds(here, 8), :] -= pushed
-                turn[pl.ds(here + k, 8), :] += pushed
-        return carry
-
-    lax.fori_loop(0, TURN // 8 - 1, longitude, 0)
+                pushed = push * slopes[k - 1][q]
+                sums[q] = sums[q] - pushed + ending(kept_columns, (k - 1) * QUADS + q, pushed, k)
+        for q in range(QUADS):
+            turn[pl.ds(base + q * TURN, 8), :] = sums[q]
+        return carry
+
+    lax.fori_loop(0, TURN // 8 - 1, longitude, 0, unroll=3)
 
     for q in range(QUADS):
         for half in range(2):
@@ -297,7 +305,7 @@
                 out_ref[pl.ds(spot + M, 1), :] |= (scale.astype(I32) & 0xFFFF) << shift
         return carry
 
-    lax.fori_loop(0, ROWS, adjoint, 0)
+    lax.fori_loop(0, ROWS, adjoint, 0, unroll=4)
 
 
 def push(place, tile, field, turned, posn, weight, top, bottom, left, right):
@@ -310,8 +318,11 @@
             pltpu.VMEM((2 * M * EXT, LANES), F32),
             pltpu.VMEM(((QUADS + 1) * TURN, LANES), F32),
             pltpu.VMEM((QUADS * TURN, LANES), F32),
+            pltpu.VMEM((RANGE * M, 8, LANES), F32),
+            pltpu.VMEM((RANGE * QUADS, 8, LANES), F32),
         ],
         name="push",
+        compiler_params=pltpu.CompilerParams(vmem_limit_bytes=12 << 20),
     )(place, tile, field, turned, posn, weight, top, bottom, left, right)
 
 
@@ -343,6 +354,7 @@
         out_shape=struct((M * BANDS, LANES)),
         scratch_shapes=[pltpu.VMEM((BANDS, M, LANES), F32)],
         name="collect",
+        compiler_params=pltpu.CompilerParams(vmem_limit_bytes=5 << 20),
     )(slots, back)
 
 

time: 127 us -> 107 us (0.84)
  Pallas kernels: 39.9 us -> 21.8 us
    pallas_call x1, Pallas kernels: 24.7 us -> 12.9 us  [push(): pl.pallas_call(push_kernel, in_specs=[SMEM, SMEM] + [VMEM] * 8, out_shape...]
    pallas_call x1, Pallas kernels: 6.62 us -> 3.64 us  [regrid(): pl.pallas_call(regrid_kernel, in_specs=[SMEM, VMEM, VMEM, VMEM, VMEM], ou...]
    pallas_call x1, Pallas kernels: 3.15 us -> 1.15 us  [pack(): pl.pallas_call(pack_kernel, out_shape=(struct((2 * DEVICES, M, LANES), BF...]
where the time goes in v3:
time: 107 us
  blocking collectives  51.4 us (48%)
  Pallas kernels  21.8 us (20%)
  starting transfers between devices  17.5 us (16%)
  waiting for transfers between devices  13.6 us (13%)
  local copies, waits for them, and re-layouts  2.5 us (2%)
    all_to_all x2, blocking collectives, exchange(): return lax.all_to_all(x, AXES, split_axis=0, concat_axis=0, tiled=True)  51.4 us
    pallas_call x1, Pallas kernels, push(): pl.pallas_call(push_kernel, in_specs=[SMEM, SMEM] + [VMEM] * 8, out_shape...  12.9 us
    all_to_all x1, starting transfers between devices, exchange(): return lax.all_to_all(x, AXES, split_axis=0, concat_axis=0, tiled=True)  11.5 us
    all_to_all x1, waiting for transfers between devices, exchange(): return lax.all_to_all(x, AXES, split_axis=0, concat_axis=0, tiled=True)  8.42 us
    ppermute x1, waiting for transfers between devices, local(): lax.ppermute(west, 'face', [((i + 1) % faces, i) for i in range(faces)])  3.99 us
    pallas_call x1, Pallas kernels, regrid(): pl.pallas_call(regrid_kernel, in_specs=[SMEM, VMEM, VMEM, VMEM, VMEM], ou...  3.64 us
    pallas_call x1, Pallas kernels, collect(): pl.pallas_call(collect_kernel, in_specs=[SMEM, VMEM], out_shape=struct((M...  3.31 us
    ppermute x1, starting transfers between devices, local(): lax.ppermute(east, 'face', [(i, (i + 1) % faces) for i in range(faces)])  2.68 us
  transfers between devices with their start and end apart: 5, of which 3 were waited for; matrix products, arithmetic and copies ran while one was open for 1% of the time, Pallas kernels for 0%

profile of v3, /device:TPU:1, one launch (start us, length us, event | category | flops | bytes accessed | tf_op | source)
XLA Modules:
  0.0 106.9 jit_solution(13883736700184186044)
XLA Ops:
  0.0 0.7 copy-done.3
  0.7 0.7 copy-done.4
  1.4 0.8 request.1
  2.1 11.5 %all-to-all-start = ((s32[128,1,128]{2,1,0:T(1,128)}), s32[128,1,128]{2,1,0:T(1,128)S(1)}, u32[]{:S(2)}, u32[]{:S(2)}) async-start(s32[128,1,128]{2,1,0:T(1,128)} %bitcast.3), calls=%async_computation | async-start | bytes 131072 | tf_op jit(solution)/shard_map/all_to_all | solution.py:362
  13.6 1.1 %copy.13 = bf16[16,64,128]{2,0,1:T(8,128)(2,1)S(1)} copy(bf16[16,64,128]{2,1,0:T(8,128)(2,1)} %param.6) | data formatting | bytes 524288 | tf_op args[0]
  14.8 8.4 %all-to-all-done = s32[128,1,128]{2,1,0:T(1,128)S(1)} async-done(((s32[128,1,128]{2,1,0:T(1,128)}), s32[128,1,128]{2,1,0:T(1,128)S(1)}, u32[]{:S(2)}, u32[]{:S(2)}) %all-to-all-start) | async-done | bytes 65568 | tf_op jit(solution)/shard_map/all_to_all | solution.py:362
  23.2 1.2 %pack.1 = (bf16[256,16,128]{2,1,0:T(8,128)(2,1)S(1)}, s32[8,128]{1,0:T(8,128)S(1)}) custom-call(s32[128,128]{1,0:T(8,128)S(1)} %bitcast.22, bf16[64,16,128]{2,1,0:T(8,128)(2,1)S(1)} %bitcast.20), custom_call_target="tpu_custom_call" | custom-call | tf_op jit(solution)/shard_map/pack/pallas_call | solution.py:91
  24.3 0.0 copy-start
  24.4 0.0 copy-start.1
  24.4 0.0 copy-start.2
  24.4 23.7 %all_to_all.21 = bf16[128,2,16,128]{3,2,1,0:T(8,128)(2,1)S(1)} all-to-all(bf16[128,2,16,128]{3,2,1,0:T(8,128)(2,1)S(1)} %bitcast.21), channel_id=1, replica_groups=mesh['face'=4,'tile'=32] {'face','tile'}, dimensions={0} | all-to-all | bytes 2097152 | tf_op jit(solution)/shard_map/all_to_all | solution.py:362
  48.1 0.0 copy-done.1
  48.1 3.6 %regrid.1 = (f32[1088,128]{1,0:T(8,128)S(1)}, f32[1280,128]{1,0:T(8,128)S(1)}, s32[256,128]{1,0:T(8,128)S(1)}, f32[256,128]{1,0:T(8,128)S(1)}, f32[272,128]{1,0:...) custom-call(s32[8,128]{1,0:T(8,128)S(1)} %get-tuple-element.19.place_ref, ...), custom_call_target="tpu_custom_call" | custom-call | tf_op jit(solution)/shard_map/regrid/pallas_call | solution.py:169
  51.8 2.0 %collective-permute-start = (f32[272,128]{1,0:T(8,128)S(1)}, f32[272,128]{1,0:T(8,128)S(1)}, u32[]{:S(2)}, u32[]{:S(2)}) collective-permute-start(f32[272,128]{1,0:T(8,128)S(1)} %get-tuple-element.25), channel_id=1, source_target_pairs={{0,1},{1,2},{2,3},{3,4},{4,5},{5,6},{6,7},{7,8},{8,9},{9,10},{10,1... | collective-permute-start | bytes 417800 | tf_op jit(solution)/shard_map/ppermute | solution.py:382
  53.8 1.3 %collective-permute-start.1 = (f32[272,128]{1,0:T(8,128)S(1)}, f32[272,128]{1,0:T(8,128)S(1)}, u32[]{:S(2)}, u32[]{:S(2)}) collective-permute-start(f32[272,128]{1,0:T(8,128)S(1)} %get-tuple-element.26), channel_id=1, source_target_pairs={{1,0},{2,1},{3,2},{4,3},{5,4},{6,5},{7,6},{8,7},{9,8},{10,9},{11,1... | collective-permute-start | bytes 417800 | tf_op jit(solution)/shard_map/ppermute | solution.py:381
  55.1 2.7 %collective-permute-start.2 = (f32[40,128]{1,0:T(8,128)S(1)}, f32[40,128]{1,0:T(8,128)S(1)}, u32[]{:S(2)}, u32[]{:S(2)}) collective-permute-start(f32[40,128]{1,0:T(8,128)S(1)} %get-tuple-element.27), channel_id=1, source_target_pairs={{0,32},{32,64},{64,96},{96,0},{1,33},{33,65},{65,97},{97,1},{2,34}... | collective-permute-start | bytes 61448 | tf_op jit(solution)/shard_map/ppermute | solution.py:384
  57.8 0.0 collective-permute-start.3
  57.8 1.2 %collective-permute-done.2.left_ref = f32[40,128]{1,0:T(8,128)S(1)} collective-permute-done((f32[40,128]{1,0:T(8,128)S(1)}, f32[40,128]{1,0:T(8,128)S(1)}, u32[]{:S(2)}, u32[]{:S(2)}) %collective-permute-start.2) | collective-permute-done | bytes 20512 | tf_op jit(solution)/shard_map/ppermute | solution.py:384
  58.9 4.0 %collective-permute-done.3.right_ref = f32[40,128]{1,0:T(8,128)S(1)} collective-permute-done((f32[40,128]{1,0:T(8,128)S(1)}, f32[40,128]{1,0:T(8,128)S(1)}, u32[]{:S(2)}, u32[]{:S(2)}) %collective-permute-start.3) | collective-permute-done | bytes 20512 | tf_op jit(solution)/shard_map/ppermute | solution.py:383
  62.9 0.0 collective-permute-done.top_ref
  62.9 0.0 collective-permute-done.1.bottom_ref
  62.9 12.9 %push.1 = s32[2176,128]{1,0:T(8,128)S(1)} custom-call(s32[8,128]{1,0:T(8,128)S(1)} %get-tuple-element.19.place_ref, s32[1]{0:T(128)} %bitcast.6.tile_ref, f32[1088,128]{1,0:T(8,128)S(1)} %get-tuple-element.21.field_ref, f32[1280,128]{1,0:T(8,128)S(1)} %get-tuple-element.22.turned_ref, s32[256,128]{1,0:T(8,128)S(1)} %get-tuple-element.23.posn_ref, ...), custom_call_target="tpu_custom_call" | custom-call | tf_op jit(solution)/shard_map/push/pallas_call | solution.py:312
  75.9 27.7 %all_to_all.22 = s32[128,17,1,128]{3,2,1,0:T(1,128)S(1)} all-to-all(s32[128,17,1,128]{3,2,1,0:T(1,128)S(1)} %bitcast.17), channel_id=1, replica_groups=mesh['face'=4,'tile'=32] {'face','tile'}, dimensions={0} | all-to-all | bytes 2228224 | tf_op jit(solution)/shard_map/all_to_all | solution.py:362
  103.5 3.3 %collect.1 = f32[1024,128]{1,0:T(8,128)} custom-call(s32[8,128]{1,0:T(8,128)S(1)} %get-tuple-element.18.slots_ref, s32[2176,128]{1,0:T(8,128)S(1)} %bitcast.18), custom_call_target="tpu_custom_call" | custom-call | tf_op jit(solution)/shard_map/collect/pallas_call | solution.py:351
  (4 shorter events, 0.0 us)
Async XLA Ops:
  0.0 0.7 copy-start.3
  0.7 0.7 copy-start.4
  2.1 21.0 %all-to-all-start = ((s32[128,1,128]{2,1,0:T(1,128)}), s32[128,1,128]{2,1,0:T(1,128)S(1)}, u32[]{:S(2)}, u32[]{:S(2)}) async-start(s32[128,1,128]{2,1,0:T(1,128)} %bitcast.3), calls=%async_computation | async-start | bytes 131072 | tf_op jit(solution)/shard_map/all_to_all | solution.py:362
  24.3 23.8 %copy-start = (s32[4,64,128]{2,1,0:T(8,128)S(1)}, s32[4,64,128]{2,1,0:T(8,128)}, u32[]{:S(2)}) copy-start(s32[4,64,128]{2,1,0:T(8,128)} %param.9) | copy-start | bytes 393220
  24.4 23.7 %copy-start.1 = (f32[4,64,128]{2,1,0:T(8,128)S(1)}, f32[4,64,128]{2,1,0:T(8,128)}, u32[]{:S(2)}) copy-start(f32[4,64,128]{2,1,0:T(8,128)} %param.10) | copy-start | bytes 393220
  24.4 23.7 %copy-start.2 = (f32[32,256]{1,0:T(8,128)S(1)}, f32[32,256]{1,0:T(8,128)}, u32[]{:S(2)}) copy-start(f32[32,256]{1,0:T(8,128)} %truth_ref.1) | copy-start | bytes 98308
  51.8 11.2 %collective-permute-start = (f32[272,128]{1,0:T(8,128)S(1)}, f32[272,128]{1,0:T(8,128)S(1)}, u32[]{:S(2)}, u32[]{:S(2)}) collective-permute-start(f32[272,128]{1,0:T(8,128)S(1)} %get-tuple-element.25), channel_id=1, source_target_pairs={{0,1},{1,2},{2,3},{3,4},{4,5},{5,6},{6,7},{7,8},{8,9},{9,10},{10,1... | collective-permute-start | bytes 417800 | tf_op jit(solution)/shard_map/ppermute | solution.py:382
  53.8 9.1 %collective-permute-start.1 = (f32[272,128]{1,0:T(8,128)S(1)}, f32[272,128]{1,0:T(8,128)S(1)}, u32[]{:S(2)}, u32[]{:S(2)}) collective-permute-start(f32[272,128]{1,0:T(8,128)S(1)} %get-tuple-element.26), channel_id=1, source_target_pairs={{1,0},{2,1},{3,2},{4,3},{5,4},{6,5},{7,6},{8,7},{9,8},{10,9},{11,1... | collective-permute-start | bytes 417800 | tf_op jit(solution)/shard_map/ppermute | solution.py:381
  55.1 3.8 %collective-permute-start.2 = (f32[40,128]{1,0:T(8,128)S(1)}, f32[40,128]{1,0:T(8,128)S(1)}, u32[]{:S(2)}, u32[]{:S(2)}) collective-permute-start(f32[40,128]{1,0:T(8,128)S(1)} %get-tuple-element.27), channel_id=1, source_target_pairs={{0,32},{32,64},{64,96},{96,0},{1,33},{33,65},{65,97},{97,1},{2,34}... | collective-permute-start | bytes 61448 | tf_op jit(solution)/shard_map/ppermute | solution.py:384
  57.8 5.2 %collective-permute-start.3 = (f32[40,128]{1,0:T(8,128)S(1)}, f32[40,128]{1,0:T(8,128)S(1)}, u32[]{:S(2)}, u32[]{:S(2)}) collective-permute-start(f32[40,128]{1,0:T(8,128)S(1)} %get-tuple-element.28), channel_id=1, source_target_pairs={{32,0},{64,32},{96,64},{0,96},{33,1},{65,33},{97,65},{1,97},{34,2}... | collective-permute-start | bytes 61448 | tf_op jit(solution)/shard_map/ppermute | solution.py:383

commit v4 on v3

--- a/solution.py
+++ b/solution.py
@@ -15,7 +15,6 @@
 DEVICES = 128
 POINTS = 4
 QUADS = M // 4
-TURN = 2 * LANES + 2 * RANGE
 MESSAGE = M + 1
 TOP = 32700.0
 F32 = jnp.float32
@@ -97,9 +96,32 @@
     )(asked, bands)
 
 
+def prepare_kernel(pos_ref, factor_ref, posn_ref, weight_ref):
+    for half in range(2):
+        factors = [factor_ref[pl.ds(j * BANDS + half, ROWS, stride=2), :] for j in range(POINTS)]
+        total = factors[0] + factors[1] + factors[2] + factors[3]
+        for j in range(POINTS):
+            spot = j * BANDS + half * ROWS
+            posn_ref[pl.ds(spot, ROWS), :] = pos_ref[pl.ds(j * BANDS + half, ROWS, stride=2), :]
+            weight_ref[pl.ds(spot, ROWS), :] = factors[j] / total
+
+
+def prepare(pos, factor):
+    return pl.pallas_call(
+        prepare_kernel,
+        out_shape=(
+            struct((POINTS * BANDS, LANES), I32),
+            struct((POINTS * BANDS, LANES)),
+        ),
+        name="prepare",
+        cost_estimate=pl.CostEstimate(flops=1 << 20, bytes_accessed=1 << 20, transcendentals=0),
+        compiler_params=pltpu.CompilerParams(vmem_limit_bytes=2 << 20),
+    )(pos, factor)
+
+
 def regrid_kernel(
-    place_ref, recv_ref, pos_ref, factor_ref, truth_ref,
-    field_ref, turned_ref, posn_ref, weight_ref, north_ref, south_ref, west_ref, east_ref,
+    place_ref, recv_ref, posn_ref, weight_ref, truth_ref,
+    field_ref, turned_ref, north_ref, south_ref, west_ref, east_ref,
     low_ref, high_ref,
 ):
     def spread(row, carry):
@@ -110,14 +132,6 @@
         return carry
 
     lax.fori_loop(0, ROWS, spread, 0, unroll=4)
-
-    for half in range(2):
-        factors = [factor_ref[pl.ds(j * BANDS + half, ROWS, stride=2), :] for j in range(POINTS)]
-        total = factors[0] + factors[1] + factors[2] + factors[3]
-        for j in range(POINTS):
-            spot = j * BANDS + half * ROWS
-            posn_ref[pl.ds(spot, ROWS), :] = pos_ref[pl.ds(j * BANDS + half, ROWS, stride=2), :]
-            weight_ref[pl.ds(spot, ROWS), :] = factors[j] / total
 
     def regrid(block, carry):
         row = pl.multiple_of(block * 8, 8)
@@ -163,7 +177,7 @@
 SMEM = pl.BlockSpec(memory_space=pltpu.SMEM)
 
 
-def regrid(place, recv, pos, factor, truth):
+def regrid(place, recv, posn, weight, truth):
     tall = struct(((M + 1) * 2 * RANGE, LANES))
     wide = struct(((QUADS + 1) * RANGE, LANES))
     return pl.pallas_call(
@@ -172,14 +186,12 @@
         out_shape=(
             struct(((M + 1) * BANDS, LANES)),
             struct(((QUADS + 1) * 2 * LANES, LANES)),
-            struct((POINTS * BANDS, LANES), I32),
-            struct((POINTS * BANDS, LANES)),
             tall, tall, wide, wide,
         ),
         scratch_shapes=[pltpu.VMEM((M * BANDS, LANES), F32)] * 2,
         name="regrid",
         compiler_params=pltpu.CompilerParams(vmem_limit_bytes=8 << 20),
-    )(place, recv, pos, factor, truth)
+    )(place, recv, posn, weight, truth)
 
 
 def steep(diff):
@@ -188,26 +200,80 @@
     return value, (diff * root) * (value * root)
 
 
+def column_pushes(rows):
+    totals, slopes, sights = [], [], []
+    for k in range(1, RANGE + 1):
+        pairs = [steep(rows(q, 0) - rows(q, k)) for q in range(QUADS)]
+        slopes.append([p[1] for p in pairs])
+        totals.append((pairs[0][0] + pairs[1][0]) + (pairs[2][0] + pairs[3][0]))
+        sights.append(steep(rows(QUADS, 0) - rows(QUADS, k))[0])
+    totals = [t + pltpu.roll(t, 2 * ROWS, 1) for t in totals]
+    totals = [t + pltpu.roll(t, ROWS, 1) for t in totals]
+    pushes = []
+    for k in range(1, RANGE + 1):
+        push = (1.0 / (k * M)) * (sights[k - 1] - totals[k - 1] * (1.0 / M))
+        pushes.append([push * slope for slope in slopes[k - 1]])
+    return pushes
+
+
+def ending(kept, spot, pushed, k):
+    moved = pltpu.roll(pushed, k % 8, 0)
+    earlier = kept[spot]
+    kept[spot] = moved
+    return jnp.where(row_ids() >= k, moved, earlier)
+
+
+def column_sums(kept, rows):
+    sums = [jnp.zeros((8, LANES), F32)] * QUADS
+    for k, pushes in enumerate(column_pushes(rows), 1):
+        for q in range(QUADS):
+            sums[q] = sums[q] - pushes[q] + ending(kept, (k - 1) * QUADS + q, pushes[q], k)
+    return sums
+
+
+WIDTH = 2 * LANES
+INNER = WIDTH - 2 * RANGE
+
+
+def inner_kernel(turned_ref, turn_ref, kept_ref):
+    kept_ref[...] = jnp.zeros_like(kept_ref)
+
+    def block(b, carry):
+        base = pl.multiple_of(b * 8, 8)
+        sums = column_sums(kept_ref, lambda q, k: turned_ref[pl.ds(base + (q * WIDTH + k), 8), :])
+        for q in range(QUADS):
+            turn_ref[pl.ds(base + q * WIDTH, 8), :] = sums[q]
+        return carry
+
+    lax.fori_loop(0, INNER // 8, block, 0, unroll=3)
+
+
+def inner(turned):
+    return pl.pallas_call(
+        inner_kernel,
+        out_shape=(struct((QUADS * WIDTH, LANES)), struct((RANGE * QUADS, 8, LANES))),
+        name="inner",
+        cost_estimate=pl.CostEstimate(flops=16 << 20, bytes_accessed=12 << 20, transcendentals=2 << 20),
+        compiler_params=pltpu.CompilerParams(vmem_limit_bytes=2 << 20),
+    )(turned)
+
+
 def push_kernel(
-    place_ref, tile_ref, field_ref, turned_ref, posn_ref, weight_ref, top_ref, bottom_ref, left_ref, right_ref,
-    out_ref, ext, grad, side, turn, kept_rows, kept_columns,
+    place_ref, tile_ref, field_ref, turned_ref, turn_ref, kept_ref, posn_ref, weight_ref,
+    top_ref, bottom_ref, left_ref, right_ref,
+    out_ref, ext, grad, west, east, kept_columns, kept_rows,
 ):
     for mh in range(2 * (M + 1)):
         ext[pl.ds(mh * EXT, 8), :] = top_ref[pl.ds(mh * 8, 8), :]
         ext[pl.ds(mh * EXT + 8, ROWS), :] = field_ref[pl.ds(mh * ROWS, ROWS), :]
         ext[pl.ds(mh * EXT + 8 + ROWS, 8), :] = bottom_ref[pl.ds(mh * 8, 8), :]
     for q in range(QUADS + 1):
-        side[pl.ds(q * TURN, 8), :] = left_ref[pl.ds(q * 8, 8), :]
-        side[pl.ds(q * TURN + 8, 2 * LANES), :] = turned_ref[pl.ds(q * 2 * LANES, 2 * LANES), :]
-        side[pl.ds(q * TURN + 8 + 2 * LANES, 8), :] = right_ref[pl.ds(q * 8, 8), :]
+        west[pl.ds(q * 16, 8), :] = left_ref[pl.ds(q * 8, 8), :]
+        west[pl.ds(q * 16 + 8, 8), :] = turned_ref[pl.ds(q * WIDTH, 8), :]
+        east[pl.ds(q * 24, 16), :] = turned_ref[pl.ds(q * WIDTH + INNER, 16), :]
+        east[pl.ds(q * 24 + 16, 8), :] = right_ref[pl.ds(q * 8, 8), :]
     out_ref[...] = jnp.zeros_like(out_ref)
     first_row = tile_ref[0] * ROWS - RANGE
-
-    def ending(kept, spot, pushed, k):
-        moved = pltpu.roll(pushed, k % 8, 0)
-        earlier = kept[spot]
-        kept[spot] = moved
-        return jnp.where(row_ids() >= k, moved, earlier)
 
     def latitude(step, carry):
         half = step // 5
@@ -238,35 +304,22 @@
 
     lax.fori_loop(0, 10, latitude, 0, unroll=2)
 
-    def longitude(block, carry):
-        base = pl.multiple_of(block * 8, 8)
-        totals, slopes, sights = [], [], []
-        for k in range(1, RANGE + 1):
-            def diff(q):
-                here = base + q * TURN
-                return side[pl.ds(here, 8), :] - side[pl.ds(here + k, 8), :]
-
-            pairs = [steep(diff(q)) for q in range(QUADS)]
-            slopes.append([p[1] for p in pairs])
-            totals.append((pairs[0][0] + pairs[1][0]) + (pairs[2][0] + pairs[3][0]))
-            sights.append(steep(diff(QUADS))[0])
-        totals = [t + pltpu.roll(t, 2 * ROWS, 1) for t in totals]
-        totals = [t + pltpu.roll(t, ROWS, 1) for t in totals]
-        sums = [jnp.zeros((8, LANES), F32)] * QUADS
-        for k in range(1, RANGE + 1):
-            push = (1.0 / (k * M)) * (sights[k - 1] - totals[k - 1] * (1.0 / M))
-            for q in range(QUADS):
-                pushed = push * slopes[k - 1][q]
-                sums[q] = sums[q] - pushed + ending(kept_columns, (k - 1) * QUADS + q, pushed, k)
+    added = [jnp.zeros((8, LANES), F32)] * QUADS
+    for k, pushes in enumerate(column_pushes(lambda q, k: west[pl.ds(q * 16 + k, 8), :]), 1):
         for q in range(QUADS):
-            turn[pl.ds(base + q * TURN, 8), :] = sums[q]
-        return carry
-
-    lax.fori_loop(0, TURN // 8 - 1, longitude, 0, unroll=3)
+            added[q] = added[q] + jnp.where(row_ids() < k, pltpu.roll(pushes[q], k % 8, 0), 0.0)
+    kept_columns[...] = kept_ref[...]
+    near = column_sums(kept_columns, lambda q, k: east[pl.ds(q * 24 + k, 8), :])
+    last = column_sums(kept_columns, lambda q, k: east[pl.ds(q * 24 + 8 + k, 8), :])
 
     for q in range(QUADS):
+        first = turn_ref[pl.ds(q * WIDTH, 8), :] + added[q]
+        halves = [
+            jnp.concatenate([first, turn_ref[pl.ds(q * WIDTH + 8, LANES - 8), :]], axis=0),
+            jnp.concatenate([turn_ref[pl.ds(q * WIDTH + LANES, INNER - LANES), :], near[q], last[q]], axis=0),
+        ]
         for half in range(2):
-            back = jnp.transpose(turn[pl.ds(q * TURN + 8 + half * LANES, LANES), :])
+            back = jnp.transpose(halves[half])
             for i in range(4):
                 spot = ((4 * q + i) * 2 + half) * EXT + 8
                 grad[pl.ds(spot, ROWS), :] += back[i * ROWS : (i + 1) * ROWS]
@@ -308,22 +361,22 @@
     lax.fori_loop(0, ROWS, adjoint, 0, unroll=4)
 
 
-def push(place, tile, field, turned, posn, weight, top, bottom, left, right):
+def push(place, tile, *arrays):
     return pl.pallas_call(
         push_kernel,
-        in_specs=[SMEM, SMEM] + [VMEM] * 8,
+        in_specs=[SMEM, SMEM] + [VMEM] * len(arrays),
         out_shape=struct((DEVICES * MESSAGE, LANES), I32),
         scratch_shapes=[
             pltpu.VMEM((2 * (M + 1) * EXT, LANES), F32),
             pltpu.VMEM((2 * M * EXT, LANES), F32),
-            pltpu.VMEM(((QUADS + 1) * TURN, LANES), F32),
-            pltpu.VMEM((QUADS * TURN, LANES), F32),
+            pltpu.VMEM(((QUADS + 1) * 16, LANES), F32),
+            pltpu.VMEM(((QUADS + 1) * 24, LANES), F32),
+            pltpu.VMEM((RANGE * QUADS, 8, LANES), F32),
             pltpu.VMEM((RANGE * M, 8, LANES), F32),
-            pltpu.VMEM((RANGE * QUADS, 8, LANES), F32),
         ],
         name="push",
-        compiler_params=pltpu.CompilerParams(vmem_limit_bytes=12 << 20),
-    )(place, tile, field, turned, posn, weight, top, bottom, left, right)
+        compiler_params=pltpu.CompilerParams(vmem_limit_bytes=6 << 20),
+    )(place, tile, *arrays)
 
 
 def collect_kernel(slots_ref, back_ref, out_ref, sums):
@@ -365,17 +418,15 @@
 def local(predicted_field, parent_band_holder, parent_band_slot, neighbour_positions, unscaled_neighbour_factor, truth_field):
     tiles, faces = lax.axis_size("tile"), lax.axis_size("face")
     bands = jnp.transpose(predicted_field, (1, 0, 2))
+    posn, weight = prepare(
+        neighbour_positions.reshape(POINTS * BANDS, LANES),
+        unscaled_neighbour_factor.reshape(POINTS * BANDS, LANES),
+    )
     wanted, place = request(parent_band_holder.T, parent_band_slot.T)
     asked = exchange(wanted)
     outgoing, slots = pack(asked, bands)
     recv = exchange(outgoing.reshape(DEVICES, 2, M, LANES)).reshape(2 * DEVICES, M, LANES)
-    field, turned, posn, weight, north, south, west, east = regrid(
-        place,
-        recv,
-        neighbour_positions.reshape(POINTS * BANDS, LANES),
-        unscaled_neighbour_factor.reshape(POINTS * BANDS, LANES),
-        truth_field,
-    )
+    field, turned, north, south, west, east = regrid(place, recv, posn, weight, truth_field)
     up = [(i + 1, i) for i in range(tiles - 1)]
     down = [(i, i + 1) for i in range(tiles - 1)]
     bottom = lax.ppermute(north, "tile", up)
@@ -383,7 +434,8 @@
     right = lax.ppermute(west, "face", [((i + 1) % faces, i) for i in range(faces)])
     left = lax.ppermute(east, "face", [(i, (i + 1) % faces) for i in range(faces)])
     tile = lax.axis_index("tile").astype(I32).reshape(1)
-    back = push(place, tile, field, turned, posn, weight, top, bottom, left, right)
+    turn, kept = inner(turned)
+    back = push(place, tile, field, turned, turn, kept, posn, weight, top, bottom, left, right)
     back = exchange(back.reshape(DEVICES, MESSAGE, 1, LANES)).reshape(DEVICES * MESSAGE, LANES)
     return collect(slots, back).reshape(M, BANDS, LANES)
 

time: 107 us -> 105 us (0.981)
  blocking collectives: 51.4 us -> 27.7 us
  waiting for transfers between devices: 13.6 us -> 30 us
  starting transfers between devices: 17.5 us -> 22 us
  Pallas kernels: 21.8 us -> 22.9 us
    all_to_all x2 -> x1, blocking collectives: 51.4 us -> 27.7 us  [exchange(): return lax.all_to_all(x, AXES, split_axis=0, concat_axis=0, tiled=True)]
    all_to_all x1 -> x2, waiting for transfers between devices: 8.42 us -> 27.8 us  [exchange(): return lax.all_to_all(x, AXES, split_axis=0, concat_axis=0, tiled=True)]
    all_to_all x1 -> x2, starting transfers between devices: 11.5 us -> 16 us  [exchange(): return lax.all_to_all(x, AXES, split_axis=0, concat_axis=0, tiled=True)]
    ppermute x1, waiting for transfers between devices: 3.99 us -> 2.2 us  [local(): lax.ppermute(west, 'face', [((i + 1) % faces, i) for i in range(faces)])]
    ppermute x1, waiting for transfers between devices: 1.16 us -> 0.01 us  [local(): lax.ppermute(east, 'face', [(i, (i + 1) % faces) for i in range(faces)])]
    pallas_call x1 -> x3, Pallas kernels: 12.9 us -> 13 us  [the longest x1 10.1 us: push(): pl.pallas_call(push_kernel, in_specs=[SMEM, SMEM] + [VMEM] * len(arrays),...]
  transfers between devices with their start and end apart: 5 -> 6, of which waited for: 3 -> 3; matrix products, arithmetic and copies ran while one was open for 1% -> 1% of each run, Pallas kernels for 0% -> 3%
where the time goes in v4:
time: 105 us
  waiting for transfers between devices  30 us (29%)
  blocking collectives  27.7 us (26%)
  Pallas kernels  22.9 us (22%)
  starting transfers between devices  22 us (21%)
  local copies, waits for them, and re-layouts  2.5 us (2%)
    all_to_all x2, waiting for transfers between devices, exchange(): return lax.all_to_all(x, AXES, split_axis=0, concat_axis=0, tiled=True)  27.8 us
    all_to_all x1, blocking collectives, exchange(): return lax.all_to_all(x, AXES, split_axis=0, concat_axis=0, tiled=True)  27.7 us
    all_to_all x2, starting transfers between devices, exchange(): return lax.all_to_all(x, AXES, split_axis=0, concat_axis=0, tiled=True)  16 us
    pallas_call x1, Pallas kernels, push(): pl.pallas_call(push_kernel, in_specs=[SMEM, SMEM] + [VMEM] * len(arrays),...  10.1 us
    pallas_call x1, Pallas kernels, regrid(): pl.pallas_call(regrid_kernel, in_specs=[SMEM, VMEM, VMEM, VMEM, VMEM], ou...  3.61 us
    pallas_call x1, Pallas kernels, collect(): pl.pallas_call(collect_kernel, in_specs=[SMEM, VMEM], out_shape=struct((M...  3.3 us
    pallas_call x1, Pallas kernels, inner(): pl.pallas_call(inner_kernel, out_shape=(struct((QUADS * WIDTH, LANES)), s...  2.93 us
    ppermute x1, starting transfers between devices, local(): lax.ppermute(east, 'face', [(i, (i + 1) % faces) for i in range(faces)])  2.68 us
  transfers between devices with their start and end apart: 6, of which 3 were waited for; matrix products, arithmetic and copies ran while one was open for 1% of the time, Pallas kernels for 3%

profile of v4, /device:TPU:1, one launch (start us, length us, event | category | flops | bytes accessed | tf_op | source)
XLA Modules:
  0.0 105.1 jit_solution(14242870964865639846)
XLA Ops:
  0.0 0.7 copy-done.3
  0.7 0.7 copy-done.4
  1.4 0.8 request.1
  2.1 11.5 %all-to-all-start = ((s32[128,1,128]{2,1,0:T(1,128)}), s32[128,1,128]{2,1,0:T(1,128)S(1)}, u32[]{:S(2)}, u32[]{:S(2)}) async-start(s32[128,1,128]{2,1,0:T(1,128)} %bitcast.3), calls=%async_computation | async-start | bytes 131072 | tf_op jit(solution)/shard_map/all_to_all | solution.py:415
  13.6 1.1 %copy.13 = bf16[16,64,128]{2,0,1:T(8,128)(2,1)S(1)} copy(bf16[16,64,128]{2,1,0:T(8,128)(2,1)} %param.6) | data formatting | bytes 524288 | tf_op args[0]
  14.8 8.4 %all-to-all-done = s32[128,1,128]{2,1,0:T(1,128)S(1)} async-done(((s32[128,1,128]{2,1,0:T(1,128)}), s32[128,1,128]{2,1,0:T(1,128)S(1)}, u32[]{:S(2)}, u32[]{:S(2)}) %all-to-all-start) | async-done | bytes 65568 | tf_op jit(solution)/shard_map/all_to_all | solution.py:415
  23.2 2.1 %pack.1 = (bf16[256,16,128]{2,1,0:T(8,128)(2,1)}, s32[8,128]{1,0:T(8,128)S(1)}) custom-call(s32[128,128]{1,0:T(8,128)S(1)} %bitcast.21, bf16[64,16,128]{2,1,0:T(8,128)(2,1)S(1)} %bitcast.20), custom_call_target="tpu_custom_call" | custom-call | tf_op jit(solution)/shard_map/pack/pallas_call | solution.py:90
  25.3 0.0 copy-start
  25.4 0.0 copy-start.1
  25.4 0.0 copy-start.2
  25.4 4.5 %all-to-all-start.1 = ((bf16[128,2,16,128]{3,2,1,0:T(8,128)(2,1)}), bf16[128,2,16,128]{3,2,1,0:T(8,128)(2,1)S(1)}, u32[]{:S(2)}, u32[]{:S(2)}) async-start(bf16[128,2,16,128]{3,2,1,0:T(8,128)(2,1)} %bitcast.7), calls=%async_computation.1 | async-start | bytes 2097152 | tf_op jit(solution)/shard_map/all_to_all | solution.py:415
  30.0 19.3 %all-to-all-done.1 = bf16[128,2,16,128]{3,2,1,0:T(8,128)(2,1)S(1)} async-done(((bf16[128,2,16,128]{3,2,1,0:T(8,128)(2,1)}), bf16[128,2,16,128]{3,2,1,0:T(8,128)(2,1)S(1)}, u32[]{:S(2)}, u32[]{:S(2)}) %all-to-all-start.1) | async-done | bytes 1048608 | tf_op jit(solution)/shard_map/all_to_all | solution.py:415
  49.3 3.6 %regrid.1 = (f32[1088,128]{1,0:T(8,128)S(1)}, f32[1280,128]{1,0:T(8,128)S(1)}, f32[272,128]{1,0:T(8,128)S(1)}, f32[272,128]{1,0:T(8,128)S(1)}, f32[40,128]{1,0:T(8,128)S(1)}, /*index=5*/f32[40,128]{1,0:T(8,128)S(1)}) custom-call(s32[8,128]{1,0:T(8,128)S(1)} %get-tuple-element.21.place_ref, bf16[256,16,128]{2,1,0:T(8,128)(2,1)S(1)} %bitcast.19, ...), custom_call_target="tpu_custom_call" | custom-call | tf_op jit(solution)/shard_map/regrid/pallas_call | solution.py:183
  52.9 2.0 %collective-permute-start = (f32[272,128]{1,0:T(8,128)S(1)}, f32[272,128]{1,0:T(8,128)S(1)}, u32[]{:S(2)}, u32[]{:S(2)}) collective-permute-start(f32[272,128]{1,0:T(8,128)S(1)} %get-tuple-element.29), channel_id=1, source_target_pairs={{0,1},{1,2},{2,3},{3,4},{4,5},{5,6},{6,7},{7,8},{8,9},{9,10},{10,1... | collective-permute-start | bytes 417800 | tf_op jit(solution)/shard_map/ppermute | solution.py:433
  55.0 1.3 %collective-permute-start.1 = (f32[272,128]{1,0:T(8,128)S(1)}, f32[272,128]{1,0:T(8,128)S(1)}, u32[]{:S(2)}, u32[]{:S(2)}) collective-permute-start(f32[272,128]{1,0:T(8,128)S(1)} %get-tuple-element.30), channel_id=1, source_target_pairs={{1,0},{2,1},{3,2},{4,3},{5,4},{6,5},{7,6},{8,7},{9,8},{10,9},{11,1... | collective-permute-start | bytes 417800 | tf_op jit(solution)/shard_map/ppermute | solution.py:432
  56.3 2.7 %collective-permute-start.2 = (f32[40,128]{1,0:T(8,128)S(1)}, f32[40,128]{1,0:T(8,128)S(1)}, u32[]{:S(2)}, u32[]{:S(2)}) collective-permute-start(f32[40,128]{1,0:T(8,128)S(1)} %get-tuple-element.31), channel_id=1, source_target_pairs={{0,32},{32,64},{64,96},{96,0},{1,33},{33,65},{65,97},{97,1},{2,34}... | collective-permute-start | bytes 61448 | tf_op jit(solution)/shard_map/ppermute | solution.py:435
  58.9 0.0 collective-permute-start.3
  58.9 2.9 %inner.1 = (f32[1024,128]{1,0:T(8,128)S(1)}, f32[32,8,128]{2,1,0:T(8,128)S(1)}) custom-call(f32[1280,128]{1,0:T(8,128)S(1)} %get-tuple-element.26.turned_ref), custom_call_target="tpu_custom_call" | custom-call | flops 16777216 | bytes 12582912 | tf_op jit(solution)/shard_map/inner/pallas_call | solution.py:252
  61.9 0.0 collective-permute-done.2.left_ref
  61.9 2.2 %collective-permute-done.3.right_ref = f32[40,128]{1,0:T(8,128)S(1)} collective-permute-done((f32[40,128]{1,0:T(8,128)S(1)}, f32[40,128]{1,0:T(8,128)S(1)}, u32[]{:S(2)}, u32[]{:S(2)}) %collective-permute-start.3) | collective-permute-done | bytes 20512 | tf_op jit(solution)/shard_map/ppermute | solution.py:434
  64.1 0.0 collective-permute-done.1.bottom_ref
  64.1 10.1 %push.1 = s32[2176,128]{1,0:T(8,128)S(1)} custom-call(s32[8,128]{1,0:T(8,128)S(1)} %get-tuple-element.21.place_ref, s32[1]{0:T(128)} %bitcast.6.tile_ref, f32[1088,128]{1,0:T(8,128)S(1)} %get-tuple-element.25.field_ref, f32[1280,128]{1,0:T(8,128)S(1)} %get-tuple-element.26.turned_ref, f32[1024,128]{1,0:T(8,128)S(1)} %get-tuple-element.27.turn_ref, ...), custom_call_target="tpu_custom_call" | custom-call | tf_op jit(solution)/shard_map/push/pallas_call | solution.py:365
  74.2 27.7 %all_to_all.21 = s32[128,17,1,128]{3,2,1,0:T(1,128)S(1)} all-to-all(s32[128,17,1,128]{3,2,1,0:T(1,128)S(1)} %bitcast.17), channel_id=1, replica_groups=mesh['face'=4,'tile'=32] {'face','tile'}, dimensions={0} | all-to-all | bytes 2228224 | tf_op jit(solution)/shard_map/all_to_all | solution.py:415
  101.8 3.3 %collect.1 = f32[1024,128]{1,0:T(8,128)} custom-call(s32[8,128]{1,0:T(8,128)S(1)} %get-tuple-element.20.slots_ref, s32[2176,128]{1,0:T(8,128)S(1)} %bitcast.18), custom_call_target="tpu_custom_call" | custom-call | tf_op jit(solution)/shard_map/collect/pallas_call | solution.py:404
  (7 shorter events, 0.0 us)
Async XLA Ops:
  0.0 0.7 copy-start.3
  0.7 0.7 copy-start.4
  2.1 21.0 %all-to-all-start = ((s32[128,1,128]{2,1,0:T(1,128)}), s32[128,1,128]{2,1,0:T(1,128)S(1)}, u32[]{:S(2)}, u32[]{:S(2)}) async-start(s32[128,1,128]{2,1,0:T(1,128)} %bitcast.3), calls=%async_computation | async-start | bytes 131072 | tf_op jit(solution)/shard_map/all_to_all | solution.py:415
  25.3 4.6 %copy-start = (s32[4,64,128]{2,1,0:T(8,128)S(1)}, s32[4,64,128]{2,1,0:T(8,128)}, u32[]{:S(2)}) copy-start(s32[4,64,128]{2,1,0:T(8,128)} %param.9) | copy-start | bytes 393220
  25.4 4.6 %copy-start.1 = (f32[4,64,128]{2,1,0:T(8,128)S(1)}, f32[4,64,128]{2,1,0:T(8,128)}, u32[]{:S(2)}) copy-start(f32[4,64,128]{2,1,0:T(8,128)} %param.10) | copy-start | bytes 393220
  25.4 23.9 %copy-start.2 = (f32[32,256]{1,0:T(8,128)S(1)}, f32[32,256]{1,0:T(8,128)}, u32[]{:S(2)}) copy-start(f32[32,256]{1,0:T(8,128)} %truth_ref.1) | copy-start | bytes 98308
  25.4 23.9 %all-to-all-start.1 = ((bf16[128,2,16,128]{3,2,1,0:T(8,128)(2,1)}), bf16[128,2,16,128]{3,2,1,0:T(8,128)(2,1)S(1)}, u32[]{:S(2)}, u32[]{:S(2)}) async-start(bf16[128,2,16,128]{3,2,1,0:T(8,128)(2,1)} %bitcast.7), calls=%async_computation.1 | async-start | bytes 2097152 | tf_op jit(solution)/shard_map/all_to_all | solution.py:415
  52.9 11.2 %collective-permute-start = (f32[272,128]{1,0:T(8,128)S(1)}, f32[272,128]{1,0:T(8,128)S(1)}, u32[]{:S(2)}, u32[]{:S(2)}) collective-permute-start(f32[272,128]{1,0:T(8,128)S(1)} %get-tuple-element.29), channel_id=1, source_target_pairs={{0,1},{1,2},{2,3},{3,4},{4,5},{5,6},{6,7},{7,8},{8,9},{9,10},{10,1... | collective-permute-start | bytes 417800 | tf_op jit(solution)/shard_map/ppermute | solution.py:433
  55.0 9.1 %collective-permute-start.1 = (f32[272,128]{1,0:T(8,128)S(1)}, f32[272,128]{1,0:T(8,128)S(1)}, u32[]{:S(2)}, u32[]{:S(2)}) collective-permute-start(f32[272,128]{1,0:T(8,128)S(1)} %get-tuple-element.30), channel_id=1, source_target_pairs={{1,0},{2,1},{3,2},{4,3},{5,4},{6,5},{7,6},{8,7},{9,8},{10,9},{11,1... | collective-permute-start | bytes 417800 | tf_op jit(solution)/shard_map/ppermute | solution.py:432
  56.3 5.6 %collective-permute-start.2 = (f32[40,128]{1,0:T(8,128)S(1)}, f32[40,128]{1,0:T(8,128)S(1)}, u32[]{:S(2)}, u32[]{:S(2)}) collective-permute-start(f32[40,128]{1,0:T(8,128)S(1)} %get-tuple-element.31), channel_id=1, source_target_pairs={{0,32},{32,64},{64,96},{96,0},{1,33},{33,65},{65,97},{97,1},{2,34}... | collective-permute-start | bytes 61448 | tf_op jit(solution)/shard_map/ppermute | solution.py:435
  58.9 5.1 %collective-permute-start.3 = (f32[40,128]{1,0:T(8,128)S(1)}, f32[40,128]{1,0:T(8,128)S(1)}, u32[]{:S(2)}, u32[]{:S(2)}) collective-permute-start(f32[40,128]{1,0:T(8,128)S(1)} %get-tuple-element.32), channel_id=1, source_target_pairs={{32,0},{64,32},{96,64},{0,96},{33,1},{65,33},{97,65},{1,97},{34,2}... | collective-permute-start | bytes 61448 | tf_op jit(solution)/shard_map/ppermute | solution.py:434

commit v5 on v4

--- a/solution.py
+++ b/solution.py
@@ -35,7 +35,15 @@
     return lax.broadcasted_iota(I32, (rows, LANES), 0)
 
 
-def request_kernel(holder_ref, slot_ref, wanted_ref, place_ref):
+def request_kernel(holder_hbm, slot_hbm, wanted_ref, place_ref, holder_ref, slot_ref, sems):
+    copies = [
+        pltpu.make_async_copy(holder_hbm, holder_ref, sems.at[0]),
+        pltpu.make_async_copy(slot_hbm, slot_ref, sems.at[1]),
+    ]
+    for copy in copies:
+        copy.start()
+    for copy in copies:
+        copy.wait()
     owner = lax.broadcasted_iota(I32, (DEVICES, BANDS), 0).astype(F32)
     band = lax.broadcasted_iota(I32, (1, BANDS), 1)
     big = float(1 << 20)
@@ -65,9 +73,10 @@
 def request(holder, slot):
     return pl.pallas_call(
         request_kernel,
+        in_specs=[pl.BlockSpec(memory_space=pl.ANY)] * 2,
         out_shape=(struct((DEVICES, LANES), I32), struct((8, LANES), I32)),
+        scratch_shapes=[pltpu.VMEM((2, BANDS), I32)] * 2 + [pltpu.SemaphoreType.DMA((2,))],
         name="request",
-        compiler_params=pltpu.CompilerParams(vmem_limit_bytes=1 << 20),
     )(holder, slot)
 
 
@@ -131,7 +140,7 @@
                 tab[pl.ds(half * ROWS + row, M, stride=BANDS), :] = strip
         return carry
 
-    lax.fori_loop(0, ROWS, spread, 0, unroll=4)
+    lax.fori_loop(0, ROWS, spread, 0, unroll=8)
 
     def regrid(block, carry):
         row = pl.multiple_of(block * 8, 8)
@@ -379,8 +388,9 @@
     )(place, tile, *arrays)
 
 
-def collect_kernel(slots_ref, back_ref, out_ref, sums):
-    sums[...] = jnp.zeros_like(sums)
+def collect_kernel(slots_ref, back_ref, out_ref, *sums):
+    for part in sums:
+        part[...] = jnp.zeros_like(part)
 
     def step(i, carry):
         codes = back_ref[pl.ds(i * MESSAGE, M), :]
@@ -388,13 +398,13 @@
         for r in range(2):
             code, scale = [((x << 16) if r == 0 else x) >> 16 for x in (codes, scales)]
             scale = jnp.exp2(scale.astype(F32) * (1.0 / 256.0)) * (1.0 / TOP)
-            sums[slots_ref[r, i]] += code.astype(F32) * scale
-        return carry
-
-    lax.fori_loop(0, DEVICES, step, 0, unroll=4)
+            sums[r][slots_ref[r, i]] += code.astype(F32) * scale
+        return carry
+
+    lax.fori_loop(0, DEVICES, step, 0, unroll=8)
 
     def turn(s, carry):
-        out_ref[pl.ds(s, M, stride=BANDS), :] = sums[s]
+        out_ref[pl.ds(s, M, stride=BANDS), :] = sums[0][s] + sums[1][s]
         return carry
 
     lax.fori_loop(0, BANDS, turn, 0, unroll=8)
@@ -405,7 +415,7 @@
         collect_kernel,
         in_specs=[SMEM, VMEM],
         out_shape=struct((M * BANDS, LANES)),
-        scratch_shapes=[pltpu.VMEM((BANDS, M, LANES), F32)],
+        scratch_shapes=[pltpu.VMEM((BANDS, M, LANES), F32)] * 2,
         name="collect",
         compiler_params=pltpu.CompilerParams(vmem_limit_bytes=5 << 20),
     )(slots, back)
@@ -423,7 +433,7 @@
         unscaled_neighbour_factor.reshape(POINTS * BANDS, LANES),
     )
     wanted, place = request(parent_band_holder.T, parent_band_slot.T)
-    asked = exchange(wanted)
+    asked, posn, weight = lax.optimization_barrier((exchange(wanted), posn, weight))
     outgoing, slots = pack(asked, bands)
     recv = exchange(outgoing.reshape(DEVICES, 2, M, LANES)).reshape(2 * DEVICES, M, LANES)
     field, turned, north, south, west, east = regrid(place, recv, posn, weight, truth_field)

time: 105 us -> 103 us (0.981)
  blocking collectives: 27.7 us -> 51.4 us
  waiting for transfers between devices: 30 us -> 8.81 us
  starting transfers between devices: 22 us -> 17.5 us
    all_to_all x1 -> x2, blocking collectives: 27.7 us -> 51.4 us  [exchange(): return lax.all_to_all(x, AXES, split_axis=0, concat_axis=0, tiled=True)]
    all_to_all x2 -> x1, waiting for transfers between devices: 27.8 us -> 6.58 us  [exchange(): return lax.all_to_all(x, AXES, split_axis=0, concat_axis=0, tiled=True)]
    all_to_all x2 -> x1, starting transfers between devices: 16 us -> 11.5 us  [exchange(): return lax.all_to_all(x, AXES, split_axis=0, concat_axis=0, tiled=True)]
    unnamed x11 -> x9, local copies, waits for them, and re-layouts: 2.5 us -> 2.94 us
  transfers between devices with their start and end apart: 6 -> 5, of which waited for: 3 -> 2; matrix products, arithmetic and copies ran while one was open for 1% -> 1% of each run, Pallas kernels for 3% -> 3%
where the time goes in v5:
time: 103 us
  blocking collectives  51.4 us (50%)
  Pallas kernels  21.9 us (21%)
  starting transfers between devices  17.5 us (17%)
  waiting for transfers between devices  8.81 us (9%)
  local copies, waits for them, and re-layouts  2.94 us (3%)
    all_to_all x2, blocking collectives, exchange(): return lax.all_to_all(x, AXES, split_axis=0, concat_axis=0, tiled=True)  51.4 us
    all_to_all x1, starting transfers between devices, exchange(): return lax.all_to_all(x, AXES, split_axis=0, concat_axis=0, tiled=True)  11.5 us
    pallas_call x1, Pallas kernels, push(): pl.pallas_call(push_kernel, in_specs=[SMEM, SMEM] + [VMEM] * len(arrays),...  10.1 us
    all_to_all x1, waiting for transfers between devices, exchange(): return lax.all_to_all(x, AXES, split_axis=0, concat_axis=0, tiled=True)  6.58 us
    pallas_call x1, Pallas kernels, regrid(): pl.pallas_call(regrid_kernel, in_specs=[SMEM, VMEM, VMEM, VMEM, VMEM], ou...  3.59 us
    unnamed x9, local copies, waits for them, and re-layouts  2.94 us
    pallas_call x1, Pallas kernels, inner(): pl.pallas_call(inner_kernel, out_shape=(struct((QUADS * WIDTH, LANES)), s...  2.9 us
    pallas_call x1, Pallas kernels, collect(): pl.pallas_call(collect_kernel, in_specs=[SMEM, VMEM], out_shape=struct((M...  2.68 us
  transfers between devices with their start and end apart: 5, of which 2 were waited for; matrix products, arithmetic and copies ran while one was open for 1% of the time, Pallas kernels for 3%

profile of v5, /device:TPU:1, one launch (start us, length us, event | category | flops | bytes accessed | tf_op | source)
XLA Modules:
  0.0 102.7 jit_solution(14837499131353759001)
XLA Ops:
  0.0 1.5 %request.1 = (s32[128,128]{1,0:T(8,128)}, s32[8,128]{1,0:T(8,128)}) custom-call(s32[2,64]{1,0:T(2,128)} %bitcast.26, s32[2,64]{1,0:T(2,128)} %bitcast.27), custom_call_target="tpu_custom_call" | custom-call | tf_op jit(solution)/shard_map/request/pallas_call | solution.py:74
  1.5 11.5 %all-to-all-start = ((s32[128,1,128]{2,1,0:T(1,128)}), s32[128,1,128]{2,1,0:T(1,128)S(1)}, u32[]{:S(2)}, u32[]{:S(2)}) async-start(s32[128,1,128]{2,1,0:T(1,128)} %bitcast.25), calls=%async_computation | async-start | bytes 131072 | tf_op jit(solution)/shard_map/all_to_all | solution.py:425
  13.0 1.1 %copy.13 = bf16[16,64,128]{2,0,1:T(8,128)(2,1)S(1)} copy(bf16[16,64,128]{2,1,0:T(8,128)(2,1)} %param.6) | data formatting | bytes 524288 | tf_op args[0]
  14.1 0.0 copy-start
  14.1 0.9 copy-done
  15.0 0.9 copy-done.1
  16.0 6.6 %all-to-all-done = s32[128,1,128]{2,1,0:T(1,128)S(1)} async-done(((s32[128,1,128]{2,1,0:T(1,128)}), s32[128,1,128]{2,1,0:T(1,128)S(1)}, u32[]{:S(2)}, u32[]{:S(2)}) %all-to-all-start) | async-done | bytes 65568 | tf_op jit(solution)/shard_map/all_to_all | solution.py:425
  22.6 1.2 %pack.1 = (bf16[256,16,128]{2,1,0:T(8,128)(2,1)S(1)}, s32[8,128]{1,0:T(8,128)S(1)}) custom-call(s32[128,128]{1,0:T(8,128)S(1)} %bitcast.22, bf16[64,16,128]{2,1,0:T(8,128)(2,1)S(1)} %bitcast.20), custom_call_target="tpu_custom_call" | custom-call | tf_op jit(solution)/shard_map/pack/pallas_call | solution.py:99
  23.7 0.0 copy-start.2
  23.7 0.0 copy-start.3
  23.7 23.7 %all_to_all.22 = bf16[128,2,16,128]{3,2,1,0:T(8,128)(2,1)S(1)} all-to-all(bf16[128,2,16,128]{3,2,1,0:T(8,128)(2,1)S(1)} %bitcast.21), channel_id=1, replica_groups=mesh['face'=4,'tile'=32] {'face','tile'}, dimensions={0} | all-to-all | bytes 2097152 | tf_op jit(solution)/shard_map/all_to_all | solution.py:425
  47.5 3.6 %regrid.1 = (f32[1088,128]{1,0:T(8,128)S(1)}, f32[1280,128]{1,0:T(8,128)S(1)}, f32[272,128]{1,0:T(8,128)S(1)}, f32[272,128]{1,0:T(8,128)S(1)}, f32[40,128]{1,0:T(8,128)S(1)}, /*index=5*/f32[40,128]{1,0:T(8,128)S(1)}) custom-call(s32[8,128]{1,0:T(8,128)S(1)} %copy-done.3, bf16[256,16,128]{2,1,0:T(8,128)(2,1)S(1)} %bitcast.19, ...), custom_call_target="tpu_custom_call" | custom-call | tf_op jit(solution)/shard_map/regrid/pallas_call | solution.py:192
  51.1 2.0 %collective-permute-start = (f32[272,128]{1,0:T(8,128)S(1)}, f32[272,128]{1,0:T(8,128)S(1)}, u32[]{:S(2)}, u32[]{:S(2)}) collective-permute-start(f32[272,128]{1,0:T(8,128)S(1)} %get-tuple-element.35), channel_id=1, source_target_pairs={{0,1},{1,2},{2,3},{3,4},{4,5},{5,6},{6,7},{7,8},{8,9},{9,10},{10,1... | collective-permute-start | bytes 417800 | tf_op jit(solution)/shard_map/ppermute | solution.py:443
  53.1 1.3 %collective-permute-start.1 = (f32[272,128]{1,0:T(8,128)S(1)}, f32[272,128]{1,0:T(8,128)S(1)}, u32[]{:S(2)}, u32[]{:S(2)}) collective-permute-start(f32[272,128]{1,0:T(8,128)S(1)} %get-tuple-element.36), channel_id=1, source_target_pairs={{1,0},{2,1},{3,2},{4,3},{5,4},{6,5},{7,6},{8,7},{9,8},{10,9},{11,1... | collective-permute-start | bytes 417800 | tf_op jit(solution)/shard_map/ppermute | solution.py:442
  54.4 2.7 %collective-permute-start.2 = (f32[40,128]{1,0:T(8,128)S(1)}, f32[40,128]{1,0:T(8,128)S(1)}, u32[]{:S(2)}, u32[]{:S(2)}) collective-permute-start(f32[40,128]{1,0:T(8,128)S(1)} %get-tuple-element.37), channel_id=1, source_target_pairs={{0,32},{32,64},{64,96},{96,0},{1,33},{33,65},{65,97},{97,1},{2,34}... | collective-permute-start | bytes 61448 | tf_op jit(solution)/shard_map/ppermute | solution.py:445
  57.1 0.0 collective-permute-start.3
  57.1 2.9 %inner.1 = (f32[1024,128]{1,0:T(8,128)S(1)}, f32[32,8,128]{2,1,0:T(8,128)S(1)}) custom-call(f32[1280,128]{1,0:T(8,128)S(1)} %get-tuple-element.32.turned_ref), custom_call_target="tpu_custom_call" | custom-call | flops 16777216 | bytes 12582912 | tf_op jit(solution)/shard_map/inner/pallas_call | solution.py:261
  60.0 0.0 collective-permute-done.2.left_ref
  60.0 2.2 %collective-permute-done.3.right_ref = f32[40,128]{1,0:T(8,128)S(1)} collective-permute-done((f32[40,128]{1,0:T(8,128)S(1)}, f32[40,128]{1,0:T(8,128)S(1)}, u32[]{:S(2)}, u32[]{:S(2)}) %collective-permute-start.3) | collective-permute-done | bytes 20512 | tf_op jit(solution)/shard_map/ppermute | solution.py:444
  62.2 0.0 collective-permute-done.top_ref
  62.2 0.0 collective-permute-done.1.bottom_ref
  62.2 10.1 %push.1 = s32[2176,128]{1,0:T(8,128)S(1)} custom-call(s32[8,128]{1,0:T(8,128)S(1)} %copy-done.3, s32[1]{0:T(128)} %bitcast.8.tile_ref, f32[1088,128]{1,0:T(8,128)S(1)} %get-tuple-element.31.field_ref, f32[1280,128]{1,0:T(8,128)S(1)} %get-tuple-element.32.turned_ref, f32[1024,128]{1,0:T(8,128)S(1)} %get-tuple-element.33.turn_ref, ...), custom_call_target="tpu_custom_call" | custom-call | tf_op jit(solution)/shard_map/push/pallas_call | solution.py:374
  72.3 27.7 %all_to_all.23 = s32[128,17,1,128]{3,2,1,0:T(1,128)S(1)} all-to-all(s32[128,17,1,128]{3,2,1,0:T(1,128)S(1)} %bitcast.17), channel_id=1, replica_groups=mesh['face'=4,'tile'=32] {'face','tile'}, dimensions={0} | all-to-all | bytes 2228224 | tf_op jit(solution)/shard_map/all_to_all | solution.py:425
  100.0 2.7 %collect.1 = f32[1024,128]{1,0:T(8,128)} custom-call(s32[8,128]{1,0:T(8,128)S(1)} %get-tuple-element.26.slots_ref, s32[2176,128]{1,0:T(8,128)S(1)} %bitcast.18), custom_call_target="tpu_custom_call" | custom-call | tf_op jit(solution)/shard_map/collect/pallas_call | solution.py:414
  (4 shorter events, 0.0 us)
Async XLA Ops:
  1.5 21.0 %all-to-all-start = ((s32[128,1,128]{2,1,0:T(1,128)}), s32[128,1,128]{2,1,0:T(1,128)S(1)}, u32[]{:S(2)}, u32[]{:S(2)}) async-start(s32[128,1,128]{2,1,0:T(1,128)} %bitcast.25), calls=%async_computation | async-start | bytes 131072 | tf_op jit(solution)/shard_map/all_to_all | solution.py:425
  14.1 0.9 copy-start
  15.0 0.9 copy-start.1
  23.7 23.7 %copy-start.2 = (f32[32,256]{1,0:T(8,128)S(1)}, f32[32,256]{1,0:T(8,128)}, u32[]{:S(2)}) copy-start(f32[32,256]{1,0:T(8,128)} %truth_ref.1) | copy-start | bytes 98308
  23.7 23.7 %copy-start.3 = (s32[8,128]{1,0:T(8,128)S(1)}, s32[8,128]{1,0:T(8,128)}, u32[]{:S(2)}) copy-start(s32[8,128]{1,0:T(8,128)} %get-tuple-element.27.place_ref) | copy-start | bytes 12292
  51.1 11.2 %collective-permute-start = (f32[272,128]{1,0:T(8,128)S(1)}, f32[272,128]{1,0:T(8,128)S(1)}, u32[]{:S(2)}, u32[]{:S(2)}) collective-permute-start(f32[272,128]{1,0:T(8,128)S(1)} %get-tuple-element.35), channel_id=1, source_target_pairs={{0,1},{1,2},{2,3},{3,4},{4,5},{5,6},{6,7},{7,8},{8,9},{9,10},{10,1... | collective-permute-start | bytes 417800 | tf_op jit(solution)/shard_map/ppermute | solution.py:443
  53.1 9.1 %collective-permute-start.1 = (f32[272,128]{1,0:T(8,128)S(1)}, f32[272,128]{1,0:T(8,128)S(1)}, u32[]{:S(2)}, u32[]{:S(2)}) collective-permute-start(f32[272,128]{1,0:T(8,128)S(1)} %get-tuple-element.36), channel_id=1, source_target_pairs={{1,0},{2,1},{3,2},{4,3},{5,4},{6,5},{7,6},{8,7},{9,8},{10,9},{11,1... | collective-permute-start | bytes 417800 | tf_op jit(solution)/shard_map/ppermute | solution.py:442
  54.4 5.6 %collective-permute-start.2 = (f32[40,128]{1,0:T(8,128)S(1)}, f32[40,128]{1,0:T(8,128)S(1)}, u32[]{:S(2)}, u32[]{:S(2)}) collective-permute-start(f32[40,128]{1,0:T(8,128)S(1)} %get-tuple-element.37), channel_id=1, source_target_pairs={{0,32},{32,64},{64,96},{96,0},{1,33},{33,65},{65,97},{97,1},{2,34}... | collective-permute-start | bytes 61448 | tf_op jit(solution)/shard_map/ppermute | solution.py:445
  57.1 5.1 %collective-permute-start.3 = (f32[40,128]{1,0:T(8,128)S(1)}, f32[40,128]{1,0:T(8,128)S(1)}, u32[]{:S(2)}, u32[]{:S(2)}) collective-permute-start(f32[40,128]{1,0:T(8,128)S(1)} %get-tuple-element.38), channel_id=1, source_target_pairs={{32,0},{64,32},{96,64},{0,96},{33,1},{65,33},{97,65},{1,97},{34,2}... | collective-permute-start | bytes 61448 | tf_op jit(solution)/shard_map/ppermute | solution.py:444

commit v6 on v5

--- a/solution.py
+++ b/solution.py
@@ -129,8 +129,8 @@
 
 
 def regrid_kernel(
-    place_ref, recv_ref, posn_ref, weight_ref, truth_ref,
-    field_ref, turned_ref, north_ref, south_ref, west_ref, east_ref,
+    place_ref, tile_ref, face_ref, recv_ref, posn_ref, weight_ref, truth_ref,
+    field_ref, turned_ref, tall0_ref, tall1_ref, wide0_ref, wide1_ref,
     low_ref, high_ref,
 ):
     def spread(row, carry):
@@ -163,11 +163,13 @@
 
     for half in range(2):
         field_ref[pl.ds(M * BANDS + half * ROWS, ROWS), :] = truth_ref[:, half * LANES : (half + 1) * LANES]
+    odd = tile_ref[0] & 1
     for m in range(M + 1):
         for half in range(2):
             spot = m * BANDS + half * ROWS
-            north_ref[pl.ds((2 * m + half) * 8, 8), :] = field_ref[pl.ds(spot, 8), :]
-            south_ref[pl.ds((2 * m + half) * 8, 8), :] = field_ref[pl.ds(spot + ROWS - 8, 8), :]
+            for message, edge in ((tall0_ref, 1 - odd), (tall1_ref, odd)):
+                rows = pl.ds(pl.multiple_of(spot + edge * (ROWS - 8), 8), 8)
+                message[pl.ds((2 * m + half) * 8, 8), :] = field_ref[rows, :]
     for q in range(QUADS + 1):
         for half in range(2):
             if q < QUADS:
@@ -176,22 +178,23 @@
                 parts = [truth_ref[:, half * LANES : (half + 1) * LANES]] * 4
             turned = jnp.transpose(jnp.concatenate(parts, axis=0))
             turned_ref[pl.ds(q * 2 * LANES + half * LANES, LANES), :] = turned
-            if half == 0:
-                west_ref[pl.ds(q * 8, 8), :] = turned[:8]
-            else:
-                east_ref[pl.ds(q * 8, 8), :] = turned[LANES - 8 :]
+    odd = face_ref[0] & 1
+    for q in range(QUADS + 1):
+        for message, edge in ((wide0_ref, 1 - odd), (wide1_ref, odd)):
+            columns = pl.ds(pl.multiple_of(q * 2 * LANES + edge * (2 * LANES - 8), 8), 8)
+            message[pl.ds(q * 8, 8), :] = turned_ref[columns, :]
 
 
 VMEM = pl.BlockSpec(memory_space=pltpu.VMEM)
 SMEM = pl.BlockSpec(memory_space=pltpu.SMEM)
 
 
-def regrid(place, recv, posn, weight, truth):
+def regrid(place, tile, face, recv, posn, weight, truth):
     tall = struct(((M + 1) * 2 * RANGE, LANES))
     wide = struct(((QUADS + 1) * RANGE, LANES))
     return pl.pallas_call(
         regrid_kernel,
-        in_specs=[SMEM, VMEM, VMEM, VMEM, VMEM],
+        in_specs=[SMEM] * 3 + [VMEM] * 4,
         out_shape=(
             struct(((M + 1) * BANDS, LANES)),
             struct(((QUADS + 1) * 2 * LANES, LANES)),
@@ -200,7 +203,7 @@
         scratch_shapes=[pltpu.VMEM((M * BANDS, LANES), F32)] * 2,
         name="regrid",
         compiler_params=pltpu.CompilerParams(vmem_limit_bytes=8 << 20),
-    )(place, recv, posn, weight, truth)
+    )(place, tile, face, recv, posn, weight, truth)
 
 
 def steep(diff):
@@ -268,19 +271,23 @@
 
 
 def push_kernel(
-    place_ref, tile_ref, field_ref, turned_ref, turn_ref, kept_ref, posn_ref, weight_ref,
-    top_ref, bottom_ref, left_ref, right_ref,
+    place_ref, tile_ref, face_ref, field_ref, turned_ref, turn_ref, kept_ref, posn_ref, weight_ref,
+    tall0_ref, tall1_ref, wide0_ref, wide1_ref,
     out_ref, ext, grad, west, east, kept_columns, kept_rows,
 ):
+    odd = tile_ref[0] & 1
     for mh in range(2 * (M + 1)):
-        ext[pl.ds(mh * EXT, 8), :] = top_ref[pl.ds(mh * 8, 8), :]
+        for message, below in ((tall0_ref, 1 - odd), (tall1_ref, odd)):
+            rows = pl.ds(pl.multiple_of(mh * EXT + below * (ROWS + 8), 8), 8)
+            ext[rows, :] = message[pl.ds(mh * 8, 8), :]
         ext[pl.ds(mh * EXT + 8, ROWS), :] = field_ref[pl.ds(mh * ROWS, ROWS), :]
-        ext[pl.ds(mh * EXT + 8 + ROWS, 8), :] = bottom_ref[pl.ds(mh * 8, 8), :]
+    even = jnp.full((8, LANES), face_ref[0] & 1, I32) == 0
     for q in range(QUADS + 1):
-        west[pl.ds(q * 16, 8), :] = left_ref[pl.ds(q * 8, 8), :]
+        ones, twos = wide0_ref[pl.ds(q * 8, 8), :], wide1_ref[pl.ds(q * 8, 8), :]
+        west[pl.ds(q * 16, 8), :] = jnp.where(even, twos, ones)
         west[pl.ds(q * 16 + 8, 8), :] = turned_ref[pl.ds(q * WIDTH, 8), :]
         east[pl.ds(q * 24, 16), :] = turned_ref[pl.ds(q * WIDTH + INNER, 16), :]
-        east[pl.ds(q * 24 + 16, 8), :] = right_ref[pl.ds(q * 8, 8), :]
+        east[pl.ds(q * 24 + 16, 8), :] = jnp.where(even, ones, twos)
     out_ref[...] = jnp.zeros_like(out_ref)
     first_row = tile_ref[0] * ROWS - RANGE
 
@@ -370,10 +377,10 @@
     lax.fori_loop(0, ROWS, adjoint, 0, unroll=4)
 
 
-def push(place, tile, *arrays):
+def push(place, tile, face, *arrays):
     return pl.pallas_call(
         push_kernel,
-        in_specs=[SMEM, SMEM] + [VMEM] * len(arrays),
+        in_specs=[SMEM] * 3 + [VMEM] * len(arrays),
         out_shape=struct((DEVICES * MESSAGE, LANES), I32),
         scratch_shapes=[
             pltpu.VMEM((2 * (M + 1) * EXT, LANES), F32),
@@ -385,7 +392,7 @@
         ],
         name="push",
         compiler_params=pltpu.CompilerParams(vmem_limit_bytes=6 << 20),
-    )(place, tile, *arrays)
+    )(place, tile, face, *arrays)
 
 
 def collect_kernel(slots_ref, back_ref, out_ref, *sums):
@@ -433,19 +440,21 @@
         unscaled_neighbour_factor.reshape(POINTS * BANDS, LANES),
     )
     wanted, place = request(parent_band_holder.T, parent_band_slot.T)
-    asked, posn, weight = lax.optimization_barrier((exchange(wanted), posn, weight))
+    tile = lax.axis_index("tile").astype(I32).reshape(1)
+    face = lax.axis_index("face").astype(I32).reshape(1)
+    asked, posn, weight, tile, face = lax.optimization_barrier((exchange(wanted), posn, weight, tile, face))
     outgoing, slots = pack(asked, bands)
     recv = exchange(outgoing.reshape(DEVICES, 2, M, LANES)).reshape(2 * DEVICES, M, LANES)
-    field, turned, north, south, west, east = regrid(place, recv, posn, weight, truth_field)
-    up = [(i + 1, i) for i in range(tiles - 1)]
-    down = [(i, i + 1) for i in range(tiles - 1)]
-    bottom = lax.ppermute(north, "tile", up)
-    top = lax.ppermute(south, "tile", down)
-    right = lax.ppermute(west, "face", [((i + 1) % faces, i) for i in range(faces)])
-    left = lax.ppermute(east, "face", [(i, (i + 1) % faces) for i in range(faces)])
-    tile = lax.axis_index("tile").astype(I32).reshape(1)
+    field, turned, *messages = regrid(place, tile, face, recv, posn, weight, truth_field)
+    rounds = [
+        ("tile", [(i, i + 1) for i in range(0, tiles - 1, 2)]),
+        ("tile", [(i, i + 1) for i in range(1, tiles - 1, 2)]),
+        ("face", [(i, i + 1) for i in range(0, faces, 2)]),
+        ("face", [(i, (i + 1) % faces) for i in range(1, faces, 2)]),
+    ]
+    messages = [lax.ppermute(m, axis, pairs + [(j, i) for i, j in pairs]) for m, (axis, pairs) in zip(messages, rounds)]
     turn, kept = inner(turned)
-    back = push(place, tile, field, turned, turn, kept, posn, weight, top, bottom, left, right)
+    back = push(place, tile, face, field, turned, turn, kept, posn, weight, *messages)
     back = exchange(back.reshape(DEVICES, MESSAGE, 1, LANES)).reshape(DEVICES * MESSAGE, LANES)
     return collect(slots, back).reshape(M, BANDS, LANES)
 

time: 103 us -> 99.8 us (0.969)
  starting transfers between devices: 17.5 us -> 15.1 us
  blocking collectives: 51.4 us -> 49.4 us
    ppermute x4, starting transfers between devices: 6.01 us -> 3.65 us  [local(): lax.ppermute(m, axis, pairs + [(j, i) for i, j in pairs])]
    all_to_all x2, blocking collectives: 51.4 us -> 49.4 us  [exchange(): return lax.all_to_all(x, AXES, split_axis=0, concat_axis=0, tiled=True)]
where the time goes in v6:
time: 99.8 us; the launch traced here: 99.4 us
  blocking collectives  49.4 us (49%)
  Pallas kernels  22.2 us (22%)
  starting transfers between devices  15.1 us (15%)
  waiting for transfers between devices  9.62 us (10%)
  local copies, waits for them, and re-layouts  2.94 us (3%)
    all_to_all x2, blocking collectives, exchange(): return lax.all_to_all(x, AXES, split_axis=0, concat_axis=0, tiled=True)  49.4 us
    all_to_all x1, starting transfers between devices, exchange(): return lax.all_to_all(x, AXES, split_axis=0, concat_axis=0, tiled=True)  11.5 us
    pallas_call x1, Pallas kernels, push(): pl.pallas_call(push_kernel, in_specs=[SMEM] * 3 + [VMEM] * len(arrays), o...  10.1 us
    all_to_all x1, waiting for transfers between devices, exchange(): return lax.all_to_all(x, AXES, split_axis=0, concat_axis=0, tiled=True)  6.57 us
    ppermute x4, starting transfers between devices, local(): lax.ppermute(m, axis, pairs + [(j, i) for i, j in pairs])  3.65 us
    pallas_call x1, Pallas kernels, regrid(): pl.pallas_call(regrid_kernel, in_specs=[SMEM] * 3 + [VMEM] * 4, out_shape...  3.6 us
    ppermute x4, waiting for transfers between devices, local(): lax.ppermute(m, axis, pairs + [(j, i) for i, j in pairs])  3.05 us
    unnamed x9, local copies, waits for them, and re-layouts  2.94 us
  transfers between devices with their start and end apart: 5, of which 2 were waited for; matrix products, arithmetic and copies ran while one was open for 1% of the time, Pallas kernels for 3%

profile of v6, /device:TPU:1, one launch (start us, length us, event | category | flops | bytes accessed | tf_op | source)
XLA Modules:
  0.0 99.4 jit_solution(15710675737079668953)
XLA Ops:
  0.0 1.5 %request.1 = (s32[128,128]{1,0:T(8,128)}, s32[8,128]{1,0:T(8,128)}) custom-call(s32[2,64]{1,0:T(2,128)} %bitcast.27, s32[2,64]{1,0:T(2,128)} %bitcast.28), custom_call_target="tpu_custom_call" | custom-call | tf_op jit(solution)/shard_map/request/pallas_call | solution.py:74
  1.5 11.5 %all-to-all-start = ((s32[128,1,128]{2,1,0:T(1,128)}), s32[128,1,128]{2,1,0:T(1,128)S(1)}, u32[]{:S(2)}, u32[]{:S(2)}) async-start(s32[128,1,128]{2,1,0:T(1,128)} %bitcast.26), calls=%async_computation | async-start | bytes 131072 | tf_op jit(solution)/shard_map/all_to_all | solution.py:432
  13.0 1.1 %copy.13 = bf16[16,64,128]{2,0,1:T(8,128)(2,1)S(1)} copy(bf16[16,64,128]{2,1,0:T(8,128)(2,1)} %param.6) | data formatting | bytes 524288 | tf_op args[0]
  14.1 0.0 copy-start
  14.2 0.9 copy-done
  15.1 0.9 copy-done.1
  16.0 6.6 %all-to-all-done = s32[128,1,128]{2,1,0:T(1,128)S(1)} async-done(((s32[128,1,128]{2,1,0:T(1,128)}), s32[128,1,128]{2,1,0:T(1,128)S(1)}, u32[]{:S(2)}, u32[]{:S(2)}) %all-to-all-start) | async-done | bytes 65568 | tf_op jit(solution)/shard_map/all_to_all | solution.py:432
  22.6 1.2 %pack.1 = (bf16[256,16,128]{2,1,0:T(8,128)(2,1)S(1)}, s32[8,128]{1,0:T(8,128)S(1)}) custom-call(s32[128,128]{1,0:T(8,128)S(1)} %bitcast.23, bf16[64,16,128]{2,1,0:T(8,128)(2,1)S(1)} %bitcast.21), custom_call_target="tpu_custom_call" | custom-call | tf_op jit(solution)/shard_map/pack/pallas_call | solution.py:99
  23.7 0.0 copy-start.2
  23.7 0.0 copy-start.3
  23.7 23.7 %all_to_all.22 = bf16[128,2,16,128]{3,2,1,0:T(8,128)(2,1)S(1)} all-to-all(bf16[128,2,16,128]{3,2,1,0:T(8,128)(2,1)S(1)} %bitcast.22), channel_id=1, replica_groups=mesh['face'=4,'tile'=32] {'face','tile'}, dimensions={0} | all-to-all | bytes 2097152 | tf_op jit(solution)/shard_map/all_to_all | solution.py:432
  47.5 3.6 %regrid.1 = (f32[1088,128]{1,0:T(8,128)S(1)}, f32[1280,128]{1,0:T(8,128)S(1)}, f32[272,128]{1,0:T(8,128)S(1)}, f32[272,128]{1,0:T(8,128)S(1)}, f32[40,128]{1,0:T(8,128)S(1)}, /*index=5*/f32[40,128]{1,0:T(8,128)S(1)}) custom-call(s32[8,128]{1,0:T(8,128)S(1)} %copy-done.3, s32[1]{0:T(128)} %bitcast.7.tile_ref, s32[1]{0:T(128)} %bitcast.8.face_ref, ...), custom_call_target="tpu_custom_call" | custom-call | tf_op jit(solution)/shard_map/regrid/pallas_call | solution.py:195
  51.1 0.2 collective-permute-start
  51.3 0.7 collective-permute-start.1
  51.9 1.6 %collective-permute-start.2 = (f32[40,128]{1,0:T(8,128)S(1)}, f32[40,128]{1,0:T(8,128)S(1)}, u32[]{:S(2)}, u32[]{:S(2)}) collective-permute-start(f32[40,128]{1,0:T(8,128)S(1)} %get-tuple-element.41), channel_id=1, source_target_pairs={{0,32},{64,96},{32,0},{96,64},{1,33},{65,97},{33,1},{97,65},{2,34}... | collective-permute-start | bytes 61448 | tf_op jit(solution)/shard_map/ppermute | solution.py:455
  53.5 1.2 %collective-permute-start.3 = (f32[40,128]{1,0:T(8,128)S(1)}, f32[40,128]{1,0:T(8,128)S(1)}, u32[]{:S(2)}, u32[]{:S(2)}) collective-permute-start(f32[40,128]{1,0:T(8,128)S(1)} %get-tuple-element.42), channel_id=1, source_target_pairs={{32,64},{96,0},{64,32},{0,96},{33,65},{97,1},{65,33},{1,97},{34,66... | collective-permute-start | bytes 61448 | tf_op jit(solution)/shard_map/ppermute | solution.py:455
  54.7 2.9 %inner.1 = (f32[1024,128]{1,0:T(8,128)S(1)}, f32[32,8,128]{2,1,0:T(8,128)S(1)}) custom-call(f32[1280,128]{1,0:T(8,128)S(1)} %get-tuple-element.36.turned_ref), custom_call_target="tpu_custom_call" | custom-call | flops 16777216 | bytes 12582912 | tf_op jit(solution)/shard_map/inner/pallas_call | solution.py:264
  57.7 0.0 collective-permute-done.2.wide0_ref
  57.7 3.0 %collective-permute-done.3.wide1_ref = f32[40,128]{1,0:T(8,128)S(1)} collective-permute-done((f32[40,128]{1,0:T(8,128)S(1)}, f32[40,128]{1,0:T(8,128)S(1)}, u32[]{:S(2)}, u32[]{:S(2)}) %collective-permute-start.3) | collective-permute-done | bytes 20512 | tf_op jit(solution)/shard_map/ppermute | solution.py:455
  60.7 0.0 collective-permute-done.tall0_ref
  60.7 0.0 collective-permute-done.1.tall1_ref
  60.7 10.1 %push.1 = s32[2176,128]{1,0:T(8,128)S(1)} custom-call(s32[8,128]{1,0:T(8,128)S(1)} %copy-done.3, s32[1]{0:T(128)} %bitcast.7.tile_ref, s32[1]{0:T(128)} %bitcast.8.face_ref, f32[1088,128]{1,0:T(8,128)S(1)} %get-tuple-element.35.field_ref, f32[1280,128]{1,0:T(8,128)S(1)} %get-tuple-element.36.turned_ref, f32[1024,128]{1,0:T(8,128)S(1)} %get-tuple-element.37.turn_ref, ...), custom_call_target="tpu_custom_call" | custom-call | tf_op jit(solution)/shard_map/push/pallas_call | solution.py:381
  70.8 25.7 %all_to_all.23 = s32[128,17,1,128]{3,2,1,0:T(1,128)S(1)} all-to-all(s32[128,17,1,128]{3,2,1,0:T(1,128)S(1)} %bitcast.18), channel_id=1, replica_groups=mesh['face'=4,'tile'=32] {'face','tile'}, dimensions={0} | all-to-all | bytes 2228224 | tf_op jit(solution)/shard_map/all_to_all | solution.py:432
  96.5 2.9 %collect.1 = f32[1024,128]{1,0:T(8,128)} custom-call(s32[8,128]{1,0:T(8,128)S(1)} %get-tuple-element.28.slots_ref, s32[2176,128]{1,0:T(8,128)S(1)} %bitcast.19), custom_call_target="tpu_custom_call" | custom-call | tf_op jit(solution)/shard_map/collect/pallas_call | solution.py:421
  (4 shorter events, 0.0 us)
Async XLA Ops:
  1.5 21.0 %all-to-all-start = ((s32[128,1,128]{2,1,0:T(1,128)}), s32[128,1,128]{2,1,0:T(1,128)S(1)}, u32[]{:S(2)}, u32[]{:S(2)}) async-start(s32[128,1,128]{2,1,0:T(1,128)} %bitcast.26), calls=%async_computation | async-start | bytes 131072 | tf_op jit(solution)/shard_map/all_to_all | solution.py:432
  14.1 0.9 copy-start
  15.1 0.9 copy-start.1
  23.7 23.7 %copy-start.2 = (f32[32,256]{1,0:T(8,128)S(1)}, f32[32,256]{1,0:T(8,128)}, u32[]{:S(2)}) copy-start(f32[32,256]{1,0:T(8,128)} %truth_ref.1) | copy-start | bytes 98308
  23.7 23.7 %copy-start.3 = (s32[8,128]{1,0:T(8,128)S(1)}, s32[8,128]{1,0:T(8,128)}, u32[]{:S(2)}) copy-start(s32[8,128]{1,0:T(8,128)} %get-tuple-element.29.place_ref) | copy-start | bytes 12292
  51.1 9.7 %collective-permute-start = (f32[272,128]{1,0:T(8,128)S(1)}, f32[272,128]{1,0:T(8,128)S(1)}, u32[]{:S(2)}, u32[]{:S(2)}) collective-permute-start(f32[272,128]{1,0:T(8,128)S(1)} %get-tuple-element.39), channel_id=1, source_target_pairs={{0,1},{2,3},{4,5},{6,7},{8,9},{10,11},{12,13},{14,15},{16,17},{18,... | collective-permute-start | bytes 417800 | tf_op jit(solution)/shard_map/ppermute | solution.py:455
  51.3 9.4 %collective-permute-start.1 = (f32[272,128]{1,0:T(8,128)S(1)}, f32[272,128]{1,0:T(8,128)S(1)}, u32[]{:S(2)}, u32[]{:S(2)}) collective-permute-start(f32[272,128]{1,0:T(8,128)S(1)} %get-tuple-element.40), channel_id=1, source_target_pairs={{1,2},{3,4},{5,6},{7,8},{9,10},{11,12},{13,14},{15,16},{17,18},{19... | collective-permute-start | bytes 417800 | tf_op jit(solution)/shard_map/ppermute | solution.py:455
  51.9 5.7 %collective-permute-start.2 = (f32[40,128]{1,0:T(8,128)S(1)}, f32[40,128]{1,0:T(8,128)S(1)}, u32[]{:S(2)}, u32[]{:S(2)}) collective-permute-start(f32[40,128]{1,0:T(8,128)S(1)} %get-tuple-element.41), channel_id=1, source_target_pairs={{0,32},{64,96},{32,0},{96,64},{1,33},{65,97},{33,1},{97,65},{2,34}... | collective-permute-start | bytes 61448 | tf_op jit(solution)/shard_map/ppermute | solution.py:455
  53.5 7.2 %collective-permute-start.3 = (f32[40,128]{1,0:T(8,128)S(1)}, f32[40,128]{1,0:T(8,128)S(1)}, u32[]{:S(2)}, u32[]{:S(2)}) collective-permute-start(f32[40,128]{1,0:T(8,128)S(1)} %get-tuple-element.42), channel_id=1, source_target_pairs={{32,64},{96,0},{64,32},{0,96},{33,65},{97,1},{65,33},{1,97},{34,66... | collective-permute-start | bytes 61448 | tf_op jit(solution)/shard_map/ppermute | solution.py:455

commit v7 on v6

--- a/solution.py
+++ b/solution.py
@@ -14,6 +14,8 @@
 EXT = ROWS + 2 * RANGE
 DEVICES = 128
 POINTS = 4
+TABLE = BANDS + 1
+GRAD = 2 * EXT + 1
 QUADS = M // 4
 MESSAGE = M + 1
 TOP = 32700.0
@@ -137,7 +139,7 @@
         for half in range(2):
             for k, tab in enumerate((low_ref, high_ref)):
                 strip = recv_ref[place_ref[k, 2 * row + half]].astype(F32)
-                tab[pl.ds(half * ROWS + row, M, stride=BANDS), :] = strip
+                tab[pl.ds(half * ROWS + row, M, stride=TABLE), :] = strip
         return carry
 
     lax.fori_loop(0, ROWS, spread, 0, unroll=8)
@@ -151,7 +153,7 @@
             lane, upper = posn[j] & (LANES - 1), posn[j] >= LANES
             for m in range(M):
                 a, b = [
-                    jnp.take_along_axis(tab[pl.ds(m * BANDS + row, 8), :], lane, axis=1, mode="promise_in_bounds")
+                    jnp.take_along_axis(tab[pl.ds(m * TABLE + row, 8), :], lane, axis=1, mode="promise_in_bounds")
                     for tab in (low_ref, high_ref)
                 ]
                 sums[m] = sums[m] + weight[j] * jnp.where(upper, b, a)
@@ -200,7 +202,7 @@
             struct(((QUADS + 1) * 2 * LANES, LANES)),
             tall, tall, wide, wide,
         ),
-        scratch_shapes=[pltpu.VMEM((M * BANDS, LANES), F32)] * 2,
+        scratch_shapes=[pltpu.VMEM((M * TABLE, LANES), F32)] * 2,
         name="regrid",
         compiler_params=pltpu.CompilerParams(vmem_limit_bytes=8 << 20),
     )(place, tile, face, recv, posn, weight, truth)
@@ -315,7 +317,7 @@
                 pushed = push * slopes[m]
                 sums[m] = sums[m] - pushed + ending(kept_rows, (k - 1) * M + m, pushed, k)
         for m in range(M):
-            grad[pl.ds(base + m * 2 * EXT, 8), :] = sums[m]
+            grad[pl.ds(base + m * GRAD, 8), :] = sums[m]
         return carry
 
     lax.fori_loop(0, 10, latitude, 0, unroll=2)
@@ -337,7 +339,7 @@
         for half in range(2):
             back = jnp.transpose(halves[half])
             for i in range(4):
-                spot = ((4 * q + i) * 2 + half) * EXT + 8
+                spot = (4 * q + i) * GRAD + half * EXT + 8
                 grad[pl.ds(spot, ROWS), :] += back[i * ROWS : (i + 1) * ROWS]
 
     cells = [(lax.broadcasted_iota(I32, (16, LANES), 0) + 16 * i).astype(F32).astype(BF16) for i in range(16)]
@@ -345,7 +347,7 @@
 
     def adjoint(row, carry):
         for half in range(2):
-            tile = grad[pl.ds(half * EXT + 8 + row, M, stride=2 * EXT), :]
+            tile = grad[pl.ds(half * EXT + 8 + row, M, stride=GRAD), :]
             parts, hots = [], []
             for j in range(POINTS):
                 spot = j * BANDS + half * ROWS + row
@@ -384,7 +386,7 @@
         out_shape=struct((DEVICES * MESSAGE, LANES), I32),
         scratch_shapes=[
             pltpu.VMEM((2 * (M + 1) * EXT, LANES), F32),
-            pltpu.VMEM((2 * M * EXT, LANES), F32),
+            pltpu.VMEM((M * GRAD, LANES), F32),
             pltpu.VMEM(((QUADS + 1) * 16, LANES), F32),
             pltpu.VMEM(((QUADS + 1) * 24, LANES), F32),
             pltpu.VMEM((RANGE * QUADS, 8, LANES), F32),
@@ -405,16 +407,18 @@
         for r in range(2):
             code, scale = [((x << 16) if r == 0 else x) >> 16 for x in (codes, scales)]
             scale = jnp.exp2(scale.astype(F32) * (1.0 / 256.0)) * (1.0 / TOP)
-            sums[r][slots_ref[r, i]] += code.astype(F32) * scale
+            sums[r][pl.ds(slots_ref[r, i] * MESSAGE, M), :] += code.astype(F32) * scale
         return carry
 
     lax.fori_loop(0, DEVICES, step, 0, unroll=8)
 
-    def turn(s, carry):
-        out_ref[pl.ds(s, M, stride=BANDS), :] = sums[0][s] + sums[1][s]
-        return carry
-
-    lax.fori_loop(0, BANDS, turn, 0, unroll=8)
+    def turn(block, carry):
+        for m in range(M):
+            where = pl.ds(block * 8 * MESSAGE + m, 8, stride=MESSAGE)
+            out_ref[pl.ds(pl.multiple_of(m * BANDS + block * 8, 8), 8), :] = sums[0][where, :] + sums[1][where, :]
+        return carry
+
+    lax.fori_loop(0, BANDS // 8, turn, 0)
 
 
 def collect(slots, back):
@@ -422,7 +426,7 @@
         collect_kernel,
         in_specs=[SMEM, VMEM],
         out_shape=struct((M * BANDS, LANES)),
-        scratch_shapes=[pltpu.VMEM((BANDS, M, LANES), F32)] * 2,
+        scratch_shapes=[pltpu.VMEM((BANDS * MESSAGE, LANES), F32)] * 2,
         name="collect",
         compiler_params=pltpu.CompilerParams(vmem_limit_bytes=5 << 20),
     )(slots, back)

time: 99.8 us -> 98.6 us (0.988)
  Pallas kernels: 22.2 us -> 21.1 us
where the time goes in v7:
time: 98.6 us; the launch traced here: 98.3 us
  blocking collectives  49.4 us (50%)
  Pallas kernels  21.1 us (21%)
  starting transfers between devices  15.1 us (15%)
  waiting for transfers between devices  9.62 us (10%)
  local copies, waits for them, and re-layouts  2.94 us (3%)
    all_to_all x2, blocking collectives, exchange(): return lax.all_to_all(x, AXES, split_axis=0, concat_axis=0, tiled=True)  49.4 us
    all_to_all x1, starting transfers between devices, exchange(): return lax.all_to_all(x, AXES, split_axis=0, concat_axis=0, tiled=True)  11.5 us
    pallas_call x1, Pallas kernels, push(): pl.pallas_call(push_kernel, in_specs=[SMEM] * 3 + [VMEM] * len(arrays), o...  10.1 us
    all_to_all x1, waiting for transfers between devices, exchange(): return lax.all_to_all(x, AXES, split_axis=0, concat_axis=0, tiled=True)  6.57 us
    ppermute x4, starting transfers between devices, local(): lax.ppermute(m, axis, pairs + [(j, i) for i, j in pairs])  3.65 us
    ppermute x4, waiting for transfers between devices, local(): lax.ppermute(m, axis, pairs + [(j, i) for i, j in pairs])  3.05 us
    unnamed x9, local copies, waits for them, and re-layouts  2.94 us
    pallas_call x1, Pallas kernels, inner(): pl.pallas_call(inner_kernel, out_shape=(struct((QUADS * WIDTH, LANES)), s...  2.94 us
  transfers between devices with their start and end apart: 5, of which 2 were waited for; matrix products, arithmetic and copies ran while one was open for 1% of the time, Pallas kernels for 3%

profile of v7, /device:TPU:1, one launch (start us, length us, event | category | flops | bytes accessed | tf_op | source)
XLA Modules:
  0.0 98.3 jit_solution(6828311688142952153)
XLA Ops:
  0.0 1.5 %request.1 = (s32[128,128]{1,0:T(8,128)}, s32[8,128]{1,0:T(8,128)}) custom-call(s32[2,64]{1,0:T(2,128)} %bitcast.27, s32[2,64]{1,0:T(2,128)} %bitcast.28), custom_call_target="tpu_custom_call" | custom-call | tf_op jit(solution)/shard_map/request/pallas_call | solution.py:76
  1.5 11.5 %all-to-all-start = ((s32[128,1,128]{2,1,0:T(1,128)}), s32[128,1,128]{2,1,0:T(1,128)S(1)}, u32[]{:S(2)}, u32[]{:S(2)}) async-start(s32[128,1,128]{2,1,0:T(1,128)} %bitcast.26), calls=%async_computation | async-start | bytes 131072 | tf_op jit(solution)/shard_map/all_to_all | solution.py:436
  13.0 1.1 %copy.13 = bf16[16,64,128]{2,0,1:T(8,128)(2,1)S(1)} copy(bf16[16,64,128]{2,1,0:T(8,128)(2,1)} %param.6) | data formatting | bytes 524288 | tf_op args[0]
  14.1 0.0 copy-start
  14.2 0.9 copy-done
  15.1 0.9 copy-done.1
  16.0 6.6 %all-to-all-done = s32[128,1,128]{2,1,0:T(1,128)S(1)} async-done(((s32[128,1,128]{2,1,0:T(1,128)}), s32[128,1,128]{2,1,0:T(1,128)S(1)}, u32[]{:S(2)}, u32[]{:S(2)}) %all-to-all-start) | async-done | bytes 65568 | tf_op jit(solution)/shard_map/all_to_all | solution.py:436
  22.6 1.2 %pack.1 = (bf16[256,16,128]{2,1,0:T(8,128)(2,1)S(1)}, s32[8,128]{1,0:T(8,128)S(1)}) custom-call(s32[128,128]{1,0:T(8,128)S(1)} %bitcast.23, bf16[64,16,128]{2,1,0:T(8,128)(2,1)S(1)} %bitcast.21), custom_call_target="tpu_custom_call" | custom-call | tf_op jit(solution)/shard_map/pack/pallas_call | solution.py:101
  23.7 0.0 copy-start.2
  23.7 0.0 copy-start.3
  23.7 23.7 %all_to_all.22 = bf16[128,2,16,128]{3,2,1,0:T(8,128)(2,1)S(1)} all-to-all(bf16[128,2,16,128]{3,2,1,0:T(8,128)(2,1)S(1)} %bitcast.22), channel_id=1, replica_groups=mesh['face'=4,'tile'=32] {'face','tile'}, dimensions={0} | all-to-all | bytes 2097152 | tf_op jit(solution)/shard_map/all_to_all | solution.py:436
  47.5 2.8 %regrid.1 = (f32[1088,128]{1,0:T(8,128)S(1)}, f32[1280,128]{1,0:T(8,128)S(1)}, f32[272,128]{1,0:T(8,128)S(1)}, f32[272,128]{1,0:T(8,128)S(1)}, f32[40,128]{1,0:T(8,128)S(1)}, /*index=5*/f32[40,128]{1,0:T(8,128)S(1)}) custom-call(s32[8,128]{1,0:T(8,128)S(1)} %copy-done.3, s32[1]{0:T(128)} %bitcast.7.tile_ref, s32[1]{0:T(128)} %bitcast.8.face_ref, ...), custom_call_target="tpu_custom_call" | custom-call | tf_op jit(solution)/shard_map/regrid/pallas_call | solution.py:197
  50.3 0.2 collective-permute-start
  50.5 0.7 collective-permute-start.1
  51.2 1.6 %collective-permute-start.2 = (f32[40,128]{1,0:T(8,128)S(1)}, f32[40,128]{1,0:T(8,128)S(1)}, u32[]{:S(2)}, u32[]{:S(2)}) collective-permute-start(f32[40,128]{1,0:T(8,128)S(1)} %get-tuple-element.41), channel_id=1, source_target_pairs={{0,32},{64,96},{32,0},{96,64},{1,33},{65,97},{33,1},{97,65},{2,34}... | collective-permute-start | bytes 61448 | tf_op jit(solution)/shard_map/ppermute | solution.py:459
  52.7 1.2 %collective-permute-start.3 = (f32[40,128]{1,0:T(8,128)S(1)}, f32[40,128]{1,0:T(8,128)S(1)}, u32[]{:S(2)}, u32[]{:S(2)}) collective-permute-start(f32[40,128]{1,0:T(8,128)S(1)} %get-tuple-element.42), channel_id=1, source_target_pairs={{32,64},{96,0},{64,32},{0,96},{33,65},{97,1},{65,33},{1,97},{34,66... | collective-permute-start | bytes 61448 | tf_op jit(solution)/shard_map/ppermute | solution.py:459
  53.9 2.9 %inner.1 = (f32[1024,128]{1,0:T(8,128)S(1)}, f32[32,8,128]{2,1,0:T(8,128)S(1)}) custom-call(f32[1280,128]{1,0:T(8,128)S(1)} %get-tuple-element.36.turned_ref), custom_call_target="tpu_custom_call" | custom-call | flops 16777216 | bytes 12582912 | tf_op jit(solution)/shard_map/inner/pallas_call | solution.py:266
  56.9 0.0 collective-permute-done.2.wide0_ref
  56.9 3.0 %collective-permute-done.3.wide1_ref = f32[40,128]{1,0:T(8,128)S(1)} collective-permute-done((f32[40,128]{1,0:T(8,128)S(1)}, f32[40,128]{1,0:T(8,128)S(1)}, u32[]{:S(2)}, u32[]{:S(2)}) %collective-permute-start.3) | collective-permute-done | bytes 20512 | tf_op jit(solution)/shard_map/ppermute | solution.py:459
  59.9 0.0 collective-permute-done.tall0_ref
  59.9 0.0 collective-permute-done.1.tall1_ref
  59.9 10.1 %push.1 = s32[2176,128]{1,0:T(8,128)S(1)} custom-call(s32[8,128]{1,0:T(8,128)S(1)} %copy-done.3, s32[1]{0:T(128)} %bitcast.7.tile_ref, s32[1]{0:T(128)} %bitcast.8.face_ref, f32[1088,128]{1,0:T(8,128)S(1)} %get-tuple-element.35.field_ref, f32[1280,128]{1,0:T(8,128)S(1)} %get-tuple-element.36.turned_ref, f32[1024,128]{1,0:T(8,128)S(1)} %get-tuple-element.37.turn_ref, ...), custom_call_target="tpu_custom_call" | custom-call | tf_op jit(solution)/shard_map/push/pallas_call | solution.py:383
  70.0 25.7 %all_to_all.23 = s32[128,17,1,128]{3,2,1,0:T(1,128)S(1)} all-to-all(s32[128,17,1,128]{3,2,1,0:T(1,128)S(1)} %bitcast.18), channel_id=1, replica_groups=mesh['face'=4,'tile'=32] {'face','tile'}, dimensions={0} | all-to-all | bytes 2228224 | tf_op jit(solution)/shard_map/all_to_all | solution.py:436
  95.7 2.6 %collect.1 = f32[1024,128]{1,0:T(8,128)} custom-call(s32[8,128]{1,0:T(8,128)S(1)} %get-tuple-element.28.slots_ref, s32[2176,128]{1,0:T(8,128)S(1)} %bitcast.19), custom_call_target="tpu_custom_call" | custom-call | tf_op jit(solution)/shard_map/collect/pallas_call | solution.py:425
  (4 shorter events, 0.0 us)
Async XLA Ops:
  1.5 21.0 %all-to-all-start = ((s32[128,1,128]{2,1,0:T(1,128)}), s32[128,1,128]{2,1,0:T(1,128)S(1)}, u32[]{:S(2)}, u32[]{:S(2)}) async-start(s32[128,1,128]{2,1,0:T(1,128)} %bitcast.26), calls=%async_computation | async-start | bytes 131072 | tf_op jit(solution)/shard_map/all_to_all | solution.py:436
  14.1 0.9 copy-start
  15.1 0.9 copy-start.1
  23.7 23.7 %copy-start.2 = (f32[32,256]{1,0:T(8,128)S(1)}, f32[32,256]{1,0:T(8,128)}, u32[]{:S(2)}) copy-start(f32[32,256]{1,0:T(8,128)} %truth_ref.1) | copy-start | bytes 98308
  23.7 23.7 %copy-start.3 = (s32[8,128]{1,0:T(8,128)S(1)}, s32[8,128]{1,0:T(8,128)}, u32[]{:S(2)}) copy-start(s32[8,128]{1,0:T(8,128)} %get-tuple-element.29.place_ref) | copy-start | bytes 12292
  50.3 9.7 %collective-permute-start = (f32[272,128]{1,0:T(8,128)S(1)}, f32[272,128]{1,0:T(8,128)S(1)}, u32[]{:S(2)}, u32[]{:S(2)}) collective-permute-start(f32[272,128]{1,0:T(8,128)S(1)} %get-tuple-element.39), channel_id=1, source_target_pairs={{0,1},{2,3},{4,5},{6,7},{8,9},{10,11},{12,13},{14,15},{16,17},{18,... | collective-permute-start | bytes 417800 | tf_op jit(solution)/shard_map/ppermute | solution.py:459
  50.5 9.4 %collective-permute-start.1 = (f32[272,128]{1,0:T(8,128)S(1)}, f32[272,128]{1,0:T(8,128)S(1)}, u32[]{:S(2)}, u32[]{:S(2)}) collective-permute-start(f32[272,128]{1,0:T(8,128)S(1)} %get-tuple-element.40), channel_id=1, source_target_pairs={{1,2},{3,4},{5,6},{7,8},{9,10},{11,12},{13,14},{15,16},{17,18},{19... | collective-permute-start | bytes 417800 | tf_op jit(solution)/shard_map/ppermute | solution.py:459
  51.2 5.7 %collective-permute-start.2 = (f32[40,128]{1,0:T(8,128)S(1)}, f32[40,128]{1,0:T(8,128)S(1)}, u32[]{:S(2)}, u32[]{:S(2)}) collective-permute-start(f32[40,128]{1,0:T(8,128)S(1)} %get-tuple-element.41), channel_id=1, source_target_pairs={{0,32},{64,96},{32,0},{96,64},{1,33},{65,97},{33,1},{97,65},{2,34}... | collective-permute-start | bytes 61448 | tf_op jit(solution)/shard_map/ppermute | solution.py:459
  52.7 7.2 %collective-permute-start.3 = (f32[40,128]{1,0:T(8,128)S(1)}, f32[40,128]{1,0:T(8,128)S(1)}, u32[]{:S(2)}, u32[]{:S(2)}) collective-permute-start(f32[40,128]{1,0:T(8,128)S(1)} %get-tuple-element.42), channel_id=1, source_target_pairs={{32,64},{96,0},{64,32},{0,96},{33,65},{97,1},{65,33},{1,97},{34,66... | collective-permute-start | bytes 61448 | tf_op jit(solution)/shard_map/ppermute | solution.py:459

commit v8 on v7

--- a/solution.py
+++ b/solution.py
@@ -107,7 +107,20 @@
     )(asked, bands)
 
 
-def prepare_kernel(pos_ref, factor_ref, posn_ref, weight_ref):
+def regrid_kernel(
+    place_ref, tile_ref, face_ref, recv_ref, pos_ref, factor_ref, truth_ref,
+    field_ref, turned_ref, posn_ref, weight_ref, tall0_ref, tall1_ref, wide0_ref, wide1_ref,
+    low_ref, high_ref,
+):
+    def spread(row, carry):
+        for half in range(2):
+            for k, tab in enumerate((low_ref, high_ref)):
+                strip = recv_ref[place_ref[k, 2 * row + half]].astype(F32)
+                tab[pl.ds(half * ROWS + row, M, stride=TABLE), :] = strip
+        return carry
+
+    lax.fori_loop(0, ROWS, spread, 0, unroll=8)
+
     for half in range(2):
         factors = [factor_ref[pl.ds(j * BANDS + half, ROWS, stride=2), :] for j in range(POINTS)]
         total = factors[0] + factors[1] + factors[2] + factors[3]
@@ -115,34 +128,6 @@
             spot = j * BANDS + half * ROWS
             posn_ref[pl.ds(spot, ROWS), :] = pos_ref[pl.ds(j * BANDS + half, ROWS, stride=2), :]
             weight_ref[pl.ds(spot, ROWS), :] = factors[j] / total
-
-
-def prepare(pos, factor):
-    return pl.pallas_call(
-        prepare_kernel,
-        out_shape=(
-            struct((POINTS * BANDS, LANES), I32),
-            struct((POINTS * BANDS, LANES)),
-        ),
-        name="prepare",
-        cost_estimate=pl.CostEstimate(flops=1 << 20, bytes_accessed=1 << 20, transcendentals=0),
-        compiler_params=pltpu.CompilerParams(vmem_limit_bytes=2 << 20),
-    )(pos, factor)
-
-
-def regrid_kernel(
-    place_ref, tile_ref, face_ref, recv_ref, posn_ref, weight_ref, truth_ref,
-    field_ref, turned_ref, tall0_ref, tall1_ref, wide0_ref, wide1_ref,
-    low_ref, high_ref,
-):
-    def spread(row, carry):
-        for half in range(2):
-            for k, tab in enumerate((low_ref, high_ref)):
-                strip = recv_ref[place_ref[k, 2 * row + half]].astype(F32)
-                tab[pl.ds(half * ROWS + row, M, stride=TABLE), :] = strip
-        return carry
-
-    lax.fori_loop(0, ROWS, spread, 0, unroll=8)
 
     def regrid(block, carry):
         row = pl.multiple_of(block * 8, 8)
@@ -191,7 +176,7 @@
 SMEM = pl.BlockSpec(memory_space=pltpu.SMEM)
 
 
-def regrid(place, tile, face, recv, posn, weight, truth):
+def regrid(place, tile, face, recv, pos, factor, truth):
     tall = struct(((M + 1) * 2 * RANGE, LANES))
     wide = struct(((QUADS + 1) * RANGE, LANES))
     return pl.pallas_call(
@@ -200,12 +185,14 @@
         out_shape=(
             struct(((M + 1) * BANDS, LANES)),
             struct(((QUADS + 1) * 2 * LANES, LANES)),
+            struct((POINTS * BANDS, LANES), I32),
+            struct((POINTS * BANDS, LANES)),
             tall, tall, wide, wide,
         ),
         scratch_shapes=[pltpu.VMEM((M * TABLE, LANES), F32)] * 2,
         name="regrid",
         compiler_params=pltpu.CompilerParams(vmem_limit_bytes=8 << 20),
-    )(place, tile, face, recv, posn, weight, truth)
+    )(place, tile, face, recv, pos, factor, truth)
 
 
 def steep(diff):
@@ -439,17 +426,21 @@
 def local(predicted_field, parent_band_holder, parent_band_slot, neighbour_positions, unscaled_neighbour_factor, truth_field):
     tiles, faces = lax.axis_size("tile"), lax.axis_size("face")
     bands = jnp.transpose(predicted_field, (1, 0, 2))
-    posn, weight = prepare(
-        neighbour_positions.reshape(POINTS * BANDS, LANES),
-        unscaled_neighbour_factor.reshape(POINTS * BANDS, LANES),
-    )
     wanted, place = request(parent_band_holder.T, parent_band_slot.T)
     tile = lax.axis_index("tile").astype(I32).reshape(1)
     face = lax.axis_index("face").astype(I32).reshape(1)
-    asked, posn, weight, tile, face = lax.optimization_barrier((exchange(wanted), posn, weight, tile, face))
+    asked, tile, face = lax.optimization_barrier((exchange(wanted), tile, face))
     outgoing, slots = pack(asked, bands)
     recv = exchange(outgoing.reshape(DEVICES, 2, M, LANES)).reshape(2 * DEVICES, M, LANES)
-    field, turned, *messages = regrid(place, tile, face, recv, posn, weight, truth_field)
+    field, turned, posn, weight, *messages = regrid(
+        place,
+        tile,
+        face,
+        recv,
+        neighbour_positions.reshape(POINTS * BANDS, LANES),
+        unscaled_neighbour_factor.reshape(POINTS * BANDS, LANES),
+        truth_field,
+    )
     rounds = [
         ("tile", [(i, i + 1) for i in range(0, tiles - 1, 2)]),
         ("tile", [(i, i + 1) for i in range(1, tiles - 1, 2)]),

time: 98.6 us -> 98.6 us (level)
  local copies, waits for them, and re-layouts: 2.94 us -> 1.15 us
  waiting for transfers between devices: 9.62 us -> 11.4 us
    all_to_all x1, waiting for transfers between devices: 6.57 us -> 8.41 us  [exchange(): return lax.all_to_all(x, AXES, split_axis=0, concat_axis=0, tiled=True)]
    unnamed x9, local copies, waits for them, and re-layouts: 2.94 us -> 1.15 us
where the time goes in v8:
time: 98.6 us; the launch traced here: 98.4 us
  blocking collectives  49.4 us (50%)
  Pallas kernels  21.1 us (21%)
  starting transfers between devices  15.1 us (15%)
  waiting for transfers between devices  11.4 us (12%)
  local copies, waits for them, and re-layouts  1.15 us (1%)
    all_to_all x2, blocking collectives, exchange(): return lax.all_to_all(x, AXES, split_axis=0, concat_axis=0, tiled=True)  49.4 us
    all_to_all x1, starting transfers between devices, exchange(): return lax.all_to_all(x, AXES, split_axis=0, concat_axis=0, tiled=True)  11.5 us
    pallas_call x1, Pallas kernels, push(): pl.pallas_call(push_kernel, in_specs=[SMEM] * 3 + [VMEM] * len(arrays), o...  10.1 us
    all_to_all x1, waiting for transfers between devices, exchange(): return lax.all_to_all(x, AXES, split_axis=0, concat_axis=0, tiled=True)  8.41 us
    ppermute x4, starting transfers between devices, local(): lax.ppermute(m, axis, pairs + [(j, i) for i, j in pairs])  3.65 us
    ppermute x4, waiting for transfers between devices, local(): lax.ppermute(m, axis, pairs + [(j, i) for i, j in pairs])  3.03 us
    pallas_call x1, Pallas kernels, inner(): pl.pallas_call(inner_kernel, out_shape=(struct((QUADS * WIDTH, LANES)), s...  2.95 us
    pallas_call x1, Pallas kernels, regrid(): pl.pallas_call(regrid_kernel, in_specs=[SMEM] * 3 + [VMEM] * 4, out_shape...  2.85 us
  transfers between devices with their start and end apart: 5, of which 2 were waited for; matrix products, arithmetic and copies ran while one was open for 1% of the time, Pallas kernels for 3%

profile of v8, /device:TPU:1, one launch (start us, length us, event | category | flops | bytes accessed | tf_op | source)
XLA Modules:
  0.0 98.4 jit_solution(6587183488897853366)
XLA Ops:
  0.0 1.5 %request.1 = (s32[128,128]{1,0:T(8,128)}, s32[8,128]{1,0:T(8,128)}) custom-call(s32[2,64]{1,0:T(2,128)} %bitcast.27, s32[2,64]{1,0:T(2,128)} %bitcast.28), custom_call_target="tpu_custom_call" | custom-call | tf_op jit(solution)/shard_map/request/pallas_call | solution.py:76
  1.5 11.5 %all-to-all-start = ((s32[128,1,128]{2,1,0:T(1,128)}), s32[128,1,128]{2,1,0:T(1,128)S(1)}, u32[]{:S(2)}, u32[]{:S(2)}) async-start(s32[128,1,128]{2,1,0:T(1,128)} %bitcast.26), calls=%async_computation | async-start | bytes 131072 | tf_op jit(solution)/shard_map/all_to_all | solution.py:423
  13.0 1.1 %copy.13 = bf16[16,64,128]{2,0,1:T(8,128)(2,1)S(1)} copy(bf16[16,64,128]{2,1,0:T(8,128)(2,1)} %param.6) | data formatting | bytes 524288 | tf_op args[0]
  14.1 8.4 %all-to-all-done = s32[128,1,128]{2,1,0:T(1,128)S(1)} async-done(((s32[128,1,128]{2,1,0:T(1,128)}), s32[128,1,128]{2,1,0:T(1,128)S(1)}, u32[]{:S(2)}, u32[]{:S(2)}) %all-to-all-start) | async-done | bytes 65568 | tf_op jit(solution)/shard_map/all_to_all | solution.py:423
  22.6 1.2 %pack.1 = (bf16[256,16,128]{2,1,0:T(8,128)(2,1)S(1)}, s32[8,128]{1,0:T(8,128)S(1)}) custom-call(s32[128,128]{1,0:T(8,128)S(1)} %bitcast.23, bf16[64,16,128]{2,1,0:T(8,128)(2,1)S(1)} %bitcast.21), custom_call_target="tpu_custom_call" | custom-call | tf_op jit(solution)/shard_map/pack/pallas_call | solution.py:101
  23.7 0.0 copy-start
  23.7 0.0 copy-start.1
  23.7 0.0 copy-start.2
  23.8 0.0 copy-start.3
  23.8 23.7 %all_to_all.22 = bf16[128,2,16,128]{3,2,1,0:T(8,128)(2,1)S(1)} all-to-all(bf16[128,2,16,128]{3,2,1,0:T(8,128)(2,1)S(1)} %bitcast.22), channel_id=1, replica_groups=mesh['face'=4,'tile'=32] {'face','tile'}, dimensions={0} | all-to-all | bytes 2097152 | tf_op jit(solution)/shard_map/all_to_all | solution.py:423
  47.5 0.0 copy-done
  47.5 2.9 %regrid.1 = (f32[1088,128]{1,0:T(8,128)S(1)}, f32[1280,128]{1,0:T(8,128)S(1)}, s32[256,128]{1,0:T(8,128)S(1)}, f32[256,128]{1,0:T(8,128)S(1)}, f32[272,128]{1,0:...) custom-call(s32[8,128]{1,0:T(8,128)S(1)} %copy-done.3, s32[1]{0:T(128)} %bitcast.5.tile_ref, ...), custom_call_target="tpu_custom_call" | custom-call | tf_op jit(solution)/shard_map/regrid/pallas_call | solution.py:182
  50.4 0.2 collective-permute-start
  50.6 0.7 collective-permute-start.1
  51.2 1.6 %collective-permute-start.2 = (f32[40,128]{1,0:T(8,128)S(1)}, f32[40,128]{1,0:T(8,128)S(1)}, u32[]{:S(2)}, u32[]{:S(2)}) collective-permute-start(f32[40,128]{1,0:T(8,128)S(1)} %get-tuple-element.37), channel_id=1, source_target_pairs={{0,32},{64,96},{32,0},{96,64},{1,33},{65,97},{33,1},{97,65},{2,34}... | collective-permute-start | bytes 61448 | tf_op jit(solution)/shard_map/ppermute | solution.py:450
  52.8 1.2 %collective-permute-start.3 = (f32[40,128]{1,0:T(8,128)S(1)}, f32[40,128]{1,0:T(8,128)S(1)}, u32[]{:S(2)}, u32[]{:S(2)}) collective-permute-start(f32[40,128]{1,0:T(8,128)S(1)} %get-tuple-element.38), channel_id=1, source_target_pairs={{32,64},{96,0},{64,32},{0,96},{33,65},{97,1},{65,33},{1,97},{34,66... | collective-permute-start | bytes 61448 | tf_op jit(solution)/shard_map/ppermute | solution.py:450
  54.0 3.0 %inner.1 = (f32[1024,128]{1,0:T(8,128)S(1)}, f32[32,8,128]{2,1,0:T(8,128)S(1)}) custom-call(f32[1280,128]{1,0:T(8,128)S(1)} %get-tuple-element.30.turned_ref), custom_call_target="tpu_custom_call" | custom-call | flops 16777216 | bytes 12582912 | tf_op jit(solution)/shard_map/inner/pallas_call | solution.py:253
  57.0 0.0 collective-permute-done.2.wide0_ref
  57.0 3.0 %collective-permute-done.3.wide1_ref = f32[40,128]{1,0:T(8,128)S(1)} collective-permute-done((f32[40,128]{1,0:T(8,128)S(1)}, f32[40,128]{1,0:T(8,128)S(1)}, u32[]{:S(2)}, u32[]{:S(2)}) %collective-permute-start.3) | collective-permute-done | bytes 20512 | tf_op jit(solution)/shard_map/ppermute | solution.py:450
  60.0 0.0 collective-permute-done.tall0_ref
  60.0 0.0 collective-permute-done.1.tall1_ref
  60.0 10.1 %push.1 = s32[2176,128]{1,0:T(8,128)S(1)} custom-call(s32[8,128]{1,0:T(8,128)S(1)} %copy-done.3, s32[1]{0:T(128)} %bitcast.5.tile_ref, s32[1]{0:T(128)} %bitcast.6.face_ref, f32[1088,128]{1,0:T(8,128)S(1)} %get-tuple-element.29.field_ref, f32[1280,128]{1,0:T(8,128)S(1)} %get-tuple-element.30.turned_ref, f32[1024,128]{1,0:T(8,128)S(1)} %get-tuple-element.31.turn_ref, ...), custom_call_target="tpu_custom_call" | custom-call | tf_op jit(solution)/shard_map/push/pallas_call | solution.py:370
  70.1 25.7 %all_to_all.23 = s32[128,17,1,128]{3,2,1,0:T(1,128)S(1)} all-to-all(s32[128,17,1,128]{3,2,1,0:T(1,128)S(1)} %bitcast.18), channel_id=1, replica_groups=mesh['face'=4,'tile'=32] {'face','tile'}, dimensions={0} | all-to-all | bytes 2228224 | tf_op jit(solution)/shard_map/all_to_all | solution.py:423
  95.8 2.6 %collect.1 = f32[1024,128]{1,0:T(8,128)} custom-call(s32[8,128]{1,0:T(8,128)S(1)} %get-tuple-element.24.slots_ref, s32[2176,128]{1,0:T(8,128)S(1)} %bitcast.19), custom_call_target="tpu_custom_call" | custom-call | tf_op jit(solution)/shard_map/collect/pallas_call | solution.py:412
  (3 shorter events, 0.0 us)
Async XLA Ops:
  1.5 21.0 %all-to-all-start = ((s32[128,1,128]{2,1,0:T(1,128)}), s32[128,1,128]{2,1,0:T(1,128)S(1)}, u32[]{:S(2)}, u32[]{:S(2)}) async-start(s32[128,1,128]{2,1,0:T(1,128)} %bitcast.26), calls=%async_computation | async-start | bytes 131072 | tf_op jit(solution)/shard_map/all_to_all | solution.py:423
  23.7 23.8 %copy-start = (s32[4,64,128]{2,1,0:T(8,128)S(1)}, s32[4,64,128]{2,1,0:T(8,128)}, u32[]{:S(2)}) copy-start(s32[4,64,128]{2,1,0:T(8,128)} %param.9) | copy-start | bytes 393220
  23.7 23.8 %copy-start.1 = (f32[4,64,128]{2,1,0:T(8,128)S(1)}, f32[4,64,128]{2,1,0:T(8,128)}, u32[]{:S(2)}) copy-start(f32[4,64,128]{2,1,0:T(8,128)} %param.10) | copy-start | bytes 393220
  23.7 23.7 %copy-start.2 = (f32[32,256]{1,0:T(8,128)S(1)}, f32[32,256]{1,0:T(8,128)}, u32[]{:S(2)}) copy-start(f32[32,256]{1,0:T(8,128)} %truth_ref.1) | copy-start | bytes 98308
  23.8 23.7 %copy-start.3 = (s32[8,128]{1,0:T(8,128)S(1)}, s32[8,128]{1,0:T(8,128)}, u32[]{:S(2)}) copy-start(s32[8,128]{1,0:T(8,128)} %get-tuple-element.25.place_ref) | copy-start | bytes 12292
  50.4 9.7 %collective-permute-start = (f32[272,128]{1,0:T(8,128)S(1)}, f32[272,128]{1,0:T(8,128)S(1)}, u32[]{:S(2)}, u32[]{:S(2)}) collective-permute-start(f32[272,128]{1,0:T(8,128)S(1)} %get-tuple-element.35), channel_id=1, source_target_pairs={{0,1},{2,3},{4,5},{6,7},{8,9},{10,11},{12,13},{14,15},{16,17},{18,... | collective-permute-start | bytes 417800 | tf_op jit(solution)/shard_map/ppermute | solution.py:450
  50.6 9.4 %collective-permute-start.1 = (f32[272,128]{1,0:T(8,128)S(1)}, f32[272,128]{1,0:T(8,128)S(1)}, u32[]{:S(2)}, u32[]{:S(2)}) collective-permute-start(f32[272,128]{1,0:T(8,128)S(1)} %get-tuple-element.36), channel_id=1, source_target_pairs={{1,2},{3,4},{5,6},{7,8},{9,10},{11,12},{13,14},{15,16},{17,18},{19... | collective-permute-start | bytes 417800 | tf_op jit(solution)/shard_map/ppermute | solution.py:450
  51.2 5.7 %collective-permute-start.2 = (f32[40,128]{1,0:T(8,128)S(1)}, f32[40,128]{1,0:T(8,128)S(1)}, u32[]{:S(2)}, u32[]{:S(2)}) collective-permute-start(f32[40,128]{1,0:T(8,128)S(1)} %get-tuple-element.37), channel_id=1, source_target_pairs={{0,32},{64,96},{32,0},{96,64},{1,33},{65,97},{33,1},{97,65},{2,34}... | collective-permute-start | bytes 61448 | tf_op jit(solution)/shard_map/ppermute | solution.py:450
  52.8 7.2 %collective-permute-start.3 = (f32[40,128]{1,0:T(8,128)S(1)}, f32[40,128]{1,0:T(8,128)S(1)}, u32[]{:S(2)}, u32[]{:S(2)}) collective-permute-start(f32[40,128]{1,0:T(8,128)S(1)} %get-tuple-element.38), channel_id=1, source_target_pairs={{32,64},{96,0},{64,32},{0,96},{33,65},{97,1},{65,33},{1,97},{34,66... | collective-permute-start | bytes 61448 | tf_op jit(solution)/shard_map/ppermute | solution.py:450

commit v9 on v7

--- a/solution.py
+++ b/solution.py
@@ -165,7 +165,7 @@
 
     for half in range(2):
         field_ref[pl.ds(M * BANDS + half * ROWS, ROWS), :] = truth_ref[:, half * LANES : (half + 1) * LANES]
-    odd = tile_ref[0] & 1
+    odd = 1 - (tile_ref[0] & 1)
     for m in range(M + 1):
         for half in range(2):
             spot = m * BANDS + half * ROWS
@@ -180,7 +180,7 @@
                 parts = [truth_ref[:, half * LANES : (half + 1) * LANES]] * 4
             turned = jnp.transpose(jnp.concatenate(parts, axis=0))
             turned_ref[pl.ds(q * 2 * LANES + half * LANES, LANES), :] = turned
-    odd = face_ref[0] & 1
+    odd = 1 - (face_ref[0] & 1)
     for q in range(QUADS + 1):
         for message, edge in ((wide0_ref, 1 - odd), (wide1_ref, odd)):
             columns = pl.ds(pl.multiple_of(q * 2 * LANES + edge * (2 * LANES - 8), 8), 8)
@@ -277,13 +277,13 @@
     tall0_ref, tall1_ref, wide0_ref, wide1_ref,
     out_ref, ext, grad, west, east, kept_columns, kept_rows,
 ):
-    odd = tile_ref[0] & 1
+    odd = 1 - (tile_ref[0] & 1)
     for mh in range(2 * (M + 1)):
         for message, below in ((tall0_ref, 1 - odd), (tall1_ref, odd)):
             rows = pl.ds(pl.multiple_of(mh * EXT + below * (ROWS + 8), 8), 8)
             ext[rows, :] = message[pl.ds(mh * 8, 8), :]
         ext[pl.ds(mh * EXT + 8, ROWS), :] = field_ref[pl.ds(mh * ROWS, ROWS), :]
-    even = jnp.full((8, LANES), face_ref[0] & 1, I32) == 0
+    even = jnp.full((8, LANES), face_ref[0] & 1, I32) == 1
     for q in range(QUADS + 1):
         ones, twos = wide0_ref[pl.ds(q * 8, 8), :], wide1_ref[pl.ds(q * 8, 8), :]
         west[pl.ds(q * 16, 8), :] = jnp.where(even, twos, ones)
@@ -451,10 +451,10 @@
     recv = exchange(outgoing.reshape(DEVICES, 2, M, LANES)).reshape(2 * DEVICES, M, LANES)
     field, turned, *messages = regrid(place, tile, face, recv, posn, weight, truth_field)
     rounds = [
+        ("tile", [(i, i + 1) for i in range(1, tiles - 1, 2)]),
         ("tile", [(i, i + 1) for i in range(0, tiles - 1, 2)]),
-        ("tile", [(i, i + 1) for i in range(1, tiles - 1, 2)]),
+        ("face", [(i, (i + 1) % faces) for i in range(1, faces, 2)]),
         ("face", [(i, i + 1) for i in range(0, faces, 2)]),
-        ("face", [(i, (i + 1) % faces) for i in range(1, faces, 2)]),
     ]
     messages = [lax.ppermute(m, axis, pairs + [(j, i) for i, j in pairs]) for m, (axis, pairs) in zip(messages, rounds)]
     turn, kept = inner(turned)

time: 98.6 us -> 102 us (1.034)
  blocking collectives: 49.4 us -> 51 us
  starting transfers between devices: 15.1 us -> 16.2 us
    all_to_all x2, blocking collectives: 49.4 us -> 51 us  [exchange(): return lax.all_to_all(x, AXES, split_axis=0, concat_axis=0, tiled=True)]
    ppermute x4, starting transfers between devices: 3.65 us -> 4.74 us  [local(): lax.ppermute(m, axis, pairs + [(j, i) for i, j in pairs])]
where the time goes in v9:
time: 102 us
  blocking collectives  51 us (50%)
  Pallas kernels  21.1 us (21%)
  starting transfers between devices  16.2 us (16%)
  waiting for transfers between devices  10.1 us (10%)
  local copies, waits for them, and re-layouts  2.94 us (3%)
    all_to_all x2, blocking collectives, exchange(): return lax.all_to_all(x, AXES, split_axis=0, concat_axis=0, tiled=True)  51 us
    all_to_all x1, starting transfers between devices, exchange(): return lax.all_to_all(x, AXES, split_axis=0, concat_axis=0, tiled=True)  11.5 us
    pallas_call x1, Pallas kernels, push(): pl.pallas_call(push_kernel, in_specs=[SMEM] * 3 + [VMEM] * len(arrays), o...  10.1 us
    all_to_all x1, waiting for transfers between devices, exchange(): return lax.all_to_all(x, AXES, split_axis=0, concat_axis=0, tiled=True)  6.57 us
    ppermute x4, starting transfers between devices, local(): lax.ppermute(m, axis, pairs + [(j, i) for i, j in pairs])  4.74 us
    ppermute x4, waiting for transfers between devices, local(): lax.ppermute(m, axis, pairs + [(j, i) for i, j in pairs])  3.56 us
    unnamed x9, local copies, waits for them, and re-layouts  2.94 us
    pallas_call x1, Pallas kernels, inner(): pl.pallas_call(inner_kernel, out_shape=(struct((QUADS * WIDTH, LANES)), s...  2.94 us
  transfers between devices with their start and end apart: 5, of which 2 were waited for; matrix products, arithmetic and copies ran while one was open for 1% of the time, Pallas kernels for 3%

profile of v9, /device:TPU:1, one launch (start us, length us, event | category | flops | bytes accessed | tf_op | source)
XLA Modules:
  0.0 101.5 jit_solution(1541712178526917583)
XLA Ops:
  0.0 1.5 %request.1 = (s32[128,128]{1,0:T(8,128)}, s32[8,128]{1,0:T(8,128)}) custom-call(s32[2,64]{1,0:T(2,128)} %bitcast.27, s32[2,64]{1,0:T(2,128)} %bitcast.28), custom_call_target="tpu_custom_call" | custom-call | tf_op jit(solution)/shard_map/request/pallas_call | solution.py:76
  1.5 11.5 %all-to-all-start = ((s32[128,1,128]{2,1,0:T(1,128)}), s32[128,1,128]{2,1,0:T(1,128)S(1)}, u32[]{:S(2)}, u32[]{:S(2)}) async-start(s32[128,1,128]{2,1,0:T(1,128)} %bitcast.26), calls=%async_computation | async-start | bytes 131072 | tf_op jit(solution)/shard_map/all_to_all | solution.py:436
  13.0 1.1 %copy.13 = bf16[16,64,128]{2,0,1:T(8,128)(2,1)S(1)} copy(bf16[16,64,128]{2,1,0:T(8,128)(2,1)} %param.6) | data formatting | bytes 524288 | tf_op args[0]
  14.1 0.0 copy-start
  14.2 0.9 copy-done
  15.1 0.9 copy-done.1
  16.0 6.6 %all-to-all-done = s32[128,1,128]{2,1,0:T(1,128)S(1)} async-done(((s32[128,1,128]{2,1,0:T(1,128)}), s32[128,1,128]{2,1,0:T(1,128)S(1)}, u32[]{:S(2)}, u32[]{:S(2)}) %all-to-all-start) | async-done | bytes 65568 | tf_op jit(solution)/shard_map/all_to_all | solution.py:436
  22.6 1.2 %pack.1 = (bf16[256,16,128]{2,1,0:T(8,128)(2,1)S(1)}, s32[8,128]{1,0:T(8,128)S(1)}) custom-call(s32[128,128]{1,0:T(8,128)S(1)} %bitcast.23, bf16[64,16,128]{2,1,0:T(8,128)(2,1)S(1)} %bitcast.21), custom_call_target="tpu_custom_call" | custom-call | tf_op jit(solution)/shard_map/pack/pallas_call | solution.py:101
  23.7 0.0 copy-start.2
  23.7 0.0 copy-start.3
  23.7 23.7 %all_to_all.22 = bf16[128,2,16,128]{3,2,1,0:T(8,128)(2,1)S(1)} all-to-all(bf16[128,2,16,128]{3,2,1,0:T(8,128)(2,1)S(1)} %bitcast.22), channel_id=1, replica_groups=mesh['face'=4,'tile'=32] {'face','tile'}, dimensions={0} | all-to-all | bytes 2097152 | tf_op jit(solution)/shard_map/all_to_all | solution.py:436
  47.5 2.8 %regrid.1 = (f32[1088,128]{1,0:T(8,128)S(1)}, f32[1280,128]{1,0:T(8,128)S(1)}, f32[272,128]{1,0:T(8,128)S(1)}, f32[272,128]{1,0:T(8,128)S(1)}, f32[40,128]{1,0:T(8,128)S(1)}, /*index=5*/f32[40,128]{1,0:T(8,128)S(1)}) custom-call(s32[8,128]{1,0:T(8,128)S(1)} %copy-done.3, s32[1]{0:T(128)} %bitcast.7.tile_ref, s32[1]{0:T(128)} %bitcast.8.face_ref, ...), custom_call_target="tpu_custom_call" | custom-call | tf_op jit(solution)/shard_map/regrid/pallas_call | solution.py:197
  50.3 0.7 collective-permute-start
  51.0 2.3 %collective-permute-start.1 = (f32[272,128]{1,0:T(8,128)S(1)}, f32[272,128]{1,0:T(8,128)S(1)}, u32[]{:S(2)}, u32[]{:S(2)}) collective-permute-start(f32[272,128]{1,0:T(8,128)S(1)} %get-tuple-element.40), channel_id=1, source_target_pairs={{0,1},{2,3},{4,5},{6,7},{8,9},{10,11},{12,13},{14,15},{16,17},{18,... | collective-permute-start | bytes 417800 | tf_op jit(solution)/shard_map/ppermute | solution.py:459
  53.3 1.7 %collective-permute-start.2 = (f32[40,128]{1,0:T(8,128)S(1)}, f32[40,128]{1,0:T(8,128)S(1)}, u32[]{:S(2)}, u32[]{:S(2)}) collective-permute-start(f32[40,128]{1,0:T(8,128)S(1)} %get-tuple-element.41), channel_id=1, source_target_pairs={{32,64},{96,0},{64,32},{0,96},{33,65},{97,1},{65,33},{1,97},{34,66... | collective-permute-start | bytes 61448 | tf_op jit(solution)/shard_map/ppermute | solution.py:459
  55.0 0.0 collective-permute-start.3
  55.0 2.9 %inner.1 = (f32[1024,128]{1,0:T(8,128)S(1)}, f32[32,8,128]{2,1,0:T(8,128)S(1)}) custom-call(f32[1280,128]{1,0:T(8,128)S(1)} %get-tuple-element.36.turned_ref), custom_call_target="tpu_custom_call" | custom-call | flops 16777216 | bytes 12582912 | tf_op jit(solution)/shard_map/inner/pallas_call | solution.py:266
  58.0 3.6 %collective-permute-done.2.wide0_ref = f32[40,128]{1,0:T(8,128)S(1)} collective-permute-done((f32[40,128]{1,0:T(8,128)S(1)}, f32[40,128]{1,0:T(8,128)S(1)}, u32[]{:S(2)}, u32[]{:S(2)}) %collective-permute-start.2) | collective-permute-done | bytes 20512 | tf_op jit(solution)/shard_map/ppermute | solution.py:459
  61.5 0.0 collective-permute-done.3.wide1_ref
  61.5 0.0 collective-permute-done.tall0_ref
  61.5 0.0 collective-permute-done.1.tall1_ref
  61.5 10.1 %push.1 = s32[2176,128]{1,0:T(8,128)S(1)} custom-call(s32[8,128]{1,0:T(8,128)S(1)} %copy-done.3, s32[1]{0:T(128)} %bitcast.7.tile_ref, s32[1]{0:T(128)} %bitcast.8.face_ref, f32[1088,128]{1,0:T(8,128)S(1)} %get-tuple-element.35.field_ref, f32[1280,128]{1,0:T(8,128)S(1)} %get-tuple-element.36.turned_ref, f32[1024,128]{1,0:T(8,128)S(1)} %get-tuple-element.37.turn_ref, ...), custom_call_target="tpu_custom_call" | custom-call | tf_op jit(solution)/shard_map/push/pallas_call | solution.py:383
  71.6 27.3 %all_to_all.23 = s32[128,17,1,128]{3,2,1,0:T(1,128)S(1)} all-to-all(s32[128,17,1,128]{3,2,1,0:T(1,128)S(1)} %bitcast.18), channel_id=1, replica_groups=mesh['face'=4,'tile'=32] {'face','tile'}, dimensions={0} | all-to-all | bytes 2228224 | tf_op jit(solution)/shard_map/all_to_all | solution.py:436
  98.9 2.6 %collect.1 = f32[1024,128]{1,0:T(8,128)} custom-call(s32[8,128]{1,0:T(8,128)S(1)} %get-tuple-element.28.slots_ref, s32[2176,128]{1,0:T(8,128)S(1)} %bitcast.19), custom_call_target="tpu_custom_call" | custom-call | tf_op jit(solution)/shard_map/collect/pallas_call | solution.py:425
  (4 shorter events, 0.0 us)
Async XLA Ops:
  1.5 21.0 %all-to-all-start = ((s32[128,1,128]{2,1,0:T(1,128)}), s32[128,1,128]{2,1,0:T(1,128)S(1)}, u32[]{:S(2)}, u32[]{:S(2)}) async-start(s32[128,1,128]{2,1,0:T(1,128)} %bitcast.26), calls=%async_computation | async-start | bytes 131072 | tf_op jit(solution)/shard_map/all_to_all | solution.py:436
  14.1 0.9 copy-start
  15.1 0.9 copy-start.1
  23.7 23.7 %copy-start.2 = (f32[32,256]{1,0:T(8,128)S(1)}, f32[32,256]{1,0:T(8,128)}, u32[]{:S(2)}) copy-start(f32[32,256]{1,0:T(8,128)} %truth_ref.1) | copy-start | bytes 98308
  23.7 23.7 %copy-start.3 = (s32[8,128]{1,0:T(8,128)S(1)}, s32[8,128]{1,0:T(8,128)}, u32[]{:S(2)}) copy-start(s32[8,128]{1,0:T(8,128)} %get-tuple-element.29.place_ref) | copy-start | bytes 12292
  50.3 11.3 %collective-permute-start = (f32[272,128]{1,0:T(8,128)S(1)}, f32[272,128]{1,0:T(8,128)S(1)}, u32[]{:S(2)}, u32[]{:S(2)}) collective-permute-start(f32[272,128]{1,0:T(8,128)S(1)} %get-tuple-element.39), channel_id=1, source_target_pairs={{1,2},{3,4},{5,6},{7,8},{9,10},{11,12},{13,14},{15,16},{17,18},{19... | collective-permute-start | bytes 417800 | tf_op jit(solution)/shard_map/ppermute | solution.py:459
  51.0 10.6 %collective-permute-start.1 = (f32[272,128]{1,0:T(8,128)S(1)}, f32[272,128]{1,0:T(8,128)S(1)}, u32[]{:S(2)}, u32[]{:S(2)}) collective-permute-start(f32[272,128]{1,0:T(8,128)S(1)} %get-tuple-element.40), channel_id=1, source_target_pairs={{0,1},{2,3},{4,5},{6,7},{8,9},{10,11},{12,13},{14,15},{16,17},{18,... | collective-permute-start | bytes 417800 | tf_op jit(solution)/shard_map/ppermute | solution.py:459
  53.3 8.2 %collective-permute-start.2 = (f32[40,128]{1,0:T(8,128)S(1)}, f32[40,128]{1,0:T(8,128)S(1)}, u32[]{:S(2)}, u32[]{:S(2)}) collective-permute-start(f32[40,128]{1,0:T(8,128)S(1)} %get-tuple-element.41), channel_id=1, source_target_pairs={{32,64},{96,0},{64,32},{0,96},{33,65},{97,1},{65,33},{1,97},{34,66... | collective-permute-start | bytes 61448 | tf_op jit(solution)/shard_map/ppermute | solution.py:459
  55.0 6.5 %collective-permute-start.3 = (f32[40,128]{1,0:T(8,128)S(1)}, f32[40,128]{1,0:T(8,128)S(1)}, u32[]{:S(2)}, u32[]{:S(2)}) collective-permute-start(f32[40,128]{1,0:T(8,128)S(1)} %get-tuple-element.42), channel_id=1, source_target_pairs={{0,32},{64,96},{32,0},{96,64},{1,33},{65,97},{33,1},{97,65},{2,34}... | collective-permute-start | bytes 61448 | tf_op jit(solution)/shard_map/ppermute | solution.py:459

commit v10 on v7

--- a/solution.py
+++ b/solution.py
@@ -376,7 +376,7 @@
                 out_ref[pl.ds(spot + M, 1), :] |= (scale.astype(I32) & 0xFFFF) << shift
         return carry
 
-    lax.fori_loop(0, ROWS, adjoint, 0, unroll=4)
+    lax.fori_loop(0, ROWS, adjoint, 0, unroll=8)
 
 
 def push(place, tile, face, *arrays):

time: 98.6 us -> 98 us (level)
  no operation moved by 1% of the time
where the time goes in v10:
time: 98 us; the launch traced here: 97.7 us
  blocking collectives  49.4 us (50%)
  Pallas kernels  20.4 us (21%)
  starting transfers between devices  15.1 us (15%)
  waiting for transfers between devices  9.62 us (10%)
  local copies, waits for them, and re-layouts  2.94 us (3%)
    all_to_all x2, blocking collectives, exchange(): return lax.all_to_all(x, AXES, split_axis=0, concat_axis=0, tiled=True)  49.4 us
    all_to_all x1, starting transfers between devices, exchange(): return lax.all_to_all(x, AXES, split_axis=0, concat_axis=0, tiled=True)  11.5 us
    pallas_call x1, Pallas kernels, push(): pl.pallas_call(push_kernel, in_specs=[SMEM] * 3 + [VMEM] * len(arrays), o...  9.45 us
    all_to_all x1, waiting for transfers between devices, exchange(): return lax.all_to_all(x, AXES, split_axis=0, concat_axis=0, tiled=True)  6.57 us
    ppermute x4, starting transfers between devices, local(): lax.ppermute(m, axis, pairs + [(j, i) for i, j in pairs])  3.65 us
    ppermute x4, waiting for transfers between devices, local(): lax.ppermute(m, axis, pairs + [(j, i) for i, j in pairs])  3.05 us
    unnamed x9, local copies, waits for them, and re-layouts  2.94 us
    pallas_call x1, Pallas kernels, inner(): pl.pallas_call(inner_kernel, out_shape=(struct((QUADS * WIDTH, LANES)), s...  2.94 us
  transfers between devices with their start and end apart: 5, of which 2 were waited for; matrix products, arithmetic and copies ran while one was open for 1% of the time, Pallas kernels for 3%

profile of v10, /device:TPU:1, one launch (start us, length us, event | category | flops | bytes accessed | tf_op | source)
XLA Modules:
  0.0 97.7 jit_solution(1144118157465240397)
XLA Ops:
  0.0 1.5 %request.1 = (s32[128,128]{1,0:T(8,128)}, s32[8,128]{1,0:T(8,128)}) custom-call(s32[2,64]{1,0:T(2,128)} %bitcast.27, s32[2,64]{1,0:T(2,128)} %bitcast.28), custom_call_target="tpu_custom_call" | custom-call | tf_op jit(solution)/shard_map/request/pallas_call | solution.py:76
  1.5 11.5 %all-to-all-start = ((s32[128,1,128]{2,1,0:T(1,128)}), s32[128,1,128]{2,1,0:T(1,128)S(1)}, u32[]{:S(2)}, u32[]{:S(2)}) async-start(s32[128,1,128]{2,1,0:T(1,128)} %bitcast.26), calls=%async_computation | async-start | bytes 131072 | tf_op jit(solution)/shard_map/all_to_all | solution.py:436
  13.0 1.1 %copy.13 = bf16[16,64,128]{2,0,1:T(8,128)(2,1)S(1)} copy(bf16[16,64,128]{2,1,0:T(8,128)(2,1)} %param.6) | data formatting | bytes 524288 | tf_op args[0]
  14.1 0.0 copy-start
  14.2 0.9 copy-done
  15.1 0.9 copy-done.1
  16.0 6.6 %all-to-all-done = s32[128,1,128]{2,1,0:T(1,128)S(1)} async-done(((s32[128,1,128]{2,1,0:T(1,128)}), s32[128,1,128]{2,1,0:T(1,128)S(1)}, u32[]{:S(2)}, u32[]{:S(2)}) %all-to-all-start) | async-done | bytes 65568 | tf_op jit(solution)/shard_map/all_to_all | solution.py:436
  22.6 1.2 %pack.1 = (bf16[256,16,128]{2,1,0:T(8,128)(2,1)S(1)}, s32[8,128]{1,0:T(8,128)S(1)}) custom-call(s32[128,128]{1,0:T(8,128)S(1)} %bitcast.23, bf16[64,16,128]{2,1,0:T(8,128)(2,1)S(1)} %bitcast.21), custom_call_target="tpu_custom_call" | custom-call | tf_op jit(solution)/shard_map/pack/pallas_call | solution.py:101
  23.7 0.0 copy-start.2
  23.7 0.0 copy-start.3
  23.7 23.7 %all_to_all.22 = bf16[128,2,16,128]{3,2,1,0:T(8,128)(2,1)S(1)} all-to-all(bf16[128,2,16,128]{3,2,1,0:T(8,128)(2,1)S(1)} %bitcast.22), channel_id=1, replica_groups=mesh['face'=4,'tile'=32] {'face','tile'}, dimensions={0} | all-to-all | bytes 2097152 | tf_op jit(solution)/shard_map/all_to_all | solution.py:436
  47.5 2.8 %regrid.1 = (f32[1088,128]{1,0:T(8,128)S(1)}, f32[1280,128]{1,0:T(8,128)S(1)}, f32[272,128]{1,0:T(8,128)S(1)}, f32[272,128]{1,0:T(8,128)S(1)}, f32[40,128]{1,0:T(8,128)S(1)}, /*index=5*/f32[40,128]{1,0:T(8,128)S(1)}) custom-call(s32[8,128]{1,0:T(8,128)S(1)} %copy-done.3, s32[1]{0:T(128)} %bitcast.7.tile_ref, s32[1]{0:T(128)} %bitcast.8.face_ref, ...), custom_call_target="tpu_custom_call" | custom-call | tf_op jit(solution)/shard_map/regrid/pallas_call | solution.py:197
  50.3 0.2 collective-permute-start
  50.5 0.7 collective-permute-start.1
  51.2 1.6 %collective-permute-start.2 = (f32[40,128]{1,0:T(8,128)S(1)}, f32[40,128]{1,0:T(8,128)S(1)}, u32[]{:S(2)}, u32[]{:S(2)}) collective-permute-start(f32[40,128]{1,0:T(8,128)S(1)} %get-tuple-element.41), channel_id=1, source_target_pairs={{0,32},{64,96},{32,0},{96,64},{1,33},{65,97},{33,1},{97,65},{2,34}... | collective-permute-start | bytes 61448 | tf_op jit(solution)/shard_map/ppermute | solution.py:459
  52.7 1.2 %collective-permute-start.3 = (f32[40,128]{1,0:T(8,128)S(1)}, f32[40,128]{1,0:T(8,128)S(1)}, u32[]{:S(2)}, u32[]{:S(2)}) collective-permute-start(f32[40,128]{1,0:T(8,128)S(1)} %get-tuple-element.42), channel_id=1, source_target_pairs={{32,64},{96,0},{64,32},{0,96},{33,65},{97,1},{65,33},{1,97},{34,66... | collective-permute-start | bytes 61448 | tf_op jit(solution)/shard_map/ppermute | solution.py:459
  53.9 2.9 %inner.1 = (f32[1024,128]{1,0:T(8,128)S(1)}, f32[32,8,128]{2,1,0:T(8,128)S(1)}) custom-call(f32[1280,128]{1,0:T(8,128)S(1)} %get-tuple-element.36.turned_ref), custom_call_target="tpu_custom_call" | custom-call | flops 16777216 | bytes 12582912 | tf_op jit(solution)/shard_map/inner/pallas_call | solution.py:266
  56.9 0.0 collective-permute-done.2.wide0_ref
  56.9 3.0 %collective-permute-done.3.wide1_ref = f32[40,128]{1,0:T(8,128)S(1)} collective-permute-done((f32[40,128]{1,0:T(8,128)S(1)}, f32[40,128]{1,0:T(8,128)S(1)}, u32[]{:S(2)}, u32[]{:S(2)}) %collective-permute-start.3) | collective-permute-done | bytes 20512 | tf_op jit(solution)/shard_map/ppermute | solution.py:459
  59.9 0.0 collective-permute-done.tall0_ref
  59.9 0.0 collective-permute-done.1.tall1_ref
  59.9 9.4 %push.1 = s32[2176,128]{1,0:T(8,128)S(1)} custom-call(s32[8,128]{1,0:T(8,128)S(1)} %copy-done.3, s32[1]{0:T(128)} %bitcast.7.tile_ref, s32[1]{0:T(128)} %bitcast.8.face_ref, f32[1088,128]{1,0:T(8,128)S(1)} %get-tuple-element.35.field_ref, f32[1280,128]{1,0:T(8,128)S(1)} %get-tuple-element.36.turned_ref, f32[1024,128]{1,0:T(8,128)S(1)} %get-tuple-element.37.turn_ref, ...), custom_call_target="tpu_custom_call" | custom-call | tf_op jit(solution)/shard_map/push/pallas_call | solution.py:383
  69.4 25.7 %all_to_all.23 = s32[128,17,1,128]{3,2,1,0:T(1,128)S(1)} all-to-all(s32[128,17,1,128]{3,2,1,0:T(1,128)S(1)} %bitcast.18), channel_id=1, replica_groups=mesh['face'=4,'tile'=32] {'face','tile'}, dimensions={0} | all-to-all | bytes 2228224 | tf_op jit(solution)/shard_map/all_to_all | solution.py:436
  95.1 2.6 %collect.1 = f32[1024,128]{1,0:T(8,128)} custom-call(s32[8,128]{1,0:T(8,128)S(1)} %get-tuple-element.28.slots_ref, s32[2176,128]{1,0:T(8,128)S(1)} %bitcast.19), custom_call_target="tpu_custom_call" | custom-call | tf_op jit(solution)/shard_map/collect/pallas_call | solution.py:425
  (4 shorter events, 0.0 us)
Async XLA Ops:
  1.5 21.0 %all-to-all-start = ((s32[128,1,128]{2,1,0:T(1,128)}), s32[128,1,128]{2,1,0:T(1,128)S(1)}, u32[]{:S(2)}, u32[]{:S(2)}) async-start(s32[128,1,128]{2,1,0:T(1,128)} %bitcast.26), calls=%async_computation | async-start | bytes 131072 | tf_op jit(solution)/shard_map/all_to_all | solution.py:436
  14.1 0.9 copy-start
  15.1 0.9 copy-start.1
  23.7 23.7 %copy-start.2 = (f32[32,256]{1,0:T(8,128)S(1)}, f32[32,256]{1,0:T(8,128)}, u32[]{:S(2)}) copy-start(f32[32,256]{1,0:T(8,128)} %truth_ref.1) | copy-start | bytes 98308
  23.7 23.7 %copy-start.3 = (s32[8,128]{1,0:T(8,128)S(1)}, s32[8,128]{1,0:T(8,128)}, u32[]{:S(2)}) copy-start(s32[8,128]{1,0:T(8,128)} %get-tuple-element.29.place_ref) | copy-start | bytes 12292
  50.3 9.7 %collective-permute-start = (f32[272,128]{1,0:T(8,128)S(1)}, f32[272,128]{1,0:T(8,128)S(1)}, u32[]{:S(2)}, u32[]{:S(2)}) collective-permute-start(f32[272,128]{1,0:T(8,128)S(1)} %get-tuple-element.39), channel_id=1, source_target_pairs={{0,1},{2,3},{4,5},{6,7},{8,9},{10,11},{12,13},{14,15},{16,17},{18,... | collective-permute-start | bytes 417800 | tf_op jit(solution)/shard_map/ppermute | solution.py:459
  50.5 9.4 %collective-permute-start.1 = (f32[272,128]{1,0:T(8,128)S(1)}, f32[272,128]{1,0:T(8,128)S(1)}, u32[]{:S(2)}, u32[]{:S(2)}) collective-permute-start(f32[272,128]{1,0:T(8,128)S(1)} %get-tuple-element.40), channel_id=1, source_target_pairs={{1,2},{3,4},{5,6},{7,8},{9,10},{11,12},{13,14},{15,16},{17,18},{19... | collective-permute-start | bytes 417800 | tf_op jit(solution)/shard_map/ppermute | solution.py:459
  51.2 5.7 %collective-permute-start.2 = (f32[40,128]{1,0:T(8,128)S(1)}, f32[40,128]{1,0:T(8,128)S(1)}, u32[]{:S(2)}, u32[]{:S(2)}) collective-permute-start(f32[40,128]{1,0:T(8,128)S(1)} %get-tuple-element.41), channel_id=1, source_target_pairs={{0,32},{64,96},{32,0},{96,64},{1,33},{65,97},{33,1},{97,65},{2,34}... | collective-permute-start | bytes 61448 | tf_op jit(solution)/shard_map/ppermute | solution.py:459
  52.7 7.2 %collective-permute-start.3 = (f32[40,128]{1,0:T(8,128)S(1)}, f32[40,128]{1,0:T(8,128)S(1)}, u32[]{:S(2)}, u32[]{:S(2)}) collective-permute-start(f32[40,128]{1,0:T(8,128)S(1)} %get-tuple-element.42), channel_id=1, source_target_pairs={{32,64},{96,0},{64,32},{0,96},{33,65},{97,1},{65,33},{1,97},{34,66... | collective-permute-start | bytes 61448 | tf_op jit(solution)/shard_map/ppermute | solution.py:459
